TPU v7x, 768 devices: a whole 4x8x12 slice. The times are simulated.
768 devices in a mesh: dp: 16 (over x, z_lo), tensor: 48 (over z_hi, y, core).
Axes of the slice: x: 4, y: 8, z: 12 (z_hi: 3, z_lo: 4; z = z_hi * 4 + z_lo), core: 2. Of those that a mesh axis runs over, the one named last changes fastest.
Arguments:
- activations: bfloat16 [16384, 6144], P('dp', 'tensor')
- sample_rows: int32 [11264], P('dp'), may hold values from 0 to 1023
- old_factor: float32 [6144, 6144], P('tensor', 'dp'), may hold values from -6 to 6
Outputs:
- new_factor: float32 [6144, 6144], P('tensor', 'dp')
Inputs may be any that keep to these rules, and one draw needn't show every extreme that they name: `sample_rows`: each entry indexes one of its own replica's 1024 tokens; repeats may occur.
All inputs are finite; a program needn't handle non-finite values.
Results may differ from a plain program's by a relative error of at most 0.0003.
Values may be sent and summed in bfloat16 or wider, within the bound.
No kernel may reach another device: no remote copies, remote signals or barrier semaphores. Data moves between devices by JAX's collectives and lax.ppermute only.
A program may use at most 32 MiB of HBM per device.

v0:
```python
import jax
import jax.numpy as jnp
from jax import lax
from jax.sharding import PartitionSpec as P


def contract_rows(left, right):
    return lax.dot_general(
        left, right, (((0,), (0,)), ((), ())), preferred_element_type=jnp.float32
    )


def body(activations, sample_rows, old_factor):
    sampled = jnp.take(activations, sample_rows, axis=0)
    replicas = lax.axis_size("dp")
    scale = 0.1 / float(replicas * sampled.shape[0])
    block = contract_rows(sampled, lax.all_gather(sampled, "tensor", axis=1, tiled=True))
    summed = lax.psum_scatter(block, "dp", scatter_dimension=1, tiled=True)
    return 0.9 * old_factor + scale * summed


def solution(mesh):
    placed = (P("dp", "tensor"), P("dp"), P("tensor", "dp"))
    return jax.shard_map(
        body, mesh=mesh, in_specs=placed, out_specs=P("tensor", "dp"), check_vma=False
    )
```

profile of v0, /device:TPU:8, one launch (start us, length us, event | category | flops | bytes accessed | tf_op | source)
XLA Modules:
  0.0 283.6 jit_solution(11967573302251261451)
XLA Ops:
  6.5 0.0 copy-start
  6.5 0.0 all-gather.2.cloned.1.call-start
  6.5 0.7 compare_and_fusion
  7.3 0.7 compare_select_fusion
  8.0 0.0 copy-done
  8.0 0.0 copy-start.1
  8.0 2.0 gather_fusion
  10.0 0.8 broadcast_select_fusion
  10.9 0.0 all-gather.2.cloned.1.call-update
  10.9 0.0 reduce-scatter.2.cloned.1.call-start
  10.9 162.5 %all-gather.2.cloned.1.call-done = bf16[704,6144]{1,0:T(8,128)(2,1)} async-done(((bf16[704,128]{1,0:T(8,128)(2,1)}), bf16[704,6144]{1,0:T(8,128)(2,1)}) %all-gather.2.cloned.1.call-update) | async-done | bytes 8650768 | tf_op jit(solution)/shard_map/all_gather | solution.py:17
  173.4 6.7 %fusion = f32[128,6144]{1,0:T(8,128)} fusion(bf16[704,128]{1,0:T(8,128)(2,1)} %broadcast_select_fusion, bf16[704,6144]{1,0:T(8,128)(2,1)} %all-gather.2.cloned.1.call-done), kind=kOutput, calls=%fused_computation.6 | convolution fusion | flops 1107296256 | bytes 11976704 | tf_op jit(solution)/shard_map/dot_general | solution.py:8
  180.1 0.0 reduce-scatter.2.cloned.1.call-update
  180.1 95.0 %reduce-scatter.2.cloned.1.call-done = f32[128,384]{1,0:T(8,128)} async-done(((f32[128,6144]{1,0:T(8,128)}), f32[128,384]{1,0:T(8,128)}) %reduce-scatter.2.cloned.1.call-update) | async-done | bytes 196624 | tf_op jit(solution)/shard_map/reduce_scatter | solution.py:18
  275.1 0.0 copy-done.1
  275.1 1.6 multiply_add_fusion
  (1 shorter events, 0.0 us)
Async XLA Ops:
  6.5 1.4 copy-start
  6.5 166.9 %all-gather.2.cloned.1.call-start = ((), (), s32[]{:S(2)}) async-start(), calls=%async_computation.1 | async-start | bytes 8830976 | tf_op jit(solution)/shard_map/all_gather | solution.py:17
  8.0 267.1 %copy-start.1 = (f32[128,384]{1,0:T(8,128)S(1)}, f32[128,384]{1,0:T(8,128)}, u32[]{:S(2)}) copy-start(f32[128,384]{1,0:T(8,128)} %param.5) | copy-start | bytes 589828
  10.9 264.2 %reduce-scatter.2.cloned.1.call-start = ((), (), s32[]{:S(2)}) async-start(), calls=%async_computation.2 | async-start | bytes 3342336 | tf_op jit(solution)/shard_map/reduce_scatter | solution.py:18
Sparse Core Ops, SparseCore 0:
  11.3 162.0 all-gather.1
  180.3 94.7 reduce-scatter.1
where the time goes:
time: 284 us
  waiting for transfers between devices  257 us (90%)
  between operations  13.4 us (5%)
  matrix products  6.7 us (2%)
  other arithmetic  3.9 us (1%)
    all_gather x1, waiting for transfers between devices, body(): lax.all_gather(sampled, 'tensor', axis=1, tiled=True)  162 us
    reduce_scatter x1, waiting for transfers between devices, body(): summed = lax.psum_scatter(block, 'dp', scatter_dimension=1, tiled=True)  95 us
    dot_general x1, matrix products, contract_rows(): lax.dot_general(left, right, (((0,), (0,)), ((), ())), preferred_element_...  6.7 us
  transfers between devices with their start and end apart: 2, of which 2 were waited for; matrix products, arithmetic and copies ran while one was open for 0% of the time, Pallas kernels for 0%

commit v1 on v0

v1 whole, which is shorter than its diff:
```python
import jax
import jax.numpy as jnp
from jax import lax
from jax.experimental import pallas as pl
from jax.experimental.pallas import tpu as pltpu
from jax.sharding import Mesh
from jax.sharding import PartitionSpec as P

NX, NZL, NZH, NY, NC = 4, 4, 3, 8, 2
AXES = ("x", "zl", "zh", "y", "core")


def triple_perm(i):
    return [(3 * w + (i + zh) % 3, zh * 16 + w) for zh in range(NZH) for w in range(16)]


def swap_perm():
    return [
        ((x * NZL + zl) * 16 + w, w * 16 + (2 * x + zl % 2) * NC + zl // 2)
        for x in range(NX)
        for zl in range(NZL)
        for w in range(16)
    ]


def product_kernel(at_ref, a_ref, mine_ref, other_ref, out_ref):
    zh, core = at_ref[0], at_ref[1]
    rows = jnp.concatenate([a_ref[0], a_ref[1]], axis=1)
    for b_ref, cw in ((mine_ref, core), (other_ref, 1 - core)):
        cols = jnp.concatenate(
            [b_ref[lax.rem(j + NZH - zh, NZH)] for j in range(NZH)], axis=1
        )
        out_ref[0, cw] = lax.dot_general(
            rows, cols, (((0,), (0,)), ((), ())), preferred_element_type=jnp.float32
        )


def product(at, a, mine, other):
    k = a.shape[1]
    return pl.pallas_call(
        product_kernel,
        grid_spec=pltpu.PrefetchScalarGridSpec(
            num_scalar_prefetch=1,
            grid=(NX,),
            in_specs=[
                pl.BlockSpec((2, k, 128), lambda i, z: (i, 0, 0)),
                pl.BlockSpec((NZH, k, 128), lambda i, z: (0, 0, 0)),
                pl.BlockSpec((NZH, k, 128), lambda i, z: (0, 0, 0)),
            ],
            out_specs=pl.BlockSpec((1, NC, 256, 384), lambda i, z: (i, 0, 0, 0)),
        ),
        out_shape=jax.ShapeDtypeStruct((NX, NC, 256, 384), jnp.float32),
        cost_estimate=pl.CostEstimate(
            flops=2 * k * 1024 * 768, bytes_accessed=6_000_000, transcendentals=0
        ),
    )(at, a, mine, other)


def body(activations, sample_rows, old_factor):
    block = activations.at[sample_rows].get(mode="promise_in_bounds")
    k = block.shape[0]
    scale = 0.1 / float(NX * NZL * k)
    a = lax.all_gather(block, "y", axis=0)
    mine = jnp.stack([lax.ppermute(block, ("zh", "y", "core"), triple_perm(i)) for i in range(NZH)])
    other = lax.ppermute(mine, "core", [(0, 1), (1, 0)])
    at = jnp.stack([lax.axis_index("zh"), lax.axis_index("core")]).astype(jnp.int32)
    part = product(at, a, mine, other)
    part = lax.all_to_all(
        part.reshape(NX * NC, 256, 384), ("x", "core"), split_axis=0, concat_axis=0, tiled=True
    )
    part = jnp.sum(part.reshape(NX, NZL, 128, 384), axis=0)
    part = lax.all_to_all(part, "zl", split_axis=0, concat_axis=0, tiled=True)
    total = jnp.sum(part, axis=0)
    total = lax.ppermute(total, ("x", "zl", "y", "core"), swap_perm())
    return 0.9 * old_factor + scale * total


def solution(mesh):
    fine = Mesh(mesh.devices.reshape(NX, NZL, NZH, NY, NC), AXES)
    dp, tensor = ("x", "zl"), ("zh", "y", "core")
    return jax.shard_map(
        body,
        mesh=fine,
        in_specs=(P(dp, tensor), P(dp), P(tensor, dp)),
        out_specs=P(tensor, dp),
        check_vma=False,
    )
```

time: 284 us -> 176 us (0.62)
  the two profiles are of different devices: /device:TPU:8 before, /device:TPU:6 now
where the time goes in v1:
time: 176 us
  blocking collectives  67.9 us (39%)
  waiting for transfers between devices  48.9 us (28%)
  starting transfers between devices  32.3 us (18%)
  between operations  13.5 us (8%)
  Pallas kernels  6.02 us (3%)
  other arithmetic  4.27 us (2%)
  local copies, waits for them, and re-layouts  2.75 us (2%)
    all_to_all x1, blocking collectives, body(): lax.all_to_all(part.reshape(NX * NC, 256, 384), ('x', 'core'), split_axis...  41.6 us
    all_to_all x1, blocking collectives, body(): part = lax.all_to_all(part, 'zl', split_axis=0, concat_axis=0, tiled=True)  26.3 us
    ppermute x3, starting transfers between devices, body(): lax.ppermute(block, ('zh', 'y', 'core'), triple_perm(i))  25 us
    all_gather x1, waiting for transfers between devices, body(): a = lax.all_gather(block, 'y', axis=0)  17.7 us
    ppermute x1, waiting for transfers between devices, body(): total = lax.ppermute(total, ('x', 'zl', 'y', 'core'), swap_perm())  16.9 us
    ppermute x3, waiting for transfers between devices, body(): lax.ppermute(block, ('zh', 'y', 'core'), triple_perm(i))  13.1 us
    pallas_call x1, Pallas kernels, product(): pl.pallas_call(product_kernel, grid_spec=pltpu.PrefetchScalarGridSpec(num...  6.02 us
    ppermute x1, starting transfers between devices, body(): total = lax.ppermute(total, ('x', 'zl', 'y', 'core'), swap_perm())  5.37 us
  transfers between devices with their start and end apart: 6, of which 4 were waited for; matrix products, arithmetic and copies ran while one was open for 0% of the time, Pallas kernels for 0%

profile of v1, /device:TPU:6, one launch (start us, length us, event | category | flops | bytes accessed | tf_op | source)
XLA Modules:
  0.0 175.6 jit_solution(1723048497751192441)
XLA Ops:
  6.5 0.0 copy-start
  6.5 0.0 all-gather.3.cloned.1.call-start
  6.5 0.7 compare_select_fusion
  7.3 0.2 copy-done
  7.5 2.5 %gather_fusion = bf16[704,128]{1,0:T(8,128)(2,1)} fusion(bf16[1024,128]{1,0:T(8,128)(2,1)S(1)} %copy-done, s32[1024]{0:T(1024)S(1)} %pad_clamp_fusion), kind=kCustom, calls=%fused_computation | custom fusion | bytes 363264 | tf_op jit(solution)/shard_map/gather | solution.py:60
  10.0 0.0 all-gather.3.cloned.1.call-update
  10.0 1.6 collective-permute-start
  11.6 13.3 %collective-permute-start.2 = (bf16[704,128]{1,0:T(8,128)(2,1)}, bf16[704,128]{1,0:T(8,128)(2,1)S(1)}, u32[]{:S(2)}, u32[]{:S(2)}) collective-permute-start(bf16[704,128]{1,0:T(8,128)(2,1)} %gather_fusion), channel_id=1, source_target_pairs={{2,0},{5,1},{8,2},{11,3},{14,4},{17,5},{20,6},{23,7},{26,8},{29,9}... | collective-permute-start | bytes 540680 | tf_op jit(solution)/shard_map/ppermute | solution.py:64
  24.9 10.2 %collective-permute-start.1 = (bf16[704,128]{1,0:T(8,128)(2,1)}, bf16[704,128]{1,0:T(8,128)(2,1)S(1)}, u32[]{:S(2)}, u32[]{:S(2)}) collective-permute-start(bf16[704,128]{1,0:T(8,128)(2,1)} %gather_fusion), channel_id=1, source_target_pairs={{1,0},{4,1},{7,2},{10,3},{13,4},{16,5},{19,6},{22,7},{25,8},{28,9}... | collective-permute-start | bytes 540680 | tf_op jit(solution)/shard_map/ppermute | solution.py:64
  35.1 0.0 collective-permute-done
  35.1 0.0 collective-permute-done.2
  35.1 13.1 %collective-permute-done.1 = bf16[704,128]{1,0:T(8,128)(2,1)S(1)} collective-permute-done((bf16[704,128]{1,0:T(8,128)(2,1)}, bf16[704,128]{1,0:T(8,128)(2,1)S(1)}, u32[]{:S(2)}, u32[]{:S(2)}) %collective-permute-start.1) | collective-permute-done | bytes 180256 | tf_op jit(solution)/shard_map/ppermute | solution.py:64
  48.2 0.1 pad_maximum_fusion.mine_ref
  48.2 0.0 copy-start.1
  48.2 1.9 %collective-permute-start.3 = (bf16[3,704,128]{2,1,0:T(8,128)(2,1)S(1)}, bf16[3,704,128]{2,1,0:T(8,128)(2,1)S(1)}, u32[]{:S(2)}, u32[]{:S(2)}) collective-permute-start(bf16[3,704,128]{2,1,0:T(8,128)(2,1)S(1)} %pad_maximum_fusion.mine_ref), channel_id=1, source_target_pairs={{0,1},{1,0},{2,3},{3,2},{4,5},{5,4},{6,7},{7,6},{8,9},{9,8},{10,11... | collective-permute-start | bytes 1622024 | tf_op jit(solution)/shard_map/ppermute | solution.py:65
  50.2 0.7 pad_add_fusion.at_ref
  50.8 1.2 collective-permute-done.3.other_ref
  52.1 0.0 copy-start.2
  52.1 17.7 %all-gather.3.cloned.1.call-done = bf16[5632,128]{1,0:T(8,128)(2,1)} async-done(((bf16[704,128]{1,0:T(8,128)(2,1)}), bf16[5632,128]{1,0:T(8,128)(2,1)}) %all-gather.3.cloned.1.call-update) | async-done | bytes 1441808 | tf_op jit(solution)/shard_map/all_gather | solution.py:63
  69.7 0.0 copy-done.1
  69.7 0.0 copy-done.2
  69.7 6.0 %shard_map.37 = f32[4,2,256,384]{3,2,1,0:T(8,128)} custom-call(s32[2]{0:T(128)} %pad_add_fusion.at_ref, bf16[8,704,128]{2,1,0:T(8,128)(2,1)} %bitcast.10, bf16[3,704,128]{2,1,0:T(8,128)(2,1)} %copy-done.1, bf16[3,704,128]{2,1,0:T(8,128)(2,1)} %copy-done.2), custom_call_target="tpu_custom_call" | custom-call | flops 1107296256 | bytes 6000000 | tf_op jit(solution)/shard_map/pallas_call | solution.py:40
  75.8 41.6 %all_to_all.10 = f32[8,256,384]{2,1,0:T(8,128)S(1)} all-to-all(f32[8,256,384]{2,1,0:T(8,128)} %bitcast.8), channel_id=1, replica_groups=mesh['x'=4,'zl'=4,'zh'=3,'y'=8,'core'=2] {'x','core'}, dimensions={0} | all-to-all | bytes 6291456 | tf_op jit(solution)/shard_map/all_to_all | solution.py:68
  117.3 1.1 reduce_sum.18
  118.5 26.3 %all_to_all.11 = f32[4,128,384]{2,1,0:T(8,128)S(1)} all-to-all(f32[4,128,384]{2,1,0:T(8,128)} %reduce_sum.18), channel_id=1, replica_groups=mesh['x'=4,'zl'=4,'zh'=3,'y'=8,'core'=2] {'zl'}, dimensions={0} | all-to-all | bytes 1572864 | tf_op jit(solution)/shard_map/all_to_all | solution.py:72
  144.8 5.4 %collective-permute-start.4 = (f32[128,384]{1,0:T(8,128)S(1)}, f32[128,384]{1,0:T(8,128)S(1)}, u32[]{:S(2)}, u32[]{:S(2)}) collective-permute-start(f32[128,384]{1,0:T(8,128)S(1)} %reduce_sum.19), channel_id=1, source_target_pairs={{0,0},{1,48},{2,96},{3,144},{4,192},{5,240},{6,288},{7,336},{8,384... | collective-permute-start | bytes 589832 | tf_op jit(solution)/shard_map/ppermute | solution.py:74
  150.2 16.9 %collective-permute-done.4 = f32[128,384]{1,0:T(8,128)S(1)} collective-permute-done((f32[128,384]{1,0:T(8,128)S(1)}, f32[128,384]{1,0:T(8,128)S(1)}, u32[]{:S(2)}, u32[]{:S(2)}) %collective-permute-start.4) | collective-permute-done | bytes 196640 | tf_op jit(solution)/shard_map/ppermute | solution.py:74
  167.1 1.6 multiply_add_fusion
  (2 shorter events, 0.0 us)
Async XLA Ops:
  6.5 1.0 copy-start
  6.5 63.2 %all-gather.3.cloned.1.call-start = ((), (), s32[]{:S(2)}) async-start(), calls=%async_computation.2 | async-start | bytes 1622016 | tf_op jit(solution)/shard_map/all_gather | solution.py:63
  10.0 25.1 %collective-permute-start = (bf16[704,128]{1,0:T(8,128)(2,1)}, bf16[704,128]{1,0:T(8,128)(2,1)S(1)}, u32[]{:S(2)}, u32[]{:S(2)}) collective-permute-start(bf16[704,128]{1,0:T(8,128)(2,1)} %gather_fusion), channel_id=1, source_target_pairs={{0,0},{3,1},{6,2},{9,3},{12,4},{15,5},{18,6},{21,7},{24,8},{27,9},... | collective-permute-start | bytes 540680 | tf_op jit(solution)/shard_map/ppermute | solution.py:64
  11.6 23.5 %collective-permute-start.2 = (bf16[704,128]{1,0:T(8,128)(2,1)}, bf16[704,128]{1,0:T(8,128)(2,1)S(1)}, u32[]{:S(2)}, u32[]{:S(2)}) collective-permute-start(bf16[704,128]{1,0:T(8,128)(2,1)} %gather_fusion), channel_id=1, source_target_pairs={{2,0},{5,1},{8,2},{11,3},{14,4},{17,5},{20,6},{23,7},{26,8},{29,9}... | collective-permute-start | bytes 540680 | tf_op jit(solution)/shard_map/ppermute | solution.py:64
  24.9 23.3 %collective-permute-start.1 = (bf16[704,128]{1,0:T(8,128)(2,1)}, bf16[704,128]{1,0:T(8,128)(2,1)S(1)}, u32[]{:S(2)}, u32[]{:S(2)}) collective-permute-start(bf16[704,128]{1,0:T(8,128)(2,1)} %gather_fusion), channel_id=1, source_target_pairs={{1,0},{4,1},{7,2},{10,3},{13,4},{16,5},{19,6},{22,7},{25,8},{28,9}... | collective-permute-start | bytes 540680 | tf_op jit(solution)/shard_map/ppermute | solution.py:64
  48.2 21.5 %copy-start.1 = (bf16[3,704,128]{2,1,0:T(8,128)(2,1)}, bf16[3,704,128]{2,1,0:T(8,128)(2,1)S(1)}, u32[]{:S(2)}) copy-start(bf16[3,704,128]{2,1,0:T(8,128)(2,1)S(1)} %pad_maximum_fusion.mine_ref) | copy-start | bytes 1622020
  48.2 3.8 %collective-permute-start.3 = (bf16[3,704,128]{2,1,0:T(8,128)(2,1)S(1)}, bf16[3,704,128]{2,1,0:T(8,128)(2,1)S(1)}, u32[]{:S(2)}, u32[]{:S(2)}) collective-permute-start(bf16[3,704,128]{2,1,0:T(8,128)(2,1)S(1)} %pad_maximum_fusion.mine_ref), channel_id=1, source_target_pairs={{0,1},{1,0},{2,3},{3,2},{4,5},{5,4},{6,7},{7,6},{8,9},{9,8},{10,11... | collective-permute-start | bytes 1622024 | tf_op jit(solution)/shard_map/ppermute | solution.py:65
  52.1 17.7 %copy-start.2 = (bf16[3,704,128]{2,1,0:T(8,128)(2,1)}, bf16[3,704,128]{2,1,0:T(8,128)(2,1)S(1)}, u32[]{:S(2)}) copy-start(bf16[3,704,128]{2,1,0:T(8,128)(2,1)S(1)} %collective-permute-done.3.other_ref) | copy-start | bytes 1622020
  144.8 22.3 %collective-permute-start.4 = (f32[128,384]{1,0:T(8,128)S(1)}, f32[128,384]{1,0:T(8,128)S(1)}, u32[]{:S(2)}, u32[]{:S(2)}) collective-permute-start(f32[128,384]{1,0:T(8,128)S(1)} %reduce_sum.19), channel_id=1, source_target_pairs={{0,0},{1,48},{2,96},{3,144},{4,192},{5,240},{6,288},{7,336},{8,384... | collective-permute-start | bytes 589832 | tf_op jit(solution)/shard_map/ppermute | solution.py:74
Sparse Core Ops, SparseCore 0:
  10.2 59.5 all-gather.2

commit v2 on v0

v2 whole, which is shorter than its diff:
```python
import jax
import jax.numpy as jnp
from jax import lax
from jax.experimental import pallas as pl
from jax.experimental.pallas import tpu as pltpu
from jax.sharding import Mesh
from jax.sharding import PartitionSpec as P

NX, NZL, NZH, NY, NC = 4, 4, 3, 8, 2
AXES = ("x", "zl", "zh", "y", "core")
TRIPLE = ((0, 11), (1, 6), (7, 12), (2, 13), (3, 8), (9, 14), (4, 15), (5, 10))
OFFSET = (((-1, -2), (-3, -4)), ((0, 1), (2, 3)))


def triple_perm(i):
    return [
        (3 * TRIPLE[y][c] + (i + zh) % 3, zh * 16 + y * NC + c)
        for zh in range(NZH)
        for y in range(NY)
        for c in range(NC)
    ]


def ring_perm(cores):
    return [
        (y * NC + c, (y + 1 - 2 * c) % NY * NC + c) for y in range(NY) for c in cores
    ]


def place_perm():
    pairs = []
    for x in range(NX):
        for zl in range(NZL):
            for y in range(NY):
                for c in range(NC):
                    to_y = (y + OFFSET[zl % 2][zl // 2][x // 2]) % NY
                    source = ((x * NZL + zl) * NY + y) * NC + c
                    pairs.append((source, (TRIPLE[y][c] * NY + to_y) * NC + x % 2))
    return pairs


def product_kernel(at_ref, a0_ref, a1_ref, a2_ref, mine_ref, other_ref, out_ref):
    zh, core = at_ref[0], at_ref[1]
    columns = []
    for cw in range(NC):
        for j in range(NZH):
            at = lax.rem(j + NZH - zh, NZH)
            columns.append(jnp.where(core == cw, mine_ref[at], other_ref[at]))
    columns = jnp.concatenate(columns, axis=1)
    for i, (up_ref, down_ref) in enumerate(((a1_ref, a0_ref), (a2_ref, a1_ref))):
        rows = [jnp.where(core == 0, up_ref[c], down_ref[c]) for c in range(NC)]
        out = lax.dot_general(
            jnp.concatenate(rows, axis=1),
            columns,
            (((0,), (0,)), ((), ())),
            preferred_element_type=jnp.float32,
        )
        for c in range(NC):
            for cw in range(NC):
                out_ref[i * NC + c, cw] = out[c * 128 : (c + 1) * 128, cw * 384 : (cw + 1) * 384]


def product(at, a0, a1, a2, mine, other):
    k = a0.shape[1]
    vmem = pl.BlockSpec(memory_space=pltpu.VMEM)
    return pl.pallas_call(
        product_kernel,
        in_specs=[pl.BlockSpec(memory_space=pltpu.SMEM)] + [vmem] * 5,
        out_specs=vmem,
        out_shape=jax.ShapeDtypeStruct((NX, NC, 128, 384), jnp.float32),
        compiler_params=pltpu.CompilerParams(vmem_limit_bytes=32 << 20),
        cost_estimate=pl.CostEstimate(
            flops=2 * k * 512 * 768, bytes_accessed=4_000_000, transcendentals=0
        ),
    )(at, a0, a1, a2, mine, other)


def reduce_x(part):
    part = lax.all_to_all(
        part.reshape(NX * NC, 128, 384), ("x", "core"), split_axis=0, concat_axis=0, tiled=True
    )
    return jnp.sum(part.reshape(NX, NC, 128, 384), axis=0)


def body(activations, sample_rows, old_factor):
    block = activations.at[sample_rows].get(mode="promise_in_bounds")
    scale = 0.1 / float(NX * NZL * block.shape[0])
    at = jnp.stack([lax.axis_index("zh"), lax.axis_index("core")]).astype(jnp.int32)
    ring = [lax.all_gather(block, "core", axis=0)]
    for step in range(4):
        ring.append(lax.ppermute(ring[-1], ("y", "core"), ring_perm((0, 1) if step < 3 else (0,))))
    mine = jnp.stack([lax.ppermute(block, ("zh", "y", "core"), triple_perm(i)) for i in range(NZH)])
    other = lax.ppermute(mine, "core", [(0, 1), (1, 0)])
    halves = [reduce_x(product(at, *ring[2 * h : 2 * h + 3], mine, other)) for h in range(2)]
    part = jnp.concatenate(halves, axis=0)
    part = lax.all_to_all(part, "zl", split_axis=0, concat_axis=0, tiled=True)
    total = jnp.sum(part, axis=0)
    total = lax.ppermute(total, ("x", "zl", "y", "core"), place_perm())
    return 0.9 * old_factor + scale * total


def solution(mesh):
    fine = Mesh(mesh.devices.reshape(NX, NZL, NZH, NY, NC), AXES)
    dp, tensor = ("x", "zl"), ("zh", "y", "core")
    return jax.shard_map(
        body,
        mesh=fine,
        in_specs=(P(dp, tensor), P(dp), P(tensor, dp)),
        out_specs=P(tensor, dp),
        check_vma=False,
    )
```

time: 284 us -> 156 us (0.55)
  waiting for transfers between devices: 257 us -> 61.1 us
  starting transfers between devices: 0.04 us -> 57.5 us
  blocking collectives: 0 us -> 25.5 us
  between operations: 13.4 us -> 0.15 us
  matrix products: 6.7 us -> 0 us
  Pallas kernels: 0 us -> 5.11 us
    all_gather x1 -> x0, waiting for transfers between devices: 162 us -> none  [body(): lax.all_gather(sampled, 'tensor', axis=1, tiled=True)]
    reduce_scatter x1 -> x0, waiting for transfers between devices: 95 us -> none  [body(): summed = lax.psum_scatter(block, 'dp', scatter_dimension=1, tiled=True)]
    ppermute x0 -> x9, starting transfers between devices: none -> 48.4 us  [the longest x3 24.1 us: body(): lax.ppermute(block, ('zh', 'y', 'core'), triple_perm(i))]
    ppermute x0 -> x9, waiting for transfers between devices: none -> 41.1 us  [the longest x4 25.3 us: body(): lax.ppermute(ring[-1], ('y', 'core'), ring_perm((0, 1) if step < 3 else (...]
    all_to_all x0 -> x1, blocking collectives: none -> 23.4 us  [body(): part = lax.all_to_all(part, 'zl', split_axis=0, concat_axis=0, tiled=True)]
    all_to_all x0 -> x2, waiting for transfers between devices: none -> 20.1 us  [reduce_x(): lax.all_to_all(part.reshape(NX * NC, 128, 384), ('x', 'core'), split_axis...]
    all_to_all x0 -> x2, starting transfers between devices: none -> 9.1 us  [reduce_x(): lax.all_to_all(part.reshape(NX * NC, 128, 384), ('x', 'core'), split_axis...]
    dot_general x1 -> x0, matrix products: 6.7 us -> none  [contract_rows(): lax.dot_general(left, right, (((0,), (0,)), ((), ())), preferred_element_...]
  transfers between devices with their start and end apart: 2 -> 11, of which waited for: 2 -> 7; matrix products, arithmetic and copies ran while one was open for 0% -> 1% of each run, Pallas kernels for 0% -> 2%
where the time goes in v2:
time: 156 us; the launch traced here: 155 us
  waiting for transfers between devices  61.1 us (39%)
  starting transfers between devices  57.5 us (37%)
  blocking collectives  25.5 us (16%)
  Pallas kernels  5.11 us (3%)
  other arithmetic  3.32 us (2%)
  local copies, waits for them, and re-layouts  2.25 us (1%)
    ppermute x4, waiting for transfers between devices, body(): lax.ppermute(ring[-1], ('y', 'core'), ring_perm((0, 1) if step < 3 else (...  25.3 us
    ppermute x3, starting transfers between devices, body(): lax.ppermute(block, ('zh', 'y', 'core'), triple_perm(i))  24.1 us
    all_to_all x1, blocking collectives, body(): part = lax.all_to_all(part, 'zl', split_axis=0, concat_axis=0, tiled=True)  23.4 us
    all_to_all x2, waiting for transfers between devices, reduce_x(): lax.all_to_all(part.reshape(NX * NC, 128, 384), ('x', 'core'), split_axis...  20.1 us
    ppermute x4, starting transfers between devices, body(): lax.ppermute(ring[-1], ('y', 'core'), ring_perm((0, 1) if step < 3 else (...  15.7 us
    ppermute x1, waiting for transfers between devices, body(): total = lax.ppermute(total, ('x', 'zl', 'y', 'core'), place_perm())  14.7 us
    all_to_all x2, starting transfers between devices, reduce_x(): lax.all_to_all(part.reshape(NX * NC, 128, 384), ('x', 'core'), split_axis...  9.1 us
    pallas_call x2, Pallas kernels, product(): pl.pallas_call(product_kernel, in_specs=[pl.BlockSpec(memory_space=pltpu....  5.11 us
  transfers between devices with their start and end apart: 11, of which 7 were waited for; matrix products, arithmetic and copies ran while one was open for 1% of the time, Pallas kernels for 2%

profile of v2, /device:TPU:8, one launch (start us, length us, event | category | flops | bytes accessed | tf_op | source)
XLA Modules:
  0.0 155.0 jit_solution(3374226096661725653)
XLA Ops:
  0.0 0.7 compare_select_fusion
  0.7 0.2 copy-done
  1.0 2.0 %gather_fusion = bf16[704,128]{1,0:T(8,128)(2,1)S(1)} fusion(bf16[1024,128]{1,0:T(8,128)(2,1)S(1)} %copy-done, s32[1024]{0:T(1024)S(1)} %pad_clamp_fusion), kind=kCustom, calls=%fused_computation | custom fusion | bytes 363264 | tf_op jit(solution)/shard_map/gather | solution.py:86
  3.0 14.4 %collective-permute-start.2 = (bf16[704,128]{1,0:T(8,128)(2,1)S(1)}, bf16[704,128]{1,0:T(8,128)(2,1)S(1)}, u32[]{:S(2)}, u32[]{:S(2)}) collective-permute-start(bf16[704,128]{1,0:T(8,128)(2,1)S(1)} %gather_fusion), channel_id=1, source_target_pairs={{0,0},{33,1},{3,2},{18,3},{21,4},{36,5},{6,6},{39,7},{9,8},{24,9},... | collective-permute-start | bytes 540680 | tf_op jit(solution)/shard_map/ppermute | solution.py:92
  17.4 1.9 %collective-permute-start.4 = (bf16[704,128]{1,0:T(8,128)(2,1)S(1)}, bf16[704,128]{1,0:T(8,128)(2,1)S(1)}, u32[]{:S(2)}, u32[]{:S(2)}) collective-permute-start(bf16[704,128]{1,0:T(8,128)(2,1)S(1)} %gather_fusion), channel_id=1, source_target_pairs={{2,0},{35,1},{5,2},{20,3},{23,4},{38,5},{8,6},{41,7},{11,8},{26,9}... | collective-permute-start | bytes 540680 | tf_op jit(solution)/shard_map/ppermute | solution.py:92
  19.4 7.8 %collective-permute-start.3 = (bf16[704,128]{1,0:T(8,128)(2,1)S(1)}, bf16[704,128]{1,0:T(8,128)(2,1)S(1)}, u32[]{:S(2)}, u32[]{:S(2)}) collective-permute-start(bf16[704,128]{1,0:T(8,128)(2,1)S(1)} %gather_fusion), channel_id=1, source_target_pairs={{1,0},{34,1},{4,2},{19,3},{22,4},{37,5},{7,6},{40,7},{10,8},{25,9}... | collective-permute-start | bytes 540680 | tf_op jit(solution)/shard_map/ppermute | solution.py:92
  27.2 2.1 %all-gather = bf16[1408,128]{1,0:T(8,128)(2,1)S(1)} all-gather(bf16[704,128]{1,0:T(8,128)(2,1)S(1)} %gather_fusion), channel_id=2, replica_groups=mesh['x'=4,'zl'=4,'zh'=3,'y'=8,'core'=2] {'core'}, dimensions={0}, use_global_device_ids=true | all-gather | bytes 540672 | tf_op jit(solution)/shard_map/all_gather | solution.py:89
  29.2 1.9 %collective-permute-start = (bf16[2,704,128]{2,1,0:T(8,128)(2,1)S(1)}, bf16[2,704,128]{2,1,0:T(8,128)(2,1)S(1)}, u32[]{:S(2)}, u32[]{:S(2)}) collective-permute-start(bf16[2,704,128]{2,1,0:T(8,128)(2,1)S(1)} %bitcast.10), channel_id=1, source_target_pairs={{0,2},{1,15},{2,4},{3,1},{4,6},{5,3},{6,8},{7,5},{8,10},{9,7},{10,... | collective-permute-start | bytes 1081352 | tf_op jit(solution)/shard_map/ppermute | solution.py:91
  31.2 1.1 collective-permute-done.3
  32.3 0.1 pad_maximum_fusion.1.mine_ref
  32.3 3.8 %collective-permute-start.5 = (bf16[3,704,128]{2,1,0:T(8,128)(2,1)S(1)}, bf16[3,704,128]{2,1,0:T(8,128)(2,1)S(1)}, u32[]{:S(2)}, u32[]{:S(2)}) collective-permute-start(bf16[3,704,128]{2,1,0:T(8,128)(2,1)S(1)} %pad_maximum_fusion.1.mine_ref), channel_id=1, source_target_pairs={{0,1},{1,0},{2,3},{3,2},{4,5},{5,4},{6,7},{7,6},{8,9},{9,8},{10,11... | collective-permute-start | bytes 1622024 | tf_op jit(solution)/shard_map/ppermute | solution.py:93
  36.1 2.4 %collective-permute-done.a1_ref = bf16[2,704,128]{2,1,0:T(8,128)(2,1)S(1)} collective-permute-done((bf16[2,704,128]{2,1,0:T(8,128)(2,1)S(1)}, bf16[2,704,128]{2,1,0:T(8,128)(2,1)S(1)}, u32[]{:S(2)}, u32[]{:S(2)}) %collective-permute-start) | collective-permute-done | bytes 360480 | tf_op jit(solution)/shard_map/ppermute | solution.py:91
  38.5 6.5 %collective-permute-start.1 = (bf16[2,704,128]{2,1,0:T(8,128)(2,1)S(1)}, bf16[2,704,128]{2,1,0:T(8,128)(2,1)S(1)}, u32[]{:S(2)}, u32[]{:S(2)}) collective-permute-start(bf16[2,704,128]{2,1,0:T(8,128)(2,1)S(1)} %collective-permute-done.a1_ref), channel_id=1, source_target_pairs={{0,2},{1,15},{2,4},{3,1},{4,6},{5,3},{6,8},{7,5},{8,10},{9,7},{10,... | collective-permute-start | bytes 1081352 | tf_op jit(solution)/shard_map/ppermute | solution.py:91
  45.1 0.1 pad_add_fusion.at_ref
  45.1 4.8 %collective-permute-done.1.a2_ref.a0_ref = bf16[2,704,128]{2,1,0:T(8,128)(2,1)S(1)} collective-permute-done((bf16[2,704,128]{2,1,0:T(8,128)(2,1)S(1)}, bf16[2,704,128]{2,1,0:T(8,128)(2,1)S(1)}, u32[]{:S(2)}, u32[]{:S(2)}) %collective-permute-start.1) | collective-permute-done | bytes 360480 | tf_op jit(solution)/shard_map/ppermute | solution.py:91
  50.0 2.5 %shard_map.37 = f32[4,2,128,384]{3,2,1,0:T(8,128)} custom-call(s32[2]{0:T(128)S(1)} %pad_add_fusion.at_ref, bf16[2,704,128]{2,1,0:T(8,128)(2,1)S(1)} %bitcast.11, bf16[2,704,128]{2,1,0:T(8,128)(2,1)S(1)} %collective-permute-done.a1_ref, bf16[2,704,128]{2,1,0:T(8,128)(2,1)S(1)} %collective-permute-done.1.a2_ref.a0_ref, ...), custom_call_target="tpu_custom_call" | custom-call | flops 553648128 | bytes 4000000 | tf_op jit(solution)/shard_map/pallas_call | solution.py:66
  52.5 4.3 %all-to-all-start = ((f32[8,128,384]{2,1,0:T(8,128)}), f32[8,128,384]{2,1,0:T(8,128)}, u32[]{:S(2)}, u32[]{:S(2)}) async-start(f32[8,128,384]{2,1,0:T(8,128)} %bitcast.6), calls=%async_computation | async-start | bytes 3145728 | tf_op jit(solution)/shard_map/all_to_all | solution.py:79
  56.8 5.4 %collective-permute-start.6 = (bf16[2,704,128]{2,1,0:T(8,128)(2,1)S(1)}, bf16[2,704,128]{2,1,0:T(8,128)(2,1)S(1)}, u32[]{:S(2)}, u32[]{:S(2)}) collective-permute-start(bf16[2,704,128]{2,1,0:T(8,128)(2,1)S(1)} %collective-permute-done.1.a2_ref.a0_ref), channel_id=1, source_target_pairs={{0,2},{1,15},{2,4},{3,1},{4,6},{5,3},{6,8},{7,5},{8,10},{9,7},{10,... | collective-permute-start | bytes 1081352 | tf_op jit(solution)/shard_map/ppermute | solution.py:91
  62.2 9.5 %collective-permute-done.6.a1_ref = bf16[2,704,128]{2,1,0:T(8,128)(2,1)S(1)} collective-permute-done((bf16[2,704,128]{2,1,0:T(8,128)(2,1)S(1)}, bf16[2,704,128]{2,1,0:T(8,128)(2,1)S(1)}, u32[]{:S(2)}, u32[]{:S(2)}) %collective-permute-start.6) | collective-permute-done | bytes 360480 | tf_op jit(solution)/shard_map/ppermute | solution.py:91
  71.7 1.9 %collective-permute-start.7 = (bf16[2,704,128]{2,1,0:T(8,128)(2,1)S(1)}, bf16[2,704,128]{2,1,0:T(8,128)(2,1)S(1)}, u32[]{:S(2)}, u32[]{:S(2)}) collective-permute-start(bf16[2,704,128]{2,1,0:T(8,128)(2,1)S(1)} %collective-permute-done.6.a1_ref), channel_id=1, source_target_pairs={{0,2},{2,4},{4,6},{6,8},{8,10},{10,12},{12,14},{14,0},{16,18},{18,... | collective-permute-start | bytes 1081352 | tf_op jit(solution)/shard_map/ppermute | solution.py:91
  73.6 8.6 %collective-permute-done.7.a2_ref = bf16[2,704,128]{2,1,0:T(8,128)(2,1)S(1)} collective-permute-done((bf16[2,704,128]{2,1,0:T(8,128)(2,1)S(1)}, bf16[2,704,128]{2,1,0:T(8,128)(2,1)S(1)}, u32[]{:S(2)}, u32[]{:S(2)}) %collective-permute-start.7) | collective-permute-done | bytes 360480 | tf_op jit(solution)/shard_map/ppermute | solution.py:91
  82.2 2.6 %shard_map.38 = f32[4,2,128,384]{3,2,1,0:T(8,128)} custom-call(s32[2]{0:T(128)S(1)} %pad_add_fusion.at_ref, bf16[2,704,128]{2,1,0:T(8,128)(2,1)S(1)} %collective-permute-done.1.a2_ref.a0_ref, bf16[2,704,128]{2,1,0:T(8,128)(2,1)S(1)} %collective-permute-done.6.a1_ref, bf16[2,704,128]{2,1,0:T(8,128)(2,1)S(1)} %collective-permute-done.7.a2_ref, ...), custom_call_target="tpu_custom_call" | custom-call | flops 553648128 | bytes 4000000 | tf_op jit(solution)/shard_map/pallas_call | solution.py:66
  84.8 4.8 %all-to-all-start.1 = ((f32[8,128,384]{2,1,0:T(8,128)}), f32[8,128,384]{2,1,0:T(8,128)S(1)}, u32[]{:S(2)}, u32[]{:S(2)}) async-start(f32[8,128,384]{2,1,0:T(8,128)} %bitcast.8), calls=%async_computation.1 | async-start | bytes 3145728 | tf_op jit(solution)/shard_map/all_to_all | solution.py:79
  89.6 1.5 reduce_sum.27
  91.1 20.0 %all-to-all-done.1 = f32[8,128,384]{2,1,0:T(8,128)S(1)} async-done(((f32[8,128,384]{2,1,0:T(8,128)}), f32[8,128,384]{2,1,0:T(8,128)S(1)}, u32[]{:S(2)}, u32[]{:S(2)}) %all-to-all-start.1) | async-done | bytes 1572896 | tf_op jit(solution)/shard_map/all_to_all | solution.py:79
  111.2 0.1 reduce_sum.28
  111.3 0.1 pad_maximum_fusion
  111.3 0.0 copy-start.1
  111.3 23.4 %all_to_all.15 = f32[4,128,384]{2,1,0:T(8,128)S(1)} all-to-all(f32[4,128,384]{2,1,0:T(8,128)S(1)} %pad_maximum_fusion), channel_id=1, replica_groups=mesh['x'=4,'zl'=4,'zh'=3,'y'=8,'core'=2] {'zl'}, dimensions={0} | all-to-all | bytes 1572864 | tf_op jit(solution)/shard_map/all_to_all | solution.py:96
  134.8 4.8 %collective-permute-start.8 = (f32[128,384]{1,0:T(8,128)S(1)}, f32[128,384]{1,0:T(8,128)S(1)}, u32[]{:S(2)}, u32[]{:S(2)}) collective-permute-start(f32[128,384]{1,0:T(8,128)S(1)} %reduce_sum.29), channel_id=1, source_target_pairs={{0,14},{1,542},{2,48},{3,288},{4,338},{5,578},{6,100},{7,628},{8,1... | collective-permute-start | bytes 589832 | tf_op jit(solution)/shard_map/ppermute | solution.py:98
  139.6 14.7 %collective-permute-done.8 = f32[128,384]{1,0:T(8,128)S(1)} collective-permute-done((f32[128,384]{1,0:T(8,128)S(1)}, f32[128,384]{1,0:T(8,128)S(1)}, u32[]{:S(2)}, u32[]{:S(2)}) %collective-permute-start.8) | collective-permute-done | bytes 196640 | tf_op jit(solution)/shard_map/ppermute | solution.py:98
  154.3 0.7 multiply_add_fusion
  (8 shorter events, 0.1 us)
Async XLA Ops:
  0.0 1.0 copy-start
  3.0 28.1 %collective-permute-start.2 = (bf16[704,128]{1,0:T(8,128)(2,1)S(1)}, bf16[704,128]{1,0:T(8,128)(2,1)S(1)}, u32[]{:S(2)}, u32[]{:S(2)}) collective-permute-start(bf16[704,128]{1,0:T(8,128)(2,1)S(1)} %gather_fusion), channel_id=1, source_target_pairs={{0,0},{33,1},{3,2},{18,3},{21,4},{36,5},{6,6},{39,7},{9,8},{24,9},... | collective-permute-start | bytes 540680 | tf_op jit(solution)/shard_map/ppermute | solution.py:92
  17.4 13.7 %collective-permute-start.4 = (bf16[704,128]{1,0:T(8,128)(2,1)S(1)}, bf16[704,128]{1,0:T(8,128)(2,1)S(1)}, u32[]{:S(2)}, u32[]{:S(2)}) collective-permute-start(bf16[704,128]{1,0:T(8,128)(2,1)S(1)} %gather_fusion), channel_id=1, source_target_pairs={{2,0},{35,1},{5,2},{20,3},{23,4},{38,5},{8,6},{41,7},{11,8},{26,9}... | collective-permute-start | bytes 540680 | tf_op jit(solution)/shard_map/ppermute | solution.py:92
  19.4 12.9 %collective-permute-start.3 = (bf16[704,128]{1,0:T(8,128)(2,1)S(1)}, bf16[704,128]{1,0:T(8,128)(2,1)S(1)}, u32[]{:S(2)}, u32[]{:S(2)}) collective-permute-start(bf16[704,128]{1,0:T(8,128)(2,1)S(1)} %gather_fusion), channel_id=1, source_target_pairs={{1,0},{34,1},{4,2},{19,3},{22,4},{37,5},{7,6},{40,7},{10,8},{25,9}... | collective-permute-start | bytes 540680 | tf_op jit(solution)/shard_map/ppermute | solution.py:92
  29.2 9.3 %collective-permute-start = (bf16[2,704,128]{2,1,0:T(8,128)(2,1)S(1)}, bf16[2,704,128]{2,1,0:T(8,128)(2,1)S(1)}, u32[]{:S(2)}, u32[]{:S(2)}) collective-permute-start(bf16[2,704,128]{2,1,0:T(8,128)(2,1)S(1)} %bitcast.10), channel_id=1, source_target_pairs={{0,2},{1,15},{2,4},{3,1},{4,6},{5,3},{6,8},{7,5},{8,10},{9,7},{10,... | collective-permute-start | bytes 1081352 | tf_op jit(solution)/shard_map/ppermute | solution.py:91
  32.3 17.6 %collective-permute-start.5 = (bf16[3,704,128]{2,1,0:T(8,128)(2,1)S(1)}, bf16[3,704,128]{2,1,0:T(8,128)(2,1)S(1)}, u32[]{:S(2)}, u32[]{:S(2)}) collective-permute-start(bf16[3,704,128]{2,1,0:T(8,128)(2,1)S(1)} %pad_maximum_fusion.1.mine_ref), channel_id=1, source_target_pairs={{0,1},{1,0},{2,3},{3,2},{4,5},{5,4},{6,7},{7,6},{8,9},{9,8},{10,11... | collective-permute-start | bytes 1622024 | tf_op jit(solution)/shard_map/ppermute | solution.py:93
  38.5 11.5 %collective-permute-start.1 = (bf16[2,704,128]{2,1,0:T(8,128)(2,1)S(1)}, bf16[2,704,128]{2,1,0:T(8,128)(2,1)S(1)}, u32[]{:S(2)}, u32[]{:S(2)}) collective-permute-start(bf16[2,704,128]{2,1,0:T(8,128)(2,1)S(1)} %collective-permute-done.a1_ref), channel_id=1, source_target_pairs={{0,2},{1,15},{2,4},{3,1},{4,6},{5,3},{6,8},{7,5},{8,10},{9,7},{10,... | collective-permute-start | bytes 1081352 | tf_op jit(solution)/shard_map/ppermute | solution.py:91
  52.5 32.2 %all-to-all-start = ((f32[8,128,384]{2,1,0:T(8,128)}), f32[8,128,384]{2,1,0:T(8,128)}, u32[]{:S(2)}, u32[]{:S(2)}) async-start(f32[8,128,384]{2,1,0:T(8,128)} %bitcast.6), calls=%async_computation | async-start | bytes 3145728 | tf_op jit(solution)/shard_map/all_to_all | solution.py:79
  56.8 14.8 %collective-permute-start.6 = (bf16[2,704,128]{2,1,0:T(8,128)(2,1)S(1)}, bf16[2,704,128]{2,1,0:T(8,128)(2,1)S(1)}, u32[]{:S(2)}, u32[]{:S(2)}) collective-permute-start(bf16[2,704,128]{2,1,0:T(8,128)(2,1)S(1)} %collective-permute-done.1.a2_ref.a0_ref), channel_id=1, source_target_pairs={{0,2},{1,15},{2,4},{3,1},{4,6},{5,3},{6,8},{7,5},{8,10},{9,7},{10,... | collective-permute-start | bytes 1081352 | tf_op jit(solution)/shard_map/ppermute | solution.py:91
  71.7 10.5 %collective-permute-start.7 = (bf16[2,704,128]{2,1,0:T(8,128)(2,1)S(1)}, bf16[2,704,128]{2,1,0:T(8,128)(2,1)S(1)}, u32[]{:S(2)}, u32[]{:S(2)}) collective-permute-start(bf16[2,704,128]{2,1,0:T(8,128)(2,1)S(1)} %collective-permute-done.6.a1_ref), channel_id=1, source_target_pairs={{0,2},{2,4},{4,6},{6,8},{8,10},{10,12},{12,14},{14,0},{16,18},{18,... | collective-permute-start | bytes 1081352 | tf_op jit(solution)/shard_map/ppermute | solution.py:91
  84.8 26.4 %all-to-all-start.1 = ((f32[8,128,384]{2,1,0:T(8,128)}), f32[8,128,384]{2,1,0:T(8,128)S(1)}, u32[]{:S(2)}, u32[]{:S(2)}) async-start(f32[8,128,384]{2,1,0:T(8,128)} %bitcast.8), calls=%async_computation.1 | async-start | bytes 3145728 | tf_op jit(solution)/shard_map/all_to_all | solution.py:79
  111.3 42.9 %copy-start.1 = (f32[128,384]{1,0:T(8,128)S(1)}, f32[128,384]{1,0:T(8,128)}, u32[]{:S(2)}) copy-start(f32[128,384]{1,0:T(8,128)} %param.5) | copy-start | bytes 589828
  134.8 19.4 %collective-permute-start.8 = (f32[128,384]{1,0:T(8,128)S(1)}, f32[128,384]{1,0:T(8,128)S(1)}, u32[]{:S(2)}, u32[]{:S(2)}) collective-permute-start(f32[128,384]{1,0:T(8,128)S(1)} %reduce_sum.29), channel_id=1, source_target_pairs={{0,14},{1,542},{2,48},{3,288},{4,338},{5,578},{6,100},{7,628},{8,1... | collective-permute-start | bytes 589832 | tf_op jit(solution)/shard_map/ppermute | solution.py:98

commit v3 on v2

v3 whole, which is shorter than its diff:
```python
import math

import jax
import jax.numpy as jnp
from jax import lax
from jax.experimental import pallas as pl
from jax.experimental.pallas import tpu as pltpu
from jax.sharding import Mesh
from jax.sharding import PartitionSpec as P

NX, NZL, NZH, NY, NC = 4, 4, 3, 8, 2
AXES = ("x", "zl", "zh", "y", "core")
TRIPLE = ((0, 11), (1, 6), (7, 12), (2, 13), (3, 8), (9, 14), (4, 15), (5, 10))
OFFSET = (((-1, -2), (-3, -4)), ((0, 1), (2, 3)))
LANES = 128
ROWS = 128
CODED = NZH * ROWS + 16
TOP = 32767.0


def triple_perm(i):
    return [
        (3 * TRIPLE[y][c] + (i + zh) % 3, zh * 16 + y * NC + c)
        for zh in range(NZH)
        for y in range(NY)
        for c in range(NC)
    ]


def ring_perm(cores):
    return [
        (y * NC + c, (y + 1 - 2 * c) % NY * NC + c) for y in range(NY) for c in cores
    ]


def place_perm():
    pairs = []
    for x in range(NX):
        for zl in range(NZL):
            for y in range(NY):
                for c in range(NC):
                    to_y = (y + OFFSET[zl % 2][zl // 2][x // 2]) % NY
                    source = ((x * NZL + zl) * NY + y) * NC + c
                    pairs.append((source, (TRIPLE[y][c] * NY + to_y) * NC + x % 2))
    return pairs


def encode(value, put):
    most = jnp.max(jnp.abs(value), axis=(0, 1), keepdims=True)
    e = jnp.ceil(4.0 / math.log(2.0) * jnp.log(jnp.maximum(most, 2.0**-120)))
    root = jnp.sqrt(jnp.abs(value)) * (TOP * jnp.exp(e * (-math.log(2.0) / 8)))
    q = jnp.where(value < 0, -root, root)
    q = jnp.round(q).astype(jnp.int32).astype(jnp.int16)
    for j in range(NZH):
        put(slice(j * ROWS, (j + 1) * ROWS), q[:, j * LANES : (j + 1) * LANES])
    scale = jnp.broadcast_to(e, (16, LANES)).astype(jnp.int32).astype(jnp.int16)
    put(slice(NZH * ROWS, CODED), scale)


def decode(ref, at):
    e = ref[at, NZH * ROWS : CODED].astype(jnp.int32).astype(jnp.float32)[0:1]
    scale = jnp.exp(e * (math.log(2.0) / 8)) * (1.0 / TOP)
    root = ref[at, 0 : NZH * ROWS].astype(jnp.int32).astype(jnp.float32) * scale
    return root * jnp.abs(root)


def store(ref, *at):
    def put(rows, value):
        ref[(*at, rows)] = value

    return put


def triple_kernel(at_ref, *refs):
    out_ref = refs[NZH]
    for i in range(NZH):
        j = lax.rem(i + at_ref[0], NZH)
        out_ref[:, pl.ds(pl.multiple_of(j * LANES, LANES), LANES)] = refs[i][...]


def product_kernel(at_ref, a0_ref, a1_ref, a2_ref, mine_ref, other_ref, out_ref):
    core = at_ref[1]
    for i, (up_ref, down_ref) in enumerate(((a1_ref, a0_ref), (a2_ref, a1_ref))):
        rows = [jnp.where(core == 0, up_ref[c], down_ref[c]) for c in range(NC)]
        rows = jnp.concatenate(rows, axis=1)
        for columns_ref, cw in ((mine_ref, core), (other_ref, 1 - core)):
            out = lax.dot_general(
                rows, columns_ref[...], (((0,), (0,)), ((), ())), preferred_element_type=jnp.float32
            )
            for c in range(NC):
                encode(out[c * ROWS : (c + 1) * ROWS], store(out_ref, i * NC + c, cw))


def sum_x_kernel(part_ref, out_ref):
    for c in range(NC):
        total = decode(part_ref, c)
        for x in range(1, NX):
            total = total + decode(part_ref, x * NC + c)
        blocks = [total[j * ROWS : (j + 1) * ROWS] for j in range(NZH)]
        encode(jnp.concatenate(blocks, axis=1), store(out_ref, c))


def sum_zl_kernel(part_ref, out_ref):
    total = decode(part_ref, 0)
    for zl in range(1, NZL):
        total = total + decode(part_ref, zl)
    for j in range(NZH):
        out_ref[:, j * LANES : (j + 1) * LANES] = total[j * ROWS : (j + 1) * ROWS]


def call(kernel, shape, dtype, flops, *arrays, scalars=False):
    specs = [pl.BlockSpec(memory_space=pltpu.VMEM)] * (len(arrays) - scalars)
    if scalars:
        specs = [pl.BlockSpec(memory_space=pltpu.SMEM)] + specs
    return pl.pallas_call(
        kernel,
        in_specs=specs,
        out_specs=pl.BlockSpec(memory_space=pltpu.VMEM),
        out_shape=jax.ShapeDtypeStruct(shape, dtype),
        compiler_params=pltpu.CompilerParams(vmem_limit_bytes=24 << 20),
        cost_estimate=pl.CostEstimate(flops=flops, bytes_accessed=2_000_000, transcendentals=0),
    )(*arrays)


def exchange(part, axes):
    return lax.all_to_all(part, axes, split_axis=0, concat_axis=0, tiled=True)


def body(activations, sample_rows, old_factor):
    block = activations.at[sample_rows].get(mode="promise_in_bounds")
    k = block.shape[0]
    scale = 0.1 / float(NX * NZL * k)
    at = jnp.stack([lax.axis_index("zh"), lax.axis_index("core")]).astype(jnp.int32)
    ring = [lax.all_gather(block, "core", axis=0)]
    for step in range(4):
        ring.append(lax.ppermute(ring[-1], ("y", "core"), ring_perm((0, 1) if step < 3 else (0,))))
    block, _ = lax.optimization_barrier((block, ring[0]))
    mine = [lax.ppermute(block, ("zh", "y", "core"), triple_perm(i)) for i in range(NZH)]
    *mine, ring[1] = lax.optimization_barrier((*mine, ring[1]))
    mine = call(triple_kernel, (k, 384), jnp.bfloat16, 0, at, *mine, scalars=True)
    other = lax.ppermute(mine, "core", [(0, 1), (1, 0)])
    part = []
    for half in range(2):
        out = call(
            product_kernel, (NX, NC, CODED, LANES), jnp.int16, 2 * k * 512 * 768,
            at, *ring[2 * half : 2 * half + 3], mine, other, scalars=True,
        )
        out = exchange(out.reshape(NX * NC, CODED, LANES), ("x", "core"))
        part.append(call(sum_x_kernel, (NC, CODED, LANES), jnp.int16, 0, out))
    part = exchange(jnp.concatenate(part, axis=0), "zl")
    total = call(sum_zl_kernel, (ROWS, 384), jnp.float32, 0, part)
    total = lax.ppermute(total, ("x", "zl", "y", "core"), place_perm())
    return 0.9 * old_factor + scale * total


def solution(mesh):
    fine = Mesh(mesh.devices.reshape(NX, NZL, NZH, NY, NC), AXES)
    dp, tensor = ("x", "zl"), ("zh", "y", "core")
    return jax.shard_map(
        body,
        mesh=fine,
        in_specs=(P(dp, tensor), P(dp), P(tensor, dp)),
        out_specs=P(tensor, dp),
        check_vma=False,
    )
```

time: 156 us -> 140 us (0.90)
  waiting for transfers between devices: 61.1 us -> 47.7 us
  blocking collectives: 25.5 us -> 16.5 us
  starting transfers between devices: 57.5 us -> 62.6 us
  Pallas kernels: 5.11 us -> 8.39 us
  other arithmetic: 3.32 us -> 1.56 us
    all_to_all x1, blocking collectives: 23.4 us -> 14.5 us  [exchange(): return lax.all_to_all(part, axes, split_axis=0, concat_axis=0, tiled=True)]
    ppermute x4, waiting for transfers between devices: 25.3 us -> 17.7 us  [body(): lax.ppermute(ring[-1], ('y', 'core'), ring_perm((0, 1) if step < 3 else (...]
    ppermute x1, starting transfers between devices: 3.79 us -> 11.3 us  [body(): other = lax.ppermute(mine, 'core', [(0, 1), (1, 0)])]
    all_to_all x2, waiting for transfers between devices: 20.1 us -> 12.9 us  [exchange(): return lax.all_to_all(part, axes, split_axis=0, concat_axis=0, tiled=True)]
    pallas_call x2 -> x6, Pallas kernels: 5.11 us -> 8.39 us  [call(): pl.pallas_call(kernel, in_specs=specs, out_specs=pl.BlockSpec(memory_spac...]
    ppermute x3, starting transfers between devices: 24.1 us -> 21.5 us  [body(): lax.ppermute(block, ('zh', 'y', 'core'), triple_perm(i))]
    ppermute x4, starting transfers between devices: 15.7 us -> 13.8 us  [body(): lax.ppermute(ring[-1], ('y', 'core'), ring_perm((0, 1) if step < 3 else (...]
    all_to_all x2, starting transfers between devices: 9.1 us -> 10.9 us  [exchange(): return lax.all_to_all(part, axes, split_axis=0, concat_axis=0, tiled=True)]
  transfers between devices with their start and end apart: 11 -> 11, of which waited for: 7 -> 6; matrix products, arithmetic and copies ran while one was open for 1% -> 0% of each run, Pallas kernels for 2% -> 5%
where the time goes in v3:
time: 140 us; the launch traced here: 139 us
  starting transfers between devices  62.6 us (45%)
  waiting for transfers between devices  47.7 us (34%)
  blocking collectives  16.5 us (12%)
  Pallas kernels  8.39 us (6%)
  local copies, waits for them, and re-layouts  2.25 us (2%)
  other arithmetic  1.56 us (1%)
    ppermute x3, starting transfers between devices, body(): lax.ppermute(block, ('zh', 'y', 'core'), triple_perm(i))  21.5 us
    ppermute x4, waiting for transfers between devices, body(): lax.ppermute(ring[-1], ('y', 'core'), ring_perm((0, 1) if step < 3 else (...  17.7 us
    all_to_all x1, blocking collectives, exchange(): return lax.all_to_all(part, axes, split_axis=0, concat_axis=0, tiled=True)  14.5 us
    ppermute x1, waiting for transfers between devices, body(): total = lax.ppermute(total, ('x', 'zl', 'y', 'core'), place_perm())  14.2 us
    ppermute x4, starting transfers between devices, body(): lax.ppermute(ring[-1], ('y', 'core'), ring_perm((0, 1) if step < 3 else (...  13.8 us
    all_to_all x2, waiting for transfers between devices, exchange(): return lax.all_to_all(part, axes, split_axis=0, concat_axis=0, tiled=True)  12.9 us
    ppermute x1, starting transfers between devices, body(): other = lax.ppermute(mine, 'core', [(0, 1), (1, 0)])  11.3 us
    all_to_all x2, starting transfers between devices, exchange(): return lax.all_to_all(part, axes, split_axis=0, concat_axis=0, tiled=True)  10.9 us
  transfers between devices with their start and end apart: 11, of which 6 were waited for; matrix products, arithmetic and copies ran while one was open for 0% of the time, Pallas kernels for 5%

profile of v3, /device:TPU:8, one launch (start us, length us, event | category | flops | bytes accessed | tf_op | source)
XLA Modules:
  0.0 139.2 jit_solution(3201146397936661584)
XLA Ops:
  0.0 0.7 compare_select_fusion
  0.7 0.2 copy-done
  1.0 2.0 %gather_fusion = bf16[704,128]{1,0:T(8,128)(2,1)S(1)} fusion(bf16[1024,128]{1,0:T(8,128)(2,1)S(1)} %copy-done, s32[1024]{0:T(1024)S(1)} %pad_clamp_fusion), kind=kCustom, calls=%fused_computation | custom fusion | bytes 363264 | tf_op jit(solution)/shard_map/gather | solution.py:130
  3.0 2.1 %all-gather = bf16[1408,128]{1,0:T(8,128)(2,1)S(1)} all-gather(bf16[704,128]{1,0:T(8,128)(2,1)S(1)} %gather_fusion), channel_id=2, replica_groups=mesh['x'=4,'zl'=4,'zh'=3,'y'=8,'core'=2] {'core'}, dimensions={0}, use_global_device_ids=true | all-gather | bytes 540672 | tf_op jit(solution)/shard_map/all_gather | solution.py:134
  5.1 3.5 %collective-permute-start.3 = (bf16[2,704,128]{2,1,0:T(8,128)(2,1)S(1)}, bf16[2,704,128]{2,1,0:T(8,128)(2,1)S(1)}, u32[]{:S(2)}, u32[]{:S(2)}) collective-permute-start(bf16[2,704,128]{2,1,0:T(8,128)(2,1)S(1)} %bitcast.5), channel_id=1, source_target_pairs={{0,2},{1,15},{2,4},{3,1},{4,6},{5,3},{6,8},{7,5},{8,10},{9,7},{10,... | collective-permute-start | bytes 1081352 | tf_op jit(solution)/shard_map/ppermute | solution.py:136
  8.5 14.4 %collective-permute-start = (bf16[704,128]{1,0:T(8,128)(2,1)S(1)}, bf16[704,128]{1,0:T(8,128)(2,1)S(1)}, u32[]{:S(2)}, u32[]{:S(2)}) collective-permute-start(bf16[704,128]{1,0:T(8,128)(2,1)S(1)} %gather_fusion), channel_id=1, source_target_pairs={{0,0},{33,1},{3,2},{18,3},{21,4},{36,5},{6,6},{39,7},{9,8},{24,9},... | collective-permute-start | bytes 540680 | tf_op jit(solution)/shard_map/ppermute | solution.py:138
  23.0 1.9 %collective-permute-start.1 = (bf16[704,128]{1,0:T(8,128)(2,1)S(1)}, bf16[704,128]{1,0:T(8,128)(2,1)S(1)}, u32[]{:S(2)}, u32[]{:S(2)}) collective-permute-start(bf16[704,128]{1,0:T(8,128)(2,1)S(1)} %gather_fusion), channel_id=1, source_target_pairs={{1,0},{34,1},{4,2},{19,3},{22,4},{37,5},{7,6},{40,7},{10,8},{25,9}... | collective-permute-start | bytes 540680 | tf_op jit(solution)/shard_map/ppermute | solution.py:138
  24.9 5.2 %collective-permute-start.2 = (bf16[704,128]{1,0:T(8,128)(2,1)S(1)}, bf16[704,128]{1,0:T(8,128)(2,1)S(1)}, u32[]{:S(2)}, u32[]{:S(2)}) collective-permute-start(bf16[704,128]{1,0:T(8,128)(2,1)S(1)} %gather_fusion), channel_id=1, source_target_pairs={{2,0},{35,1},{5,2},{20,3},{23,4},{38,5},{8,6},{41,7},{11,8},{26,9}... | collective-permute-start | bytes 540680 | tf_op jit(solution)/shard_map/ppermute | solution.py:138
  30.1 0.1 pad_add_fusion.1.at_ref
  30.2 0.0 collective-permute-done.refs_0_
  30.2 0.5 collective-permute-done.1.refs_1_
  30.7 2.4 %collective-permute-done.2.refs_2_ = bf16[704,128]{1,0:T(8,128)(2,1)S(1)} collective-permute-done((bf16[704,128]{1,0:T(8,128)(2,1)S(1)}, bf16[704,128]{1,0:T(8,128)(2,1)S(1)}, u32[]{:S(2)}, u32[]{:S(2)}) %collective-permute-start.2) | collective-permute-done | bytes 180256 | tf_op jit(solution)/shard_map/ppermute | solution.py:138
  33.1 0.0 collective-permute-done.3.a1_ref
  33.1 0.6 shard_map.37.mine_ref
  33.7 11.3 %collective-permute-start.5 = (bf16[704,384]{1,0:T(8,128)(2,1)S(1)}, bf16[704,384]{1,0:T(8,128)(2,1)S(1)}, u32[]{:S(2)}, u32[]{:S(2)}) collective-permute-start(bf16[704,384]{1,0:T(8,128)(2,1)S(1)} %shard_map.37.mine_ref), channel_id=1, source_target_pairs={{0,1},{1,0},{2,3},{3,2},{4,5},{5,4},{6,7},{7,6},{8,9},{9,8},{10,11... | collective-permute-start | bytes 1622024 | tf_op jit(solution)/shard_map/ppermute | solution.py:141
  45.0 4.5 %collective-permute-start.4 = (bf16[2,704,128]{2,1,0:T(8,128)(2,1)S(1)}, bf16[2,704,128]{2,1,0:T(8,128)(2,1)S(1)}, u32[]{:S(2)}, u32[]{:S(2)}) collective-permute-start(bf16[2,704,128]{2,1,0:T(8,128)(2,1)S(1)} %collective-permute-done.3.a1_ref), channel_id=1, source_target_pairs={{0,2},{1,15},{2,4},{3,1},{4,6},{5,3},{6,8},{7,5},{8,10},{9,7},{10,... | collective-permute-start | bytes 1081352 | tf_op jit(solution)/shard_map/ppermute | solution.py:136
  49.6 9.6 %collective-permute-done.4.a2_ref.a0_ref = bf16[2,704,128]{2,1,0:T(8,128)(2,1)S(1)} collective-permute-done((bf16[2,704,128]{2,1,0:T(8,128)(2,1)S(1)}, bf16[2,704,128]{2,1,0:T(8,128)(2,1)S(1)}, u32[]{:S(2)}, u32[]{:S(2)}) %collective-permute-start.4) | collective-permute-done | bytes 360480 | tf_op jit(solution)/shard_map/ppermute | solution.py:136
  59.2 3.2 %collective-permute-start.6 = (bf16[2,704,128]{2,1,0:T(8,128)(2,1)S(1)}, bf16[2,704,128]{2,1,0:T(8,128)(2,1)S(1)}, u32[]{:S(2)}, u32[]{:S(2)}) collective-permute-start(bf16[2,704,128]{2,1,0:T(8,128)(2,1)S(1)} %collective-permute-done.4.a2_ref.a0_ref), channel_id=1, source_target_pairs={{0,2},{1,15},{2,4},{3,1},{4,6},{5,3},{6,8},{7,5},{8,10},{9,7},{10,... | collective-permute-start | bytes 1081352 | tf_op jit(solution)/shard_map/ppermute | solution.py:136
  62.4 3.2 %shard_map.38 = s16[4,2,400,128]{3,2,1,0:T(8,128)(2,1)} custom-call(s32[2]{0:T(128)S(1)} %pad_add_fusion.1.at_ref, bf16[2,704,128]{2,1,0:T(8,128)(2,1)S(1)} %bitcast.6, bf16[2,704,128]{2,1,0:T(8,128)(2,1)S(1)} %collective-permute-done.3.a1_ref, bf16[2,704,128]{2,1,0:T(8,128)(2,1)S(1)} %collective-permute-done.4.a2_ref.a0_ref, ...), custom_call_target="tpu_custom_call" | custom-call | flops 553648128 | bytes 2000000 | tf_op jit(solution)/shard_map/pallas_call | solution.py:115
  65.6 6.1 %all-to-all-start = ((s16[8,400,128]{2,1,0:T(8,128)(2,1)}), s16[8,400,128]{2,1,0:T(8,128)(2,1)S(1)}, u32[]{:S(2)}, u32[]{:S(2)}) async-start(s16[8,400,128]{2,1,0:T(8,128)(2,1)} %bitcast.3), calls=%async_computation | async-start | bytes 1638400 | tf_op jit(solution)/shard_map/all_to_all | solution.py:126
  71.7 2.6 %collective-permute-start.7 = (bf16[2,704,128]{2,1,0:T(8,128)(2,1)S(1)}, bf16[2,704,128]{2,1,0:T(8,128)(2,1)S(1)}, u32[]{:S(2)}, u32[]{:S(2)}) collective-permute-start(bf16[2,704,128]{2,1,0:T(8,128)(2,1)S(1)} %collective-permute-done.6.a1_ref), channel_id=1, source_target_pairs={{0,2},{2,4},{4,6},{6,8},{8,10},{10,12},{12,14},{14,0},{16,18},{18,... | collective-permute-start | bytes 1081352 | tf_op jit(solution)/shard_map/ppermute | solution.py:136
  74.3 8.1 %collective-permute-done.7.a2_ref = bf16[2,704,128]{2,1,0:T(8,128)(2,1)S(1)} collective-permute-done((bf16[2,704,128]{2,1,0:T(8,128)(2,1)S(1)}, bf16[2,704,128]{2,1,0:T(8,128)(2,1)S(1)}, u32[]{:S(2)}, u32[]{:S(2)}) %collective-permute-start.7) | collective-permute-done | bytes 360480 | tf_op jit(solution)/shard_map/ppermute | solution.py:136
  82.4 3.2 %shard_map.40 = s16[4,2,400,128]{3,2,1,0:T(8,128)(2,1)} custom-call(s32[2]{0:T(128)S(1)} %pad_add_fusion.1.at_ref, bf16[2,704,128]{2,1,0:T(8,128)(2,1)S(1)} %collective-permute-done.4.a2_ref.a0_ref, bf16[2,704,128]{2,1,0:T(8,128)(2,1)S(1)} %collective-permute-done.6.a1_ref, bf16[2,704,128]{2,1,0:T(8,128)(2,1)S(1)} %collective-permute-done.7.a2_ref, ...), custom_call_target="tpu_custom_call" | custom-call | flops 553648128 | bytes 2000000 | tf_op jit(solution)/shard_map/pallas_call | solution.py:115
  85.6 4.8 %all-to-all-start.1 = ((s16[8,400,128]{2,1,0:T(8,128)(2,1)}), s16[8,400,128]{2,1,0:T(8,128)(2,1)S(1)}, u32[]{:S(2)}, u32[]{:S(2)}) async-start(s16[8,400,128]{2,1,0:T(8,128)(2,1)} %bitcast.4), calls=%async_computation.1 | async-start | bytes 1638400 | tf_op jit(solution)/shard_map/all_to_all | solution.py:126
  90.4 0.6 shard_map.39
  91.0 12.9 %all-to-all-done.1.part_ref = s16[8,400,128]{2,1,0:T(8,128)(2,1)S(1)} async-done(((s16[8,400,128]{2,1,0:T(8,128)(2,1)}), s16[8,400,128]{2,1,0:T(8,128)(2,1)S(1)}, u32[]{:S(2)}, u32[]{:S(2)}) %all-to-all-start.1) | async-done | bytes 819232 | tf_op jit(solution)/shard_map/all_to_all | solution.py:126
  103.9 0.6 shard_map.41
  104.5 14.5 %all_to_all.15.part_ref = s16[4,400,128]{2,1,0:T(8,128)(2,1)S(1)} all-to-all(s16[4,400,128]{2,1,0:T(8,128)(2,1)S(1)} %pad_add_fusion), channel_id=1, replica_groups=mesh['x'=4,'zl'=4,'zh'=3,'y'=8,'core'=2] {'zl'}, dimensions={0} | all-to-all | bytes 819200 | tf_op jit(solution)/shard_map/all_to_all | solution.py:126
  119.0 0.2 shard_map.42
  119.2 5.1 %collective-permute-start.8 = (f32[128,384]{1,0:T(8,128)S(1)}, f32[128,384]{1,0:T(8,128)S(1)}, u32[]{:S(2)}, u32[]{:S(2)}) collective-permute-start(f32[128,384]{1,0:T(8,128)S(1)} %shard_map.42), channel_id=1, source_target_pairs={{0,14},{1,542},{2,48},{3,288},{4,338},{5,578},{6,100},{7,628},{8,1... | collective-permute-start | bytes 589832 | tf_op jit(solution)/shard_map/ppermute | solution.py:152
  124.3 14.2 %collective-permute-done.8 = f32[128,384]{1,0:T(8,128)S(1)} collective-permute-done((f32[128,384]{1,0:T(8,128)S(1)}, f32[128,384]{1,0:T(8,128)S(1)}, u32[]{:S(2)}, u32[]{:S(2)}) %collective-permute-start.8) | collective-permute-done | bytes 196640 | tf_op jit(solution)/shard_map/ppermute | solution.py:152
  138.5 0.7 multiply_add_fusion
  (8 shorter events, 0.1 us)
Async XLA Ops:
  0.0 1.0 copy-start
  5.1 28.0 %collective-permute-start.3 = (bf16[2,704,128]{2,1,0:T(8,128)(2,1)S(1)}, bf16[2,704,128]{2,1,0:T(8,128)(2,1)S(1)}, u32[]{:S(2)}, u32[]{:S(2)}) collective-permute-start(bf16[2,704,128]{2,1,0:T(8,128)(2,1)S(1)} %bitcast.5), channel_id=1, source_target_pairs={{0,2},{1,15},{2,4},{3,1},{4,6},{5,3},{6,8},{7,5},{8,10},{9,7},{10,... | collective-permute-start | bytes 1081352 | tf_op jit(solution)/shard_map/ppermute | solution.py:136
  8.5 21.6 %collective-permute-start = (bf16[704,128]{1,0:T(8,128)(2,1)S(1)}, bf16[704,128]{1,0:T(8,128)(2,1)S(1)}, u32[]{:S(2)}, u32[]{:S(2)}) collective-permute-start(bf16[704,128]{1,0:T(8,128)(2,1)S(1)} %gather_fusion), channel_id=1, source_target_pairs={{0,0},{33,1},{3,2},{18,3},{21,4},{36,5},{6,6},{39,7},{9,8},{24,9},... | collective-permute-start | bytes 540680 | tf_op jit(solution)/shard_map/ppermute | solution.py:138
  23.0 7.7 %collective-permute-start.1 = (bf16[704,128]{1,0:T(8,128)(2,1)S(1)}, bf16[704,128]{1,0:T(8,128)(2,1)S(1)}, u32[]{:S(2)}, u32[]{:S(2)}) collective-permute-start(bf16[704,128]{1,0:T(8,128)(2,1)S(1)} %gather_fusion), channel_id=1, source_target_pairs={{1,0},{34,1},{4,2},{19,3},{22,4},{37,5},{7,6},{40,7},{10,8},{25,9}... | collective-permute-start | bytes 540680 | tf_op jit(solution)/shard_map/ppermute | solution.py:138
  24.9 8.2 %collective-permute-start.2 = (bf16[704,128]{1,0:T(8,128)(2,1)S(1)}, bf16[704,128]{1,0:T(8,128)(2,1)S(1)}, u32[]{:S(2)}, u32[]{:S(2)}) collective-permute-start(bf16[704,128]{1,0:T(8,128)(2,1)S(1)} %gather_fusion), channel_id=1, source_target_pairs={{2,0},{35,1},{5,2},{20,3},{23,4},{38,5},{8,6},{41,7},{11,8},{26,9}... | collective-permute-start | bytes 540680 | tf_op jit(solution)/shard_map/ppermute | solution.py:138
  33.7 28.6 %collective-permute-start.5 = (bf16[704,384]{1,0:T(8,128)(2,1)S(1)}, bf16[704,384]{1,0:T(8,128)(2,1)S(1)}, u32[]{:S(2)}, u32[]{:S(2)}) collective-permute-start(bf16[704,384]{1,0:T(8,128)(2,1)S(1)} %shard_map.37.mine_ref), channel_id=1, source_target_pairs={{0,1},{1,0},{2,3},{3,2},{4,5},{5,4},{6,7},{7,6},{8,9},{9,8},{10,11... | collective-permute-start | bytes 1622024 | tf_op jit(solution)/shard_map/ppermute | solution.py:141
  45.0 14.1 %collective-permute-start.4 = (bf16[2,704,128]{2,1,0:T(8,128)(2,1)S(1)}, bf16[2,704,128]{2,1,0:T(8,128)(2,1)S(1)}, u32[]{:S(2)}, u32[]{:S(2)}) collective-permute-start(bf16[2,704,128]{2,1,0:T(8,128)(2,1)S(1)} %collective-permute-done.3.a1_ref), channel_id=1, source_target_pairs={{0,2},{1,15},{2,4},{3,1},{4,6},{5,3},{6,8},{7,5},{8,10},{9,7},{10,... | collective-permute-start | bytes 1081352 | tf_op jit(solution)/shard_map/ppermute | solution.py:136
  59.2 12.5 %collective-permute-start.6 = (bf16[2,704,128]{2,1,0:T(8,128)(2,1)S(1)}, bf16[2,704,128]{2,1,0:T(8,128)(2,1)S(1)}, u32[]{:S(2)}, u32[]{:S(2)}) collective-permute-start(bf16[2,704,128]{2,1,0:T(8,128)(2,1)S(1)} %collective-permute-done.4.a2_ref.a0_ref), channel_id=1, source_target_pairs={{0,2},{1,15},{2,4},{3,1},{4,6},{5,3},{6,8},{7,5},{8,10},{9,7},{10,... | collective-permute-start | bytes 1081352 | tf_op jit(solution)/shard_map/ppermute | solution.py:136
  65.6 20.0 %all-to-all-start = ((s16[8,400,128]{2,1,0:T(8,128)(2,1)}), s16[8,400,128]{2,1,0:T(8,128)(2,1)S(1)}, u32[]{:S(2)}, u32[]{:S(2)}) async-start(s16[8,400,128]{2,1,0:T(8,128)(2,1)} %bitcast.3), calls=%async_computation | async-start | bytes 1638400 | tf_op jit(solution)/shard_map/all_to_all | solution.py:126
  71.7 10.7 %collective-permute-start.7 = (bf16[2,704,128]{2,1,0:T(8,128)(2,1)S(1)}, bf16[2,704,128]{2,1,0:T(8,128)(2,1)S(1)}, u32[]{:S(2)}, u32[]{:S(2)}) collective-permute-start(bf16[2,704,128]{2,1,0:T(8,128)(2,1)S(1)} %collective-permute-done.6.a1_ref), channel_id=1, source_target_pairs={{0,2},{2,4},{4,6},{6,8},{8,10},{10,12},{12,14},{14,0},{16,18},{18,... | collective-permute-start | bytes 1081352 | tf_op jit(solution)/shard_map/ppermute | solution.py:136
  85.6 18.3 %all-to-all-start.1 = ((s16[8,400,128]{2,1,0:T(8,128)(2,1)}), s16[8,400,128]{2,1,0:T(8,128)(2,1)S(1)}, u32[]{:S(2)}, u32[]{:S(2)}) async-start(s16[8,400,128]{2,1,0:T(8,128)(2,1)} %bitcast.4), calls=%async_computation.1 | async-start | bytes 1638400 | tf_op jit(solution)/shard_map/all_to_all | solution.py:126
  119.0 19.5 %copy-start.1 = (f32[128,384]{1,0:T(8,128)S(1)}, f32[128,384]{1,0:T(8,128)}, u32[]{:S(2)}) copy-start(f32[128,384]{1,0:T(8,128)} %param.5) | copy-start | bytes 589828
  119.2 19.3 %collective-permute-start.8 = (f32[128,384]{1,0:T(8,128)S(1)}, f32[128,384]{1,0:T(8,128)S(1)}, u32[]{:S(2)}, u32[]{:S(2)}) collective-permute-start(f32[128,384]{1,0:T(8,128)S(1)} %shard_map.42), channel_id=1, source_target_pairs={{0,14},{1,542},{2,48},{3,288},{4,338},{5,578},{6,100},{7,628},{8,1... | collective-permute-start | bytes 589832 | tf_op jit(solution)/shard_map/ppermute | solution.py:152

commit v4 on v3

--- a/solution.py
+++ b/solution.py
@@ -91,13 +91,17 @@
                 encode(out[c * ROWS : (c + 1) * ROWS], store(out_ref, i * NC + c, cw))
 
 
-def sum_x_kernel(part_ref, out_ref):
+def sum_x_kernel(part_ref, *refs):
+    out_ref = refs[-1]
+    done = out_ref.shape[0] - NC
+    for c in range(done):
+        out_ref[c] = refs[0][c]
     for c in range(NC):
         total = decode(part_ref, c)
         for x in range(1, NX):
             total = total + decode(part_ref, x * NC + c)
         blocks = [total[j * ROWS : (j + 1) * ROWS] for j in range(NZH)]
-        encode(jnp.concatenate(blocks, axis=1), store(out_ref, c))
+        encode(jnp.concatenate(blocks, axis=1), store(out_ref, done + c))
 
 
 def sum_zl_kernel(part_ref, out_ref):
@@ -136,8 +140,8 @@
         ring.append(lax.ppermute(ring[-1], ("y", "core"), ring_perm((0, 1) if step < 3 else (0,))))
     block, _ = lax.optimization_barrier((block, ring[0]))
     mine = [lax.ppermute(block, ("zh", "y", "core"), triple_perm(i)) for i in range(NZH)]
-    *mine, ring[1] = lax.optimization_barrier((*mine, ring[1]))
-    mine = call(triple_kernel, (k, 384), jnp.bfloat16, 0, at, *mine, scalars=True)
+    mine = call(triple_kernel, (k, 384), jnp.bfloat16, 10**10, at, *mine, scalars=True)
+    mine, ring[2] = lax.optimization_barrier((mine, ring[2]))
     other = lax.ppermute(mine, "core", [(0, 1), (1, 0)])
     part = []
     for half in range(2):
@@ -146,8 +150,8 @@
             at, *ring[2 * half : 2 * half + 3], mine, other, scalars=True,
         )
         out = exchange(out.reshape(NX * NC, CODED, LANES), ("x", "core"))
-        part.append(call(sum_x_kernel, (NC, CODED, LANES), jnp.int16, 0, out))
-    part = exchange(jnp.concatenate(part, axis=0), "zl")
+        part = [call(sum_x_kernel, (NC * (half + 1), CODED, LANES), jnp.int16, 0, out, *part)]
+    part = exchange(part[0], "zl")
     total = call(sum_zl_kernel, (ROWS, 384), jnp.float32, 0, part)
     total = lax.ppermute(total, ("x", "zl", "y", "core"), place_perm())
     return 0.9 * old_factor + scale * total

time: 140 us -> 131 us (0.936)
  starting transfers between devices: 62.6 us -> 55.2 us
    ppermute x1, starting transfers between devices: 11.3 us -> 1.91 us  [body(): other = lax.ppermute(mine, 'core', [(0, 1), (1, 0)])]
    ppermute x3, waiting for transfers between devices: 2.9 us -> 0.77 us  [body(): lax.ppermute(block, ('zh', 'y', 'core'), triple_perm(i))]
    all_to_all x2, starting transfers between devices: 10.9 us -> 12.7 us  [exchange(): return lax.all_to_all(part, axes, split_axis=0, concat_axis=0, tiled=True)]
  transfers between devices with their start and end apart: 11 -> 11, of which waited for: 6 -> 5; matrix products, arithmetic and copies ran while one was open for 0% -> 0% of each run, Pallas kernels for 5% -> 6%
where the time goes in v4:
time: 131 us
  starting transfers between devices  55.2 us (42%)
  waiting for transfers between devices  46.7 us (36%)
  blocking collectives  16.5 us (13%)
  Pallas kernels  8.38 us (6%)
  local copies, waits for them, and re-layouts  2.25 us (2%)
  other arithmetic  1.53 us (1%)
    ppermute x3, starting transfers between devices, body(): lax.ppermute(block, ('zh', 'y', 'core'), triple_perm(i))  21.5 us
    ppermute x4, waiting for transfers between devices, body(): lax.ppermute(ring[-1], ('y', 'core'), ring_perm((0, 1) if step < 3 else (...  17.8 us
    ppermute x1, waiting for transfers between devices, body(): total = lax.ppermute(total, ('x', 'zl', 'y', 'core'), place_perm())  15.2 us
    all_to_all x1, blocking collectives, exchange(): return lax.all_to_all(part, axes, split_axis=0, concat_axis=0, tiled=True)  14.5 us
    ppermute x4, starting transfers between devices, body(): lax.ppermute(ring[-1], ('y', 'core'), ring_perm((0, 1) if step < 3 else (...  14.1 us
    all_to_all x2, waiting for transfers between devices, exchange(): return lax.all_to_all(part, axes, split_axis=0, concat_axis=0, tiled=True)  12.9 us
    all_to_all x2, starting transfers between devices, exchange(): return lax.all_to_all(part, axes, split_axis=0, concat_axis=0, tiled=True)  12.7 us
    pallas_call x6, Pallas kernels, call(): pl.pallas_call(kernel, in_specs=specs, out_specs=pl.BlockSpec(memory_spac...  8.38 us
  transfers between devices with their start and end apart: 11, of which 5 were waited for; matrix products, arithmetic and copies ran while one was open for 0% of the time, Pallas kernels for 6%

profile of v4, /device:TPU:8, one launch (start us, length us, event | category | flops | bytes accessed | tf_op | source)
XLA Modules:
  0.0 130.7 jit_solution(711301416147726909)
XLA Ops:
  0.0 0.7 compare_select_fusion
  0.7 0.2 copy-done
  1.0 2.0 %gather_fusion = bf16[704,128]{1,0:T(8,128)(2,1)S(1)} fusion(bf16[1024,128]{1,0:T(8,128)(2,1)S(1)} %copy-done, s32[1024]{0:T(1024)S(1)} %pad_clamp_fusion), kind=kCustom, calls=%fused_computation | custom fusion | bytes 363264 | tf_op jit(solution)/shard_map/gather | solution.py:134
  3.0 2.1 %all-gather = bf16[1408,128]{1,0:T(8,128)(2,1)S(1)} all-gather(bf16[704,128]{1,0:T(8,128)(2,1)S(1)} %gather_fusion), channel_id=2, replica_groups=mesh['x'=4,'zl'=4,'zh'=3,'y'=8,'core'=2] {'core'}, dimensions={0}, use_global_device_ids=true | all-gather | bytes 540672 | tf_op jit(solution)/shard_map/all_gather | solution.py:138
  5.1 3.5 %collective-permute-start.3 = (bf16[2,704,128]{2,1,0:T(8,128)(2,1)S(1)}, bf16[2,704,128]{2,1,0:T(8,128)(2,1)S(1)}, u32[]{:S(2)}, u32[]{:S(2)}) collective-permute-start(bf16[2,704,128]{2,1,0:T(8,128)(2,1)S(1)} %bitcast.5), channel_id=1, source_target_pairs={{0,2},{1,15},{2,4},{3,1},{4,6},{5,3},{6,8},{7,5},{8,10},{9,7},{10,... | collective-permute-start | bytes 1081352 | tf_op jit(solution)/shard_map/ppermute | solution.py:140
  8.5 14.4 %collective-permute-start = (bf16[704,128]{1,0:T(8,128)(2,1)S(1)}, bf16[704,128]{1,0:T(8,128)(2,1)S(1)}, u32[]{:S(2)}, u32[]{:S(2)}) collective-permute-start(bf16[704,128]{1,0:T(8,128)(2,1)S(1)} %gather_fusion), channel_id=1, source_target_pairs={{0,0},{33,1},{3,2},{18,3},{21,4},{36,5},{6,6},{39,7},{9,8},{24,9},... | collective-permute-start | bytes 540680 | tf_op jit(solution)/shard_map/ppermute | solution.py:142
  23.0 1.9 %collective-permute-start.1 = (bf16[704,128]{1,0:T(8,128)(2,1)S(1)}, bf16[704,128]{1,0:T(8,128)(2,1)S(1)}, u32[]{:S(2)}, u32[]{:S(2)}) collective-permute-start(bf16[704,128]{1,0:T(8,128)(2,1)S(1)} %gather_fusion), channel_id=1, source_target_pairs={{1,0},{34,1},{4,2},{19,3},{22,4},{37,5},{7,6},{40,7},{10,8},{25,9}... | collective-permute-start | bytes 540680 | tf_op jit(solution)/shard_map/ppermute | solution.py:142
  24.9 5.2 %collective-permute-start.2 = (bf16[704,128]{1,0:T(8,128)(2,1)S(1)}, bf16[704,128]{1,0:T(8,128)(2,1)S(1)}, u32[]{:S(2)}, u32[]{:S(2)}) collective-permute-start(bf16[704,128]{1,0:T(8,128)(2,1)S(1)} %gather_fusion), channel_id=1, source_target_pairs={{2,0},{35,1},{5,2},{20,3},{23,4},{38,5},{8,6},{41,7},{11,8},{26,9}... | collective-permute-start | bytes 540680 | tf_op jit(solution)/shard_map/ppermute | solution.py:142
  30.1 0.1 pad_add_fusion.at_ref
  30.2 0.0 collective-permute-done.3.a1_ref
  30.2 2.1 %collective-permute-start.4 = (bf16[2,704,128]{2,1,0:T(8,128)(2,1)S(1)}, bf16[2,704,128]{2,1,0:T(8,128)(2,1)S(1)}, u32[]{:S(2)}, u32[]{:S(2)}) collective-permute-start(bf16[2,704,128]{2,1,0:T(8,128)(2,1)S(1)} %collective-permute-done.3.a1_ref), channel_id=1, source_target_pairs={{0,2},{1,15},{2,4},{3,1},{4,6},{5,3},{6,8},{7,5},{8,10},{9,7},{10,... | collective-permute-start | bytes 1081352 | tf_op jit(solution)/shard_map/ppermute | solution.py:140
  32.3 0.8 collective-permute-done.2.refs_2_
  33.1 0.6 shard_map.37.mine_ref
  33.7 9.8 %collective-permute-done.4.a0_ref.a2_ref = bf16[2,704,128]{2,1,0:T(8,128)(2,1)S(1)} collective-permute-done((bf16[2,704,128]{2,1,0:T(8,128)(2,1)S(1)}, bf16[2,704,128]{2,1,0:T(8,128)(2,1)S(1)}, u32[]{:S(2)}, u32[]{:S(2)}) %collective-permute-start.4) | collective-permute-done | bytes 360480 | tf_op jit(solution)/shard_map/ppermute | solution.py:140
  43.5 1.9 %collective-permute-start.7 = (bf16[704,384]{1,0:T(8,128)(2,1)S(1)}, bf16[704,384]{1,0:T(8,128)(2,1)S(1)}, u32[]{:S(2)}, u32[]{:S(2)}) collective-permute-start(bf16[704,384]{1,0:T(8,128)(2,1)S(1)} %shard_map.37.mine_ref), channel_id=1, source_target_pairs={{0,1},{1,0},{2,3},{3,2},{4,5},{5,4},{6,7},{7,6},{8,9},{9,8},{10,11... | collective-permute-start | bytes 1622024 | tf_op jit(solution)/shard_map/ppermute | solution.py:145
  45.4 4.2 %collective-permute-start.5 = (bf16[2,704,128]{2,1,0:T(8,128)(2,1)S(1)}, bf16[2,704,128]{2,1,0:T(8,128)(2,1)S(1)}, u32[]{:S(2)}, u32[]{:S(2)}) collective-permute-start(bf16[2,704,128]{2,1,0:T(8,128)(2,1)S(1)} %collective-permute-done.4.a0_ref.a2_ref), channel_id=1, source_target_pairs={{0,2},{1,15},{2,4},{3,1},{4,6},{5,3},{6,8},{7,5},{8,10},{9,7},{10,... | collective-permute-start | bytes 1081352 | tf_op jit(solution)/shard_map/ppermute | solution.py:140
  49.6 0.0 collective-permute-done.7.other_ref
  49.6 3.2 %shard_map.39 = s16[4,2,400,128]{3,2,1,0:T(8,128)(2,1)} custom-call(s32[2]{0:T(128)S(1)} %pad_add_fusion.at_ref, bf16[2,704,128]{2,1,0:T(8,128)(2,1)S(1)} %bitcast.6, bf16[2,704,128]{2,1,0:T(8,128)(2,1)S(1)} %collective-permute-done.3.a1_ref, bf16[2,704,128]{2,1,0:T(8,128)(2,1)S(1)} %collective-permute-done.4.a0_ref.a2_ref, ...), custom_call_target="tpu_custom_call" | custom-call | flops 553648128 | bytes 2000000 | tf_op jit(solution)/shard_map/pallas_call | solution.py:119
  52.8 7.9 %all-to-all-start.1 = ((s16[8,400,128]{2,1,0:T(8,128)(2,1)}), s16[8,400,128]{2,1,0:T(8,128)(2,1)S(1)}, u32[]{:S(2)}, u32[]{:S(2)}) async-start(s16[8,400,128]{2,1,0:T(8,128)(2,1)} %bitcast.4), calls=%async_computation.1 | async-start | bytes 1638400 | tf_op jit(solution)/shard_map/all_to_all | solution.py:130
  60.7 0.0 collective-permute-done.5.a1_ref
  60.7 4.3 %collective-permute-start.6 = (bf16[2,704,128]{2,1,0:T(8,128)(2,1)S(1)}, bf16[2,704,128]{2,1,0:T(8,128)(2,1)S(1)}, u32[]{:S(2)}, u32[]{:S(2)}) collective-permute-start(bf16[2,704,128]{2,1,0:T(8,128)(2,1)S(1)} %collective-permute-done.5.a1_ref), channel_id=1, source_target_pairs={{0,2},{2,4},{4,6},{6,8},{8,10},{10,12},{12,14},{14,0},{16,18},{18,... | collective-permute-start | bytes 1081352 | tf_op jit(solution)/shard_map/ppermute | solution.py:140
  65.0 8.0 %collective-permute-done.6.a2_ref = bf16[2,704,128]{2,1,0:T(8,128)(2,1)S(1)} collective-permute-done((bf16[2,704,128]{2,1,0:T(8,128)(2,1)S(1)}, bf16[2,704,128]{2,1,0:T(8,128)(2,1)S(1)}, u32[]{:S(2)}, u32[]{:S(2)}) %collective-permute-start.6) | collective-permute-done | bytes 360480 | tf_op jit(solution)/shard_map/ppermute | solution.py:140
  73.0 3.2 %shard_map.38 = s16[4,2,400,128]{3,2,1,0:T(8,128)(2,1)} custom-call(s32[2]{0:T(128)S(1)} %pad_add_fusion.at_ref, bf16[2,704,128]{2,1,0:T(8,128)(2,1)S(1)} %collective-permute-done.4.a0_ref.a2_ref, bf16[2,704,128]{2,1,0:T(8,128)(2,1)S(1)} %collective-permute-done.5.a1_ref, bf16[2,704,128]{2,1,0:T(8,128)(2,1)S(1)} %collective-permute-done.6.a2_ref, ...), custom_call_target="tpu_custom_call" | custom-call | flops 553648128 | bytes 2000000 | tf_op jit(solution)/shard_map/pallas_call | solution.py:119
  76.2 4.8 %all-to-all-start = ((s16[8,400,128]{2,1,0:T(8,128)(2,1)}), s16[8,400,128]{2,1,0:T(8,128)(2,1)S(1)}, u32[]{:S(2)}, u32[]{:S(2)}) async-start(s16[8,400,128]{2,1,0:T(8,128)(2,1)} %bitcast.3), calls=%async_computation | async-start | bytes 1638400 | tf_op jit(solution)/shard_map/all_to_all | solution.py:130
  81.0 0.6 shard_map.40.refs_0_
  81.6 12.9 %all-to-all-done.part_ref = s16[8,400,128]{2,1,0:T(8,128)(2,1)S(1)} async-done(((s16[8,400,128]{2,1,0:T(8,128)(2,1)}), s16[8,400,128]{2,1,0:T(8,128)(2,1)S(1)}, u32[]{:S(2)}, u32[]{:S(2)}) %all-to-all-start) | async-done | bytes 819232 | tf_op jit(solution)/shard_map/all_to_all | solution.py:130
  94.5 0.6 shard_map.41
  95.1 14.5 %all_to_all.15.part_ref = s16[4,400,128]{2,1,0:T(8,128)(2,1)S(1)} all-to-all(s16[4,400,128]{2,1,0:T(8,128)(2,1)S(1)} %shard_map.41), channel_id=1, replica_groups=mesh['x'=4,'zl'=4,'zh'=3,'y'=8,'core'=2] {'zl'}, dimensions={0} | all-to-all | bytes 819200 | tf_op jit(solution)/shard_map/all_to_all | solution.py:130
  109.6 0.2 shard_map.42
  109.8 5.1 %collective-permute-start.8 = (f32[128,384]{1,0:T(8,128)S(1)}, f32[128,384]{1,0:T(8,128)S(1)}, u32[]{:S(2)}, u32[]{:S(2)}) collective-permute-start(f32[128,384]{1,0:T(8,128)S(1)} %shard_map.42), channel_id=1, source_target_pairs={{0,14},{1,542},{2,48},{3,288},{4,338},{5,578},{6,100},{7,628},{8,1... | collective-permute-start | bytes 589832 | tf_op jit(solution)/shard_map/ppermute | solution.py:156
  114.9 15.2 %collective-permute-done.8 = f32[128,384]{1,0:T(8,128)S(1)} collective-permute-done((f32[128,384]{1,0:T(8,128)S(1)}, f32[128,384]{1,0:T(8,128)S(1)}, u32[]{:S(2)}, u32[]{:S(2)}) %collective-permute-start.8) | collective-permute-done | bytes 196640 | tf_op jit(solution)/shard_map/ppermute | solution.py:156
  130.0 0.7 multiply_add_fusion
  (7 shorter events, 0.0 us)
Async XLA Ops:
  0.0 1.0 copy-start
  5.1 25.1 %collective-permute-start.3 = (bf16[2,704,128]{2,1,0:T(8,128)(2,1)S(1)}, bf16[2,704,128]{2,1,0:T(8,128)(2,1)S(1)}, u32[]{:S(2)}, u32[]{:S(2)}) collective-permute-start(bf16[2,704,128]{2,1,0:T(8,128)(2,1)S(1)} %bitcast.5), channel_id=1, source_target_pairs={{0,2},{1,15},{2,4},{3,1},{4,6},{5,3},{6,8},{7,5},{8,10},{9,7},{10,... | collective-permute-start | bytes 1081352 | tf_op jit(solution)/shard_map/ppermute | solution.py:140
  8.5 23.8 %collective-permute-start = (bf16[704,128]{1,0:T(8,128)(2,1)S(1)}, bf16[704,128]{1,0:T(8,128)(2,1)S(1)}, u32[]{:S(2)}, u32[]{:S(2)}) collective-permute-start(bf16[704,128]{1,0:T(8,128)(2,1)S(1)} %gather_fusion), channel_id=1, source_target_pairs={{0,0},{33,1},{3,2},{18,3},{21,4},{36,5},{6,6},{39,7},{9,8},{24,9},... | collective-permute-start | bytes 540680 | tf_op jit(solution)/shard_map/ppermute | solution.py:142
  23.0 9.3 %collective-permute-start.1 = (bf16[704,128]{1,0:T(8,128)(2,1)S(1)}, bf16[704,128]{1,0:T(8,128)(2,1)S(1)}, u32[]{:S(2)}, u32[]{:S(2)}) collective-permute-start(bf16[704,128]{1,0:T(8,128)(2,1)S(1)} %gather_fusion), channel_id=1, source_target_pairs={{1,0},{34,1},{4,2},{19,3},{22,4},{37,5},{7,6},{40,7},{10,8},{25,9}... | collective-permute-start | bytes 540680 | tf_op jit(solution)/shard_map/ppermute | solution.py:142
  24.9 8.2 %collective-permute-start.2 = (bf16[704,128]{1,0:T(8,128)(2,1)S(1)}, bf16[704,128]{1,0:T(8,128)(2,1)S(1)}, u32[]{:S(2)}, u32[]{:S(2)}) collective-permute-start(bf16[704,128]{1,0:T(8,128)(2,1)S(1)} %gather_fusion), channel_id=1, source_target_pairs={{2,0},{35,1},{5,2},{20,3},{23,4},{38,5},{8,6},{41,7},{11,8},{26,9}... | collective-permute-start | bytes 540680 | tf_op jit(solution)/shard_map/ppermute | solution.py:142
  30.2 13.3 %collective-permute-start.4 = (bf16[2,704,128]{2,1,0:T(8,128)(2,1)S(1)}, bf16[2,704,128]{2,1,0:T(8,128)(2,1)S(1)}, u32[]{:S(2)}, u32[]{:S(2)}) collective-permute-start(bf16[2,704,128]{2,1,0:T(8,128)(2,1)S(1)} %collective-permute-done.3.a1_ref), channel_id=1, source_target_pairs={{0,2},{1,15},{2,4},{3,1},{4,6},{5,3},{6,8},{7,5},{8,10},{9,7},{10,... | collective-permute-start | bytes 1081352 | tf_op jit(solution)/shard_map/ppermute | solution.py:140
  43.5 6.1 %collective-permute-start.7 = (bf16[704,384]{1,0:T(8,128)(2,1)S(1)}, bf16[704,384]{1,0:T(8,128)(2,1)S(1)}, u32[]{:S(2)}, u32[]{:S(2)}) collective-permute-start(bf16[704,384]{1,0:T(8,128)(2,1)S(1)} %shard_map.37.mine_ref), channel_id=1, source_target_pairs={{0,1},{1,0},{2,3},{3,2},{4,5},{5,4},{6,7},{7,6},{8,9},{9,8},{10,11... | collective-permute-start | bytes 1622024 | tf_op jit(solution)/shard_map/ppermute | solution.py:145
  45.4 15.3 %collective-permute-start.5 = (bf16[2,704,128]{2,1,0:T(8,128)(2,1)S(1)}, bf16[2,704,128]{2,1,0:T(8,128)(2,1)S(1)}, u32[]{:S(2)}, u32[]{:S(2)}) collective-permute-start(bf16[2,704,128]{2,1,0:T(8,128)(2,1)S(1)} %collective-permute-done.4.a0_ref.a2_ref), channel_id=1, source_target_pairs={{0,2},{1,15},{2,4},{3,1},{4,6},{5,3},{6,8},{7,5},{8,10},{9,7},{10,... | collective-permute-start | bytes 1081352 | tf_op jit(solution)/shard_map/ppermute | solution.py:140
  52.8 23.4 %all-to-all-start.1 = ((s16[8,400,128]{2,1,0:T(8,128)(2,1)}), s16[8,400,128]{2,1,0:T(8,128)(2,1)S(1)}, u32[]{:S(2)}, u32[]{:S(2)}) async-start(s16[8,400,128]{2,1,0:T(8,128)(2,1)} %bitcast.4), calls=%async_computation.1 | async-start | bytes 1638400 | tf_op jit(solution)/shard_map/all_to_all | solution.py:130
  60.7 12.4 %collective-permute-start.6 = (bf16[2,704,128]{2,1,0:T(8,128)(2,1)S(1)}, bf16[2,704,128]{2,1,0:T(8,128)(2,1)S(1)}, u32[]{:S(2)}, u32[]{:S(2)}) collective-permute-start(bf16[2,704,128]{2,1,0:T(8,128)(2,1)S(1)} %collective-permute-done.5.a1_ref), channel_id=1, source_target_pairs={{0,2},{2,4},{4,6},{6,8},{8,10},{10,12},{12,14},{14,0},{16,18},{18,... | collective-permute-start | bytes 1081352 | tf_op jit(solution)/shard_map/ppermute | solution.py:140
  76.2 18.3 %all-to-all-start = ((s16[8,400,128]{2,1,0:T(8,128)(2,1)}), s16[8,400,128]{2,1,0:T(8,128)(2,1)S(1)}, u32[]{:S(2)}, u32[]{:S(2)}) async-start(s16[8,400,128]{2,1,0:T(8,128)(2,1)} %bitcast.3), calls=%async_computation | async-start | bytes 1638400 | tf_op jit(solution)/shard_map/all_to_all | solution.py:130
  109.6 20.4 %copy-start.1 = (f32[128,384]{1,0:T(8,128)S(1)}, f32[128,384]{1,0:T(8,128)}, u32[]{:S(2)}) copy-start(f32[128,384]{1,0:T(8,128)} %param.5) | copy-start | bytes 589828
  109.8 20.3 %collective-permute-start.8 = (f32[128,384]{1,0:T(8,128)S(1)}, f32[128,384]{1,0:T(8,128)S(1)}, u32[]{:S(2)}, u32[]{:S(2)}) collective-permute-start(f32[128,384]{1,0:T(8,128)S(1)} %shard_map.42), channel_id=1, source_target_pairs={{0,14},{1,542},{2,48},{3,288},{4,338},{5,578},{6,100},{7,628},{8,1... | collective-permute-start | bytes 589832 | tf_op jit(solution)/shard_map/ppermute | solution.py:156

commit v5 on v4

--- a/solution.py
+++ b/solution.py
@@ -39,9 +39,9 @@
         for zl in range(NZL):
             for y in range(NY):
                 for c in range(NC):
-                    to_y = (y + OFFSET[zl % 2][zl // 2][x // 2]) % NY
+                    to_y = (y + OFFSET[c][zl // 2][x // 2]) % NY
                     source = ((x * NZL + zl) * NY + y) * NC + c
-                    pairs.append((source, (TRIPLE[y][c] * NY + to_y) * NC + x % 2))
+                    pairs.append((source, (TRIPLE[y][zl % 2] * NY + to_y) * NC + x % 2))
     return pairs
 
 
@@ -149,7 +149,7 @@
             product_kernel, (NX, NC, CODED, LANES), jnp.int16, 2 * k * 512 * 768,
             at, *ring[2 * half : 2 * half + 3], mine, other, scalars=True,
         )
-        out = exchange(out.reshape(NX * NC, CODED, LANES), ("x", "core"))
+        out = exchange(out.reshape(NX * NC, CODED, LANES), "x")
         part = [call(sum_x_kernel, (NC * (half + 1), CODED, LANES), jnp.int16, 0, out, *part)]
     part = exchange(part[0], "zl")
     total = call(sum_zl_kernel, (ROWS, 384), jnp.float32, 0, part)

time: 131 us -> 122 us (0.931)
  the two profiles are of different devices: /device:TPU:8 before, /device:TPU:32 now
where the time goes in v5:
time: 122 us
  starting transfers between devices  53.3 us (44%)
  waiting for transfers between devices  41.1 us (34%)
  blocking collectives  14.9 us (12%)
  Pallas kernels  8.38 us (7%)
  local copies, waits for them, and re-layouts  2.25 us (2%)
  other arithmetic  1.53 us (1%)
    ppermute x3, starting transfers between devices, body(): lax.ppermute(block, ('zh', 'y', 'core'), triple_perm(i))  20.9 us
    ppermute x4, starting transfers between devices, body(): lax.ppermute(ring[-1], ('y', 'core'), ring_perm((0, 1) if step < 3 else (...  19.7 us
    ppermute x1, waiting for transfers between devices, body(): total = lax.ppermute(total, ('x', 'zl', 'y', 'core'), place_perm())  16 us
    all_to_all x1, blocking collectives, exchange(): return lax.all_to_all(part, axes, split_axis=0, concat_axis=0, tiled=True)  12.8 us
    all_to_all x2, waiting for transfers between devices, exchange(): return lax.all_to_all(part, axes, split_axis=0, concat_axis=0, tiled=True)  11.6 us
    all_to_all x2, starting transfers between devices, exchange(): return lax.all_to_all(part, axes, split_axis=0, concat_axis=0, tiled=True)  8.88 us
    pallas_call x6, Pallas kernels, call(): pl.pallas_call(kernel, in_specs=specs, out_specs=pl.BlockSpec(memory_spac...  8.38 us
    ppermute x4, waiting for transfers between devices, body(): lax.ppermute(ring[-1], ('y', 'core'), ring_perm((0, 1) if step < 3 else (...  6.97 us
  transfers between devices with their start and end apart: 11, of which 5 were waited for; matrix products, arithmetic and copies ran while one was open for 0% of the time, Pallas kernels for 6%

profile of v5, /device:TPU:32, one launch (start us, length us, event | category | flops | bytes accessed | tf_op | source)
XLA Modules:
  0.0 121.6 jit_solution(15999084725444404123)
XLA Ops:
  0.0 0.7 compare_select_fusion
  0.7 0.2 copy-done
  1.0 2.0 %gather_fusion = bf16[704,128]{1,0:T(8,128)(2,1)S(1)} fusion(bf16[1024,128]{1,0:T(8,128)(2,1)S(1)} %copy-done, s32[1024]{0:T(1024)S(1)} %pad_clamp_fusion), kind=kCustom, calls=%fused_computation | custom fusion | bytes 363264 | tf_op jit(solution)/shard_map/gather | solution.py:134
  3.0 2.1 %all-gather = bf16[1408,128]{1,0:T(8,128)(2,1)S(1)} all-gather(bf16[704,128]{1,0:T(8,128)(2,1)S(1)} %gather_fusion), channel_id=2, replica_groups=mesh['x'=4,'zl'=4,'zh'=3,'y'=8,'core'=2] {'core'}, dimensions={0}, use_global_device_ids=true | all-gather | bytes 540672 | tf_op jit(solution)/shard_map/all_gather | solution.py:138
  5.1 2.6 %collective-permute-start.3 = (bf16[2,704,128]{2,1,0:T(8,128)(2,1)S(1)}, bf16[2,704,128]{2,1,0:T(8,128)(2,1)S(1)}, u32[]{:S(2)}, u32[]{:S(2)}) collective-permute-start(bf16[2,704,128]{2,1,0:T(8,128)(2,1)S(1)} %bitcast.5), channel_id=1, source_target_pairs={{0,2},{1,15},{2,4},{3,1},{4,6},{5,3},{6,8},{7,5},{8,10},{9,7},{10,... | collective-permute-start | bytes 1081352 | tf_op jit(solution)/shard_map/ppermute | solution.py:140
  7.6 16.6 %collective-permute-start = (bf16[704,128]{1,0:T(8,128)(2,1)S(1)}, bf16[704,128]{1,0:T(8,128)(2,1)S(1)}, u32[]{:S(2)}, u32[]{:S(2)}) collective-permute-start(bf16[704,128]{1,0:T(8,128)(2,1)S(1)} %gather_fusion), channel_id=1, source_target_pairs={{0,0},{33,1},{3,2},{18,3},{21,4},{36,5},{6,6},{39,7},{9,8},{24,9},... | collective-permute-start | bytes 540680 | tf_op jit(solution)/shard_map/ppermute | solution.py:142
  24.2 1.9 %collective-permute-start.1 = (bf16[704,128]{1,0:T(8,128)(2,1)S(1)}, bf16[704,128]{1,0:T(8,128)(2,1)S(1)}, u32[]{:S(2)}, u32[]{:S(2)}) collective-permute-start(bf16[704,128]{1,0:T(8,128)(2,1)S(1)} %gather_fusion), channel_id=1, source_target_pairs={{1,0},{34,1},{4,2},{19,3},{22,4},{37,5},{7,6},{40,7},{10,8},{25,9}... | collective-permute-start | bytes 540680 | tf_op jit(solution)/shard_map/ppermute | solution.py:142
  26.1 2.5 %collective-permute-start.2 = (bf16[704,128]{1,0:T(8,128)(2,1)S(1)}, bf16[704,128]{1,0:T(8,128)(2,1)S(1)}, u32[]{:S(2)}, u32[]{:S(2)}) collective-permute-start(bf16[704,128]{1,0:T(8,128)(2,1)S(1)} %gather_fusion), channel_id=1, source_target_pairs={{2,0},{35,1},{5,2},{20,3},{23,4},{38,5},{8,6},{41,7},{11,8},{26,9}... | collective-permute-start | bytes 540680 | tf_op jit(solution)/shard_map/ppermute | solution.py:142
  28.6 0.1 pad_add_fusion.at_ref
  28.7 4.8 %collective-permute-start.4 = (bf16[2,704,128]{2,1,0:T(8,128)(2,1)S(1)}, bf16[2,704,128]{2,1,0:T(8,128)(2,1)S(1)}, u32[]{:S(2)}, u32[]{:S(2)}) collective-permute-start(bf16[2,704,128]{2,1,0:T(8,128)(2,1)S(1)} %collective-permute-done.3.a1_ref), channel_id=1, source_target_pairs={{0,2},{1,15},{2,4},{3,1},{4,6},{5,3},{6,8},{7,5},{8,10},{9,7},{10,... | collective-permute-start | bytes 1081352 | tf_op jit(solution)/shard_map/ppermute | solution.py:140
  33.5 6.6 %collective-permute-done.refs_0_ = bf16[704,128]{1,0:T(8,128)(2,1)S(1)} collective-permute-done((bf16[704,128]{1,0:T(8,128)(2,1)S(1)}, bf16[704,128]{1,0:T(8,128)(2,1)S(1)}, u32[]{:S(2)}, u32[]{:S(2)}) %collective-permute-start) | collective-permute-done | bytes 180256 | tf_op jit(solution)/shard_map/ppermute | solution.py:142
  40.1 0.0 collective-permute-done.2.refs_2_
  40.1 0.6 shard_map.37.mine_ref
  40.8 1.9 %collective-permute-start.7 = (bf16[704,384]{1,0:T(8,128)(2,1)S(1)}, bf16[704,384]{1,0:T(8,128)(2,1)S(1)}, u32[]{:S(2)}, u32[]{:S(2)}) collective-permute-start(bf16[704,384]{1,0:T(8,128)(2,1)S(1)} %shard_map.37.mine_ref), channel_id=1, source_target_pairs={{0,1},{1,0},{2,3},{3,2},{4,5},{5,4},{6,7},{7,6},{8,9},{9,8},{10,11... | collective-permute-start | bytes 1622024 | tf_op jit(solution)/shard_map/ppermute | solution.py:145
  42.7 8.7 %collective-permute-start.5 = (bf16[2,704,128]{2,1,0:T(8,128)(2,1)S(1)}, bf16[2,704,128]{2,1,0:T(8,128)(2,1)S(1)}, u32[]{:S(2)}, u32[]{:S(2)}) collective-permute-start(bf16[2,704,128]{2,1,0:T(8,128)(2,1)S(1)} %collective-permute-done.4.a0_ref.a2_ref), channel_id=1, source_target_pairs={{0,2},{1,15},{2,4},{3,1},{4,6},{5,3},{6,8},{7,5},{8,10},{9,7},{10,... | collective-permute-start | bytes 1081352 | tf_op jit(solution)/shard_map/ppermute | solution.py:140
  51.4 0.0 collective-permute-done.7.other_ref
  51.4 3.2 %shard_map.39 = s16[4,2,400,128]{3,2,1,0:T(8,128)(2,1)} custom-call(s32[2]{0:T(128)S(1)} %pad_add_fusion.at_ref, bf16[2,704,128]{2,1,0:T(8,128)(2,1)S(1)} %bitcast.6, bf16[2,704,128]{2,1,0:T(8,128)(2,1)S(1)} %collective-permute-done.3.a1_ref, bf16[2,704,128]{2,1,0:T(8,128)(2,1)S(1)} %collective-permute-done.4.a0_ref.a2_ref, ...), custom_call_target="tpu_custom_call" | custom-call | flops 553648128 | bytes 2000000 | tf_op jit(solution)/shard_map/pallas_call | solution.py:119
  54.6 4.3 %all-to-all-start.1 = ((s16[8,400,128]{2,1,0:T(8,128)(2,1)}), s16[8,400,128]{2,1,0:T(8,128)(2,1)S(1)}, u32[]{:S(2)}, u32[]{:S(2)}) async-start(s16[8,400,128]{2,1,0:T(8,128)(2,1)} %bitcast.4), calls=%async_computation.1 | async-start | bytes 1638400 | tf_op jit(solution)/shard_map/all_to_all | solution.py:130
  58.9 0.0 collective-permute-done.5.a1_ref
  58.9 3.6 %collective-permute-start.6 = (bf16[2,704,128]{2,1,0:T(8,128)(2,1)S(1)}, bf16[2,704,128]{2,1,0:T(8,128)(2,1)S(1)}, u32[]{:S(2)}, u32[]{:S(2)}) collective-permute-start(bf16[2,704,128]{2,1,0:T(8,128)(2,1)S(1)} %collective-permute-done.5.a1_ref), channel_id=1, source_target_pairs={{0,2},{2,4},{4,6},{6,8},{8,10},{10,12},{12,14},{14,0},{16,18},{18,... | collective-permute-start | bytes 1081352 | tf_op jit(solution)/shard_map/ppermute | solution.py:140
  62.5 7.0 %collective-permute-done.6.a2_ref = bf16[2,704,128]{2,1,0:T(8,128)(2,1)S(1)} collective-permute-done((bf16[2,704,128]{2,1,0:T(8,128)(2,1)S(1)}, bf16[2,704,128]{2,1,0:T(8,128)(2,1)S(1)}, u32[]{:S(2)}, u32[]{:S(2)}) %collective-permute-start.6) | collective-permute-done | bytes 360480 | tf_op jit(solution)/shard_map/ppermute | solution.py:140
  69.5 3.2 %shard_map.38 = s16[4,2,400,128]{3,2,1,0:T(8,128)(2,1)} custom-call(s32[2]{0:T(128)S(1)} %pad_add_fusion.at_ref, bf16[2,704,128]{2,1,0:T(8,128)(2,1)S(1)} %collective-permute-done.4.a0_ref.a2_ref, bf16[2,704,128]{2,1,0:T(8,128)(2,1)S(1)} %collective-permute-done.5.a1_ref, bf16[2,704,128]{2,1,0:T(8,128)(2,1)S(1)} %collective-permute-done.6.a2_ref, ...), custom_call_target="tpu_custom_call" | custom-call | flops 553648128 | bytes 2000000 | tf_op jit(solution)/shard_map/pallas_call | solution.py:119
  72.7 0.2 all-to-all-done.1.part_ref
  72.9 4.6 %all-to-all-start = ((s16[8,400,128]{2,1,0:T(8,128)(2,1)}), s16[8,400,128]{2,1,0:T(8,128)(2,1)S(1)}, u32[]{:S(2)}, u32[]{:S(2)}) async-start(s16[8,400,128]{2,1,0:T(8,128)(2,1)} %bitcast.3), calls=%async_computation | async-start | bytes 1638400 | tf_op jit(solution)/shard_map/all_to_all | solution.py:130
  77.5 0.6 shard_map.40.refs_0_
  78.1 11.4 %all-to-all-done.part_ref = s16[8,400,128]{2,1,0:T(8,128)(2,1)S(1)} async-done(((s16[8,400,128]{2,1,0:T(8,128)(2,1)}), s16[8,400,128]{2,1,0:T(8,128)(2,1)S(1)}, u32[]{:S(2)}, u32[]{:S(2)}) %all-to-all-start) | async-done | bytes 819232 | tf_op jit(solution)/shard_map/all_to_all | solution.py:130
  89.4 0.6 shard_map.41
  90.0 12.8 %all_to_all.15.part_ref = s16[4,400,128]{2,1,0:T(8,128)(2,1)S(1)} all-to-all(s16[4,400,128]{2,1,0:T(8,128)(2,1)S(1)} %shard_map.41), channel_id=1, replica_groups=mesh['x'=4,'zl'=4,'zh'=3,'y'=8,'core'=2] {'zl'}, dimensions={0} | all-to-all | bytes 819200 | tf_op jit(solution)/shard_map/all_to_all | solution.py:130
  102.8 0.2 shard_map.42
  103.0 1.9 %collective-permute-start.8 = (f32[128,384]{1,0:T(8,128)S(1)}, f32[128,384]{1,0:T(8,128)S(1)}, u32[]{:S(2)}, u32[]{:S(2)}) collective-permute-start(f32[128,384]{1,0:T(8,128)S(1)} %shard_map.42), channel_id=1, source_target_pairs={{0,14},{1,0},{2,48},{3,50},{4,338},{5,340},{6,100},{7,102},{8,150}... | collective-permute-start | bytes 589832 | tf_op jit(solution)/shard_map/ppermute | solution.py:156
  104.9 16.0 %collective-permute-done.8 = f32[128,384]{1,0:T(8,128)S(1)} collective-permute-done((f32[128,384]{1,0:T(8,128)S(1)}, f32[128,384]{1,0:T(8,128)S(1)}, u32[]{:S(2)}, u32[]{:S(2)}) %collective-permute-start.8) | collective-permute-done | bytes 196640 | tf_op jit(solution)/shard_map/ppermute | solution.py:156
  120.9 0.7 multiply_add_fusion
  (7 shorter events, 0.0 us)
Async XLA Ops:
  0.0 1.0 copy-start
  5.1 23.6 %collective-permute-start.3 = (bf16[2,704,128]{2,1,0:T(8,128)(2,1)S(1)}, bf16[2,704,128]{2,1,0:T(8,128)(2,1)S(1)}, u32[]{:S(2)}, u32[]{:S(2)}) collective-permute-start(bf16[2,704,128]{2,1,0:T(8,128)(2,1)S(1)} %bitcast.5), channel_id=1, source_target_pairs={{0,2},{1,15},{2,4},{3,1},{4,6},{5,3},{6,8},{7,5},{8,10},{9,7},{10,... | collective-permute-start | bytes 1081352 | tf_op jit(solution)/shard_map/ppermute | solution.py:140
  7.6 32.5 %collective-permute-start = (bf16[704,128]{1,0:T(8,128)(2,1)S(1)}, bf16[704,128]{1,0:T(8,128)(2,1)S(1)}, u32[]{:S(2)}, u32[]{:S(2)}) collective-permute-start(bf16[704,128]{1,0:T(8,128)(2,1)S(1)} %gather_fusion), channel_id=1, source_target_pairs={{0,0},{33,1},{3,2},{18,3},{21,4},{36,5},{6,6},{39,7},{9,8},{24,9},... | collective-permute-start | bytes 540680 | tf_op jit(solution)/shard_map/ppermute | solution.py:142
  24.2 15.9 %collective-permute-start.1 = (bf16[704,128]{1,0:T(8,128)(2,1)S(1)}, bf16[704,128]{1,0:T(8,128)(2,1)S(1)}, u32[]{:S(2)}, u32[]{:S(2)}) collective-permute-start(bf16[704,128]{1,0:T(8,128)(2,1)S(1)} %gather_fusion), channel_id=1, source_target_pairs={{1,0},{34,1},{4,2},{19,3},{22,4},{37,5},{7,6},{40,7},{10,8},{25,9}... | collective-permute-start | bytes 540680 | tf_op jit(solution)/shard_map/ppermute | solution.py:142
  26.1 14.0 %collective-permute-start.2 = (bf16[704,128]{1,0:T(8,128)(2,1)S(1)}, bf16[704,128]{1,0:T(8,128)(2,1)S(1)}, u32[]{:S(2)}, u32[]{:S(2)}) collective-permute-start(bf16[704,128]{1,0:T(8,128)(2,1)S(1)} %gather_fusion), channel_id=1, source_target_pairs={{2,0},{35,1},{5,2},{20,3},{23,4},{38,5},{8,6},{41,7},{11,8},{26,9}... | collective-permute-start | bytes 540680 | tf_op jit(solution)/shard_map/ppermute | solution.py:142
  28.7 12.1 %collective-permute-start.4 = (bf16[2,704,128]{2,1,0:T(8,128)(2,1)S(1)}, bf16[2,704,128]{2,1,0:T(8,128)(2,1)S(1)}, u32[]{:S(2)}, u32[]{:S(2)}) collective-permute-start(bf16[2,704,128]{2,1,0:T(8,128)(2,1)S(1)} %collective-permute-done.3.a1_ref), channel_id=1, source_target_pairs={{0,2},{1,15},{2,4},{3,1},{4,6},{5,3},{6,8},{7,5},{8,10},{9,7},{10,... | collective-permute-start | bytes 1081352 | tf_op jit(solution)/shard_map/ppermute | solution.py:140
  40.8 10.7 %collective-permute-start.7 = (bf16[704,384]{1,0:T(8,128)(2,1)S(1)}, bf16[704,384]{1,0:T(8,128)(2,1)S(1)}, u32[]{:S(2)}, u32[]{:S(2)}) collective-permute-start(bf16[704,384]{1,0:T(8,128)(2,1)S(1)} %shard_map.37.mine_ref), channel_id=1, source_target_pairs={{0,1},{1,0},{2,3},{3,2},{4,5},{5,4},{6,7},{7,6},{8,9},{9,8},{10,11... | collective-permute-start | bytes 1622024 | tf_op jit(solution)/shard_map/ppermute | solution.py:145
  42.7 16.3 %collective-permute-start.5 = (bf16[2,704,128]{2,1,0:T(8,128)(2,1)S(1)}, bf16[2,704,128]{2,1,0:T(8,128)(2,1)S(1)}, u32[]{:S(2)}, u32[]{:S(2)}) collective-permute-start(bf16[2,704,128]{2,1,0:T(8,128)(2,1)S(1)} %collective-permute-done.4.a0_ref.a2_ref), channel_id=1, source_target_pairs={{0,2},{1,15},{2,4},{3,1},{4,6},{5,3},{6,8},{7,5},{8,10},{9,7},{10,... | collective-permute-start | bytes 1081352 | tf_op jit(solution)/shard_map/ppermute | solution.py:140
  54.6 18.2 %all-to-all-start.1 = ((s16[8,400,128]{2,1,0:T(8,128)(2,1)}), s16[8,400,128]{2,1,0:T(8,128)(2,1)S(1)}, u32[]{:S(2)}, u32[]{:S(2)}) async-start(s16[8,400,128]{2,1,0:T(8,128)(2,1)} %bitcast.4), calls=%async_computation.1 | async-start | bytes 1638400 | tf_op jit(solution)/shard_map/all_to_all | solution.py:130
  58.9 10.5 %collective-permute-start.6 = (bf16[2,704,128]{2,1,0:T(8,128)(2,1)S(1)}, bf16[2,704,128]{2,1,0:T(8,128)(2,1)S(1)}, u32[]{:S(2)}, u32[]{:S(2)}) collective-permute-start(bf16[2,704,128]{2,1,0:T(8,128)(2,1)S(1)} %collective-permute-done.5.a1_ref), channel_id=1, source_target_pairs={{0,2},{2,4},{4,6},{6,8},{8,10},{10,12},{12,14},{14,0},{16,18},{18,... | collective-permute-start | bytes 1081352 | tf_op jit(solution)/shard_map/ppermute | solution.py:140
  72.9 16.5 %all-to-all-start = ((s16[8,400,128]{2,1,0:T(8,128)(2,1)}), s16[8,400,128]{2,1,0:T(8,128)(2,1)S(1)}, u32[]{:S(2)}, u32[]{:S(2)}) async-start(s16[8,400,128]{2,1,0:T(8,128)(2,1)} %bitcast.3), calls=%async_computation | async-start | bytes 1638400 | tf_op jit(solution)/shard_map/all_to_all | solution.py:130
  102.8 18.1 %copy-start.1 = (f32[128,384]{1,0:T(8,128)S(1)}, f32[128,384]{1,0:T(8,128)}, u32[]{:S(2)}) copy-start(f32[128,384]{1,0:T(8,128)} %param.5) | copy-start | bytes 589828
  103.0 17.9 %collective-permute-start.8 = (f32[128,384]{1,0:T(8,128)S(1)}, f32[128,384]{1,0:T(8,128)S(1)}, u32[]{:S(2)}, u32[]{:S(2)}) collective-permute-start(f32[128,384]{1,0:T(8,128)S(1)} %shard_map.42), channel_id=1, source_target_pairs={{0,14},{1,0},{2,48},{3,50},{4,338},{5,340},{6,100},{7,102},{8,150}... | collective-permute-start | bytes 589832 | tf_op jit(solution)/shard_map/ppermute | solution.py:156

commit v6 on v5

--- a/solution.py
+++ b/solution.py
@@ -1,3 +1,4 @@
+import functools
 import math
 
 import jax
@@ -33,15 +34,15 @@
     ]
 
 
-def place_perm():
+def place_perm(half, turn):
     pairs = []
     for x in range(NX):
-        for zl in range(NZL):
+        for zl, cw in ((turn, 0), ((turn + 2) % NZL, 1)):
             for y in range(NY):
                 for c in range(NC):
-                    to_y = (y + OFFSET[c][zl // 2][x // 2]) % NY
+                    to_y = (y + OFFSET[c][half][x // 2]) % NY
                     source = ((x * NZL + zl) * NY + y) * NC + c
-                    pairs.append((source, (TRIPLE[y][zl % 2] * NY + to_y) * NC + x % 2))
+                    pairs.append((source, (TRIPLE[y][cw] * NY + to_y) * NC + x % 2))
     return pairs
 
 
@@ -57,10 +58,10 @@
     put(slice(NZH * ROWS, CODED), scale)
 
 
-def decode(ref, at):
-    e = ref[at, NZH * ROWS : CODED].astype(jnp.int32).astype(jnp.float32)[0:1]
+def decode(ref, *at):
+    e = ref[(*at, slice(NZH * ROWS, CODED))].astype(jnp.int32).astype(jnp.float32)[0:1]
     scale = jnp.exp(e * (math.log(2.0) / 8)) * (1.0 / TOP)
-    root = ref[at, 0 : NZH * ROWS].astype(jnp.int32).astype(jnp.float32) * scale
+    root = ref[(*at, slice(0, NZH * ROWS))].astype(jnp.int32).astype(jnp.float32) * scale
     return root * jnp.abs(root)
 
 
@@ -91,36 +92,42 @@
                 encode(out[c * ROWS : (c + 1) * ROWS], store(out_ref, i * NC + c, cw))
 
 
-def sum_x_kernel(part_ref, *refs):
-    out_ref = refs[-1]
-    done = out_ref.shape[0] - NC
-    for c in range(done):
-        out_ref[c] = refs[0][c]
-    for c in range(NC):
-        total = decode(part_ref, c)
+def sum_x_kernel(at_ref, part_ref, first_ref, second_ref):
+    for out_ref, cw in ((first_ref, at_ref[2]), (second_ref, 1 - at_ref[2])):
+        total = decode(part_ref, cw)
         for x in range(1, NX):
-            total = total + decode(part_ref, x * NC + c)
+            total = total + decode(part_ref, x * NC + cw)
         blocks = [total[j * ROWS : (j + 1) * ROWS] for j in range(NZH)]
-        encode(jnp.concatenate(blocks, axis=1), store(out_ref, done + c))
+        encode(jnp.concatenate(blocks, axis=1), store(out_ref))
 
 
-def sum_zl_kernel(part_ref, out_ref):
-    total = decode(part_ref, 0)
-    for zl in range(1, NZL):
-        total = total + decode(part_ref, zl)
-    for j in range(NZH):
-        out_ref[:, j * LANES : (j + 1) * LANES] = total[j * ROWS : (j + 1) * ROWS]
+def sum_zl_kernel(*refs):
+    *part, out_ref = refs
+    total = decode(part[0])
+    for ref in part[1:]:
+        total = total + decode(ref)
+    out_ref[...] = total
 
 
-def call(kernel, shape, dtype, flops, *arrays, scalars=False):
+def update_kernel(scale, *refs):
+    *part, first_ref, old_ref, out_ref = refs
+    total = first_ref[...]
+    for ref in part:
+        total = total + decode(ref)
+    for j in range(NZH):
+        at = slice(j * LANES, (j + 1) * LANES)
+        out_ref[:, at] = 0.9 * old_ref[:, at] + scale * total[j * ROWS : (j + 1) * ROWS]
+
+
+def call(kernel, out, flops, *arrays, scalars=False):
     specs = [pl.BlockSpec(memory_space=pltpu.VMEM)] * (len(arrays) - scalars)
     if scalars:
         specs = [pl.BlockSpec(memory_space=pltpu.SMEM)] + specs
     return pl.pallas_call(
         kernel,
         in_specs=specs,
-        out_specs=pl.BlockSpec(memory_space=pltpu.VMEM),
-        out_shape=jax.ShapeDtypeStruct(shape, dtype),
+        out_specs=jax.tree.map(lambda _: pl.BlockSpec(memory_space=pltpu.VMEM), out),
+        out_shape=out,
         compiler_params=pltpu.CompilerParams(vmem_limit_bytes=24 << 20),
         cost_estimate=pl.CostEstimate(flops=flops, bytes_accessed=2_000_000, transcendentals=0),
     )(*arrays)
@@ -131,30 +138,37 @@
 
 
 def body(activations, sample_rows, old_factor):
+    array = jax.ShapeDtypeStruct
     block = activations.at[sample_rows].get(mode="promise_in_bounds")
     k = block.shape[0]
     scale = 0.1 / float(NX * NZL * k)
-    at = jnp.stack([lax.axis_index("zh"), lax.axis_index("core")]).astype(jnp.int32)
+    at = [lax.axis_index("zh"), lax.axis_index("core"), lax.axis_index("zl") // 2]
+    at = jnp.stack(at).astype(jnp.int32)
     ring = [lax.all_gather(block, "core", axis=0)]
     for step in range(4):
         ring.append(lax.ppermute(ring[-1], ("y", "core"), ring_perm((0, 1) if step < 3 else (0,))))
     block, _ = lax.optimization_barrier((block, ring[0]))
     mine = [lax.ppermute(block, ("zh", "y", "core"), triple_perm(i)) for i in range(NZH)]
-    mine = call(triple_kernel, (k, 384), jnp.bfloat16, 10**10, at, *mine, scalars=True)
+    mine = call(triple_kernel, array((k, 384), jnp.bfloat16), 10**10, at, *mine, scalars=True)
     mine, ring[2] = lax.optimization_barrier((mine, ring[2]))
     other = lax.ppermute(mine, "core", [(0, 1), (1, 0)])
-    part = []
+    placed = []
     for half in range(2):
         out = call(
-            product_kernel, (NX, NC, CODED, LANES), jnp.int16, 2 * k * 512 * 768,
+            product_kernel, array((NX, NC, CODED, LANES), jnp.int16), 2 * k * 512 * 768,
             at, *ring[2 * half : 2 * half + 3], mine, other, scalars=True,
         )
         out = exchange(out.reshape(NX * NC, CODED, LANES), "x")
-        part = [call(sum_x_kernel, (NC * (half + 1), CODED, LANES), jnp.int16, 0, out, *part)]
-    part = exchange(part[0], "zl")
-    total = call(sum_zl_kernel, (ROWS, 384), jnp.float32, 0, part)
-    total = lax.ppermute(total, ("x", "zl", "y", "core"), place_perm())
-    return 0.9 * old_factor + scale * total
+        out = call(sum_x_kernel, (array((CODED, LANES), jnp.int16),) * 2, 0, at, out, scalars=True)
+        placed.append([
+            lax.ppermute(out[turn // 2], ("x", "zl", "y", "core"), place_perm(half, turn))
+            for turn in range(NZL)
+        ])
+    total = call(sum_zl_kernel, array((NZH * ROWS, LANES), jnp.float32), 0, *placed[0])
+    return call(
+        functools.partial(update_kernel, scale), array((ROWS, 384), jnp.float32), 0,
+        *placed[1], total, old_factor,
+    )
 
 
 def solution(mesh):

time: 122 us -> 126 us (1.033)
  the two profiles are of different devices: /device:TPU:32 before, /device:TPU:12 now
where the time goes in v6:
time: 126 us
  starting transfers between devices  79.1 us (63%)
  waiting for transfers between devices  30.9 us (25%)
  Pallas kernels  10.4 us (8%)
  local copies, waits for them, and re-layouts  2.25 us (2%)
  blocking collectives  2.06 us (2%)
    ppermute x8, starting transfers between devices, body(): lax.ppermute(out[turn // 2], ('x', 'zl', 'y', 'core'), place_perm(half, t...  30 us
    ppermute x3, starting transfers between devices, body(): lax.ppermute(block, ('zh', 'y', 'core'), triple_perm(i))  21.5 us
    ppermute x4, waiting for transfers between devices, body(): lax.ppermute(ring[-1], ('y', 'core'), ring_perm((0, 1) if step < 3 else (...  16.9 us
    ppermute x4, starting transfers between devices, body(): lax.ppermute(ring[-1], ('y', 'core'), ring_perm((0, 1) if step < 3 else (...  16 us
    ppermute x8, waiting for transfers between devices, body(): lax.ppermute(out[turn // 2], ('x', 'zl', 'y', 'core'), place_perm(half, t...  13.2 us
    pallas_call x7, Pallas kernels, call(): pl.pallas_call(kernel, in_specs=specs, out_specs=jax.tree.map(lambda _: p...  10.4 us
    all_to_all x2, starting transfers between devices, exchange(): return lax.all_to_all(part, axes, split_axis=0, concat_axis=0, tiled=True)  9.59 us
  transfers between devices with their start and end apart: 18, of which 6 were waited for; matrix products, arithmetic and copies ran while one was open for 0% of the time, Pallas kernels for 8%

profile of v6, /device:TPU:12, one launch (start us, length us, event | category | flops | bytes accessed | tf_op | source)
XLA Modules:
  0.0 125.7 jit_solution(6010343638040163596)
XLA Ops:
  0.0 0.7 compare_select_fusion
  1.0 2.0 %gather_fusion = bf16[704,128]{1,0:T(8,128)(2,1)S(1)} fusion(bf16[1024,128]{1,0:T(8,128)(2,1)S(1)} %copy-done, s32[1024]{0:T(1024)S(1)} %pad_clamp_fusion), kind=kCustom, calls=%fused_computation | custom fusion | bytes 363264 | tf_op jit(solution)/shard_map/gather | solution.py:142
  3.0 2.1 %all-gather = bf16[1408,128]{1,0:T(8,128)(2,1)S(1)} all-gather(bf16[704,128]{1,0:T(8,128)(2,1)S(1)} %gather_fusion), channel_id=2, replica_groups=mesh['x'=4,'zl'=4,'zh'=3,'y'=8,'core'=2] {'core'}, dimensions={0}, use_global_device_ids=true | all-gather | bytes 540672 | tf_op jit(solution)/shard_map/all_gather | solution.py:147
  5.1 3.5 %collective-permute-start.3 = (bf16[2,704,128]{2,1,0:T(8,128)(2,1)S(1)}, bf16[2,704,128]{2,1,0:T(8,128)(2,1)S(1)}, u32[]{:S(2)}, u32[]{:S(2)}) collective-permute-start(bf16[2,704,128]{2,1,0:T(8,128)(2,1)S(1)} %bitcast.6), channel_id=1, source_target_pairs={{0,2},{1,15},{2,4},{3,1},{4,6},{5,3},{6,8},{7,5},{8,10},{9,7},{10,... | collective-permute-start | bytes 1081352 | tf_op jit(solution)/shard_map/ppermute | solution.py:149
  8.5 14.4 %collective-permute-start = (bf16[704,128]{1,0:T(8,128)(2,1)S(1)}, bf16[704,128]{1,0:T(8,128)(2,1)S(1)}, u32[]{:S(2)}, u32[]{:S(2)}) collective-permute-start(bf16[704,128]{1,0:T(8,128)(2,1)S(1)} %gather_fusion), channel_id=1, source_target_pairs={{0,0},{33,1},{3,2},{18,3},{21,4},{36,5},{6,6},{39,7},{9,8},{24,9},... | collective-permute-start | bytes 540680 | tf_op jit(solution)/shard_map/ppermute | solution.py:151
  23.0 1.9 %collective-permute-start.1 = (bf16[704,128]{1,0:T(8,128)(2,1)S(1)}, bf16[704,128]{1,0:T(8,128)(2,1)S(1)}, u32[]{:S(2)}, u32[]{:S(2)}) collective-permute-start(bf16[704,128]{1,0:T(8,128)(2,1)S(1)} %gather_fusion), channel_id=1, source_target_pairs={{1,0},{34,1},{4,2},{19,3},{22,4},{37,5},{7,6},{40,7},{10,8},{25,9}... | collective-permute-start | bytes 540680 | tf_op jit(solution)/shard_map/ppermute | solution.py:151
  24.9 5.2 %collective-permute-start.2 = (bf16[704,128]{1,0:T(8,128)(2,1)S(1)}, bf16[704,128]{1,0:T(8,128)(2,1)S(1)}, u32[]{:S(2)}, u32[]{:S(2)}) collective-permute-start(bf16[704,128]{1,0:T(8,128)(2,1)S(1)} %gather_fusion), channel_id=1, source_target_pairs={{2,0},{35,1},{5,2},{20,3},{23,4},{38,5},{8,6},{41,7},{11,8},{26,9}... | collective-permute-start | bytes 540680 | tf_op jit(solution)/shard_map/ppermute | solution.py:151
  30.2 2.1 %collective-permute-start.4 = (bf16[2,704,128]{2,1,0:T(8,128)(2,1)S(1)}, bf16[2,704,128]{2,1,0:T(8,128)(2,1)S(1)}, u32[]{:S(2)}, u32[]{:S(2)}) collective-permute-start(bf16[2,704,128]{2,1,0:T(8,128)(2,1)S(1)} %collective-permute-done.3.a1_ref), channel_id=1, source_target_pairs={{0,2},{1,15},{2,4},{3,1},{4,6},{5,3},{6,8},{7,5},{8,10},{9,7},{10,... | collective-permute-start | bytes 1081352 | tf_op jit(solution)/shard_map/ppermute | solution.py:149
  32.3 0.8 collective-permute-done.2.refs_2_
  33.7 9.8 %collective-permute-done.4.a0_ref.a2_ref = bf16[2,704,128]{2,1,0:T(8,128)(2,1)S(1)} collective-permute-done((bf16[2,704,128]{2,1,0:T(8,128)(2,1)S(1)}, bf16[2,704,128]{2,1,0:T(8,128)(2,1)S(1)}, u32[]{:S(2)}, u32[]{:S(2)}) %collective-permute-start.4) | collective-permute-done | bytes 360480 | tf_op jit(solution)/shard_map/ppermute | solution.py:149
  43.5 1.9 %collective-permute-start.7 = (bf16[704,384]{1,0:T(8,128)(2,1)S(1)}, bf16[704,384]{1,0:T(8,128)(2,1)S(1)}, u32[]{:S(2)}, u32[]{:S(2)}) collective-permute-start(bf16[704,384]{1,0:T(8,128)(2,1)S(1)} %shard_map.37.mine_ref), channel_id=1, source_target_pairs={{0,1},{1,0},{2,3},{3,2},{4,5},{5,4},{6,7},{7,6},{8,9},{9,8},{10,11... | collective-permute-start | bytes 1622024 | tf_op jit(solution)/shard_map/ppermute | solution.py:154
  45.4 4.2 %collective-permute-start.5 = (bf16[2,704,128]{2,1,0:T(8,128)(2,1)S(1)}, bf16[2,704,128]{2,1,0:T(8,128)(2,1)S(1)}, u32[]{:S(2)}, u32[]{:S(2)}) collective-permute-start(bf16[2,704,128]{2,1,0:T(8,128)(2,1)S(1)} %collective-permute-done.4.a0_ref.a2_ref), channel_id=1, source_target_pairs={{0,2},{1,15},{2,4},{3,1},{4,6},{5,3},{6,8},{7,5},{8,10},{9,7},{10,... | collective-permute-start | bytes 1081352 | tf_op jit(solution)/shard_map/ppermute | solution.py:149
  49.6 3.2 %shard_map.40 = s16[4,2,400,128]{3,2,1,0:T(8,128)(2,1)} custom-call(s32[3]{0:T(128)S(1)} %pad_add_fusion.at_ref, bf16[2,704,128]{2,1,0:T(8,128)(2,1)S(1)} %bitcast.7, bf16[2,704,128]{2,1,0:T(8,128)(2,1)S(1)} %collective-permute-done.3.a1_ref, bf16[2,704,128]{2,1,0:T(8,128)(2,1)S(1)} %collective-permute-done.4.a0_ref.a2_ref, ...), custom_call_target="tpu_custom_call" | custom-call | flops 553648128 | bytes 2000000 | tf_op jit(solution)/shard_map/pallas_call | solution.py:126
  52.8 4.8 %all-to-all-start.1 = ((s16[8,400,128]{2,1,0:T(8,128)(2,1)}), s16[8,400,128]{2,1,0:T(8,128)(2,1)S(1)}, u32[]{:S(2)}, u32[]{:S(2)}) async-start(s16[8,400,128]{2,1,0:T(8,128)(2,1)} %bitcast.5), calls=%async_computation.1 | async-start | bytes 1638400 | tf_op jit(solution)/shard_map/all_to_all | solution.py:137
  57.6 1.6 %collective-permute-done.5.a1_ref = bf16[2,704,128]{2,1,0:T(8,128)(2,1)S(1)} collective-permute-done((bf16[2,704,128]{2,1,0:T(8,128)(2,1)S(1)}, bf16[2,704,128]{2,1,0:T(8,128)(2,1)S(1)}, u32[]{:S(2)}, u32[]{:S(2)}) %collective-permute-start.5) | collective-permute-done | bytes 360480 | tf_op jit(solution)/shard_map/ppermute | solution.py:149
  59.2 6.3 %collective-permute-start.6 = (bf16[2,704,128]{2,1,0:T(8,128)(2,1)S(1)}, bf16[2,704,128]{2,1,0:T(8,128)(2,1)S(1)}, u32[]{:S(2)}, u32[]{:S(2)}) collective-permute-start(bf16[2,704,128]{2,1,0:T(8,128)(2,1)S(1)} %collective-permute-done.5.a1_ref), channel_id=1, source_target_pairs={{0,2},{2,4},{4,6},{6,8},{8,10},{10,12},{12,14},{14,0},{16,18},{18,... | collective-permute-start | bytes 1081352 | tf_op jit(solution)/shard_map/ppermute | solution.py:149
  65.5 5.6 %collective-permute-done.6.a2_ref = bf16[2,704,128]{2,1,0:T(8,128)(2,1)S(1)} collective-permute-done((bf16[2,704,128]{2,1,0:T(8,128)(2,1)S(1)}, bf16[2,704,128]{2,1,0:T(8,128)(2,1)S(1)}, u32[]{:S(2)}, u32[]{:S(2)}) %collective-permute-start.6) | collective-permute-done | bytes 360480 | tf_op jit(solution)/shard_map/ppermute | solution.py:149
  71.1 3.2 %shard_map.38 = s16[4,2,400,128]{3,2,1,0:T(8,128)(2,1)} custom-call(s32[3]{0:T(128)S(1)} %pad_add_fusion.at_ref, bf16[2,704,128]{2,1,0:T(8,128)(2,1)S(1)} %collective-permute-done.4.a0_ref.a2_ref, bf16[2,704,128]{2,1,0:T(8,128)(2,1)S(1)} %collective-permute-done.5.a1_ref, bf16[2,704,128]{2,1,0:T(8,128)(2,1)S(1)} %collective-permute-done.6.a2_ref, ...), custom_call_target="tpu_custom_call" | custom-call | flops 553648128 | bytes 2000000 | tf_op jit(solution)/shard_map/pallas_call | solution.py:126
  74.2 4.8 %all-to-all-start = ((s16[8,400,128]{2,1,0:T(8,128)(2,1)}), s16[8,400,128]{2,1,0:T(8,128)(2,1)S(1)}, u32[]{:S(2)}, u32[]{:S(2)}) async-start(s16[8,400,128]{2,1,0:T(8,128)(2,1)} %bitcast.4), calls=%async_computation | async-start | bytes 1638400 | tf_op jit(solution)/shard_map/all_to_all | solution.py:137
  79.0 1.1 shard_map.41
  80.2 5.4 %collective-permute-start.12 = (s16[400,128]{1,0:T(8,128)(2,1)S(1)}, s16[400,128]{1,0:T(8,128)(2,1)S(1)}, u32[]{:S(2)}, u32[]{:S(2)}) collective-permute-start(s16[400,128]{1,0:T(8,128)(2,1)S(1)} %get-tuple-element.17), channel_id=1, source_target_pairs={{0,14},{1,0},{2,48},{3,50},{4,338},{5,340},{6,100},{7,102},{8,150}... | collective-permute-start | bytes 307208 | tf_op jit(solution)/shard_map/ppermute | solution.py:164
  85.6 0.7 collective-permute-start.13
  86.2 3.1 %collective-permute-start.14 = (s16[400,128]{1,0:T(8,128)(2,1)S(1)}, s16[400,128]{1,0:T(8,128)(2,1)S(1)}, u32[]{:S(2)}, u32[]{:S(2)}) collective-permute-start(s16[400,128]{1,0:T(8,128)(2,1)S(1)} %get-tuple-element.18), channel_id=1, source_target_pairs={{96,14},{97,0},{98,48},{99,50},{100,338},{101,340},{102,100},{103,... | collective-permute-start | bytes 307208 | tf_op jit(solution)/shard_map/ppermute | solution.py:164
  89.3 0.7 collective-permute-start.15
  90.0 1.1 shard_map.39
  91.1 4.7 %collective-permute-start.10 = (s16[400,128]{1,0:T(8,128)(2,1)S(1)}, s16[400,128]{1,0:T(8,128)(2,1)S(1)}, u32[]{:S(2)}, u32[]{:S(2)}) collective-permute-start(s16[400,128]{1,0:T(8,128)(2,1)S(1)} %get-tuple-element.16), channel_id=1, source_target_pairs={{96,10},{97,4},{98,60},{99,54},{100,350},{101,344},{102,96},{103,1... | collective-permute-start | bytes 307208 | tf_op jit(solution)/shard_map/ppermute | solution.py:164
  95.8 1.3 %collective-permute-start.11 = (s16[400,128]{1,0:T(8,128)(2,1)S(1)}, s16[400,128]{1,0:T(8,128)(2,1)S(1)}, u32[]{:S(2)}, u32[]{:S(2)}) collective-permute-start(s16[400,128]{1,0:T(8,128)(2,1)S(1)} %get-tuple-element.16), channel_id=1, source_target_pairs={{144,10},{145,4},{146,60},{147,54},{148,350},{149,344},{150,96},{1... | collective-permute-start | bytes 307208 | tf_op jit(solution)/shard_map/ppermute | solution.py:164
  97.1 13.0 %collective-permute-start.8 = (s16[400,128]{1,0:T(8,128)(2,1)S(1)}, s16[400,128]{1,0:T(8,128)(2,1)S(1)}, u32[]{:S(2)}, u32[]{:S(2)}) collective-permute-start(s16[400,128]{1,0:T(8,128)(2,1)S(1)} %get-tuple-element.15), channel_id=1, source_target_pairs={{0,10},{1,4},{2,60},{3,54},{4,350},{5,344},{6,96},{7,106},{8,146},... | collective-permute-start | bytes 307208 | tf_op jit(solution)/shard_map/ppermute | solution.py:164
  110.2 1.3 %collective-permute-start.9 = (s16[400,128]{1,0:T(8,128)(2,1)S(1)}, s16[400,128]{1,0:T(8,128)(2,1)S(1)}, u32[]{:S(2)}, u32[]{:S(2)}) collective-permute-start(s16[400,128]{1,0:T(8,128)(2,1)S(1)} %get-tuple-element.15), channel_id=1, source_target_pairs={{48,10},{49,4},{50,60},{51,54},{52,350},{53,344},{54,96},{55,106},... | collective-permute-start | bytes 307208 | tf_op jit(solution)/shard_map/ppermute | solution.py:164
  111.7 0.8 collective-permute-done.8.refs_0_
  112.5 12.4 %collective-permute-done.9.refs_1_ = s16[400,128]{1,0:T(8,128)(2,1)S(1)} collective-permute-done((s16[400,128]{1,0:T(8,128)(2,1)S(1)}, s16[400,128]{1,0:T(8,128)(2,1)S(1)}, u32[]{:S(2)}, u32[]{:S(2)}) %collective-permute-start.9) | collective-permute-done | bytes 102432 | tf_op jit(solution)/shard_map/ppermute | solution.py:164
  124.8 0.9 shard_map.43
  (20 shorter events, 1.1 us)
Async XLA Ops:
  0.0 1.0 copy-start
  5.1 25.1 %collective-permute-start.3 = (bf16[2,704,128]{2,1,0:T(8,128)(2,1)S(1)}, bf16[2,704,128]{2,1,0:T(8,128)(2,1)S(1)}, u32[]{:S(2)}, u32[]{:S(2)}) collective-permute-start(bf16[2,704,128]{2,1,0:T(8,128)(2,1)S(1)} %bitcast.6), channel_id=1, source_target_pairs={{0,2},{1,15},{2,4},{3,1},{4,6},{5,3},{6,8},{7,5},{8,10},{9,7},{10,... | collective-permute-start | bytes 1081352 | tf_op jit(solution)/shard_map/ppermute | solution.py:149
  8.5 23.8 %collective-permute-start = (bf16[704,128]{1,0:T(8,128)(2,1)S(1)}, bf16[704,128]{1,0:T(8,128)(2,1)S(1)}, u32[]{:S(2)}, u32[]{:S(2)}) collective-permute-start(bf16[704,128]{1,0:T(8,128)(2,1)S(1)} %gather_fusion), channel_id=1, source_target_pairs={{0,0},{33,1},{3,2},{18,3},{21,4},{36,5},{6,6},{39,7},{9,8},{24,9},... | collective-permute-start | bytes 540680 | tf_op jit(solution)/shard_map/ppermute | solution.py:151
  23.0 9.3 %collective-permute-start.1 = (bf16[704,128]{1,0:T(8,128)(2,1)S(1)}, bf16[704,128]{1,0:T(8,128)(2,1)S(1)}, u32[]{:S(2)}, u32[]{:S(2)}) collective-permute-start(bf16[704,128]{1,0:T(8,128)(2,1)S(1)} %gather_fusion), channel_id=1, source_target_pairs={{1,0},{34,1},{4,2},{19,3},{22,4},{37,5},{7,6},{40,7},{10,8},{25,9}... | collective-permute-start | bytes 540680 | tf_op jit(solution)/shard_map/ppermute | solution.py:151
  24.9 8.2 %collective-permute-start.2 = (bf16[704,128]{1,0:T(8,128)(2,1)S(1)}, bf16[704,128]{1,0:T(8,128)(2,1)S(1)}, u32[]{:S(2)}, u32[]{:S(2)}) collective-permute-start(bf16[704,128]{1,0:T(8,128)(2,1)S(1)} %gather_fusion), channel_id=1, source_target_pairs={{2,0},{35,1},{5,2},{20,3},{23,4},{38,5},{8,6},{41,7},{11,8},{26,9}... | collective-permute-start | bytes 540680 | tf_op jit(solution)/shard_map/ppermute | solution.py:151
  30.2 13.3 %collective-permute-start.4 = (bf16[2,704,128]{2,1,0:T(8,128)(2,1)S(1)}, bf16[2,704,128]{2,1,0:T(8,128)(2,1)S(1)}, u32[]{:S(2)}, u32[]{:S(2)}) collective-permute-start(bf16[2,704,128]{2,1,0:T(8,128)(2,1)S(1)} %collective-permute-done.3.a1_ref), channel_id=1, source_target_pairs={{0,2},{1,15},{2,4},{3,1},{4,6},{5,3},{6,8},{7,5},{8,10},{9,7},{10,... | collective-permute-start | bytes 1081352 | tf_op jit(solution)/shard_map/ppermute | solution.py:149
  43.5 6.1 %collective-permute-start.7 = (bf16[704,384]{1,0:T(8,128)(2,1)S(1)}, bf16[704,384]{1,0:T(8,128)(2,1)S(1)}, u32[]{:S(2)}, u32[]{:S(2)}) collective-permute-start(bf16[704,384]{1,0:T(8,128)(2,1)S(1)} %shard_map.37.mine_ref), channel_id=1, source_target_pairs={{0,1},{1,0},{2,3},{3,2},{4,5},{5,4},{6,7},{7,6},{8,9},{9,8},{10,11... | collective-permute-start | bytes 1622024 | tf_op jit(solution)/shard_map/ppermute | solution.py:154
  45.4 13.8 %collective-permute-start.5 = (bf16[2,704,128]{2,1,0:T(8,128)(2,1)S(1)}, bf16[2,704,128]{2,1,0:T(8,128)(2,1)S(1)}, u32[]{:S(2)}, u32[]{:S(2)}) collective-permute-start(bf16[2,704,128]{2,1,0:T(8,128)(2,1)S(1)} %collective-permute-done.4.a0_ref.a2_ref), channel_id=1, source_target_pairs={{0,2},{1,15},{2,4},{3,1},{4,6},{5,3},{6,8},{7,5},{8,10},{9,7},{10,... | collective-permute-start | bytes 1081352 | tf_op jit(solution)/shard_map/ppermute | solution.py:149
  52.8 21.4 %all-to-all-start.1 = ((s16[8,400,128]{2,1,0:T(8,128)(2,1)}), s16[8,400,128]{2,1,0:T(8,128)(2,1)S(1)}, u32[]{:S(2)}, u32[]{:S(2)}) async-start(s16[8,400,128]{2,1,0:T(8,128)(2,1)} %bitcast.5), calls=%async_computation.1 | async-start | bytes 1638400 | tf_op jit(solution)/shard_map/all_to_all | solution.py:137
  59.2 11.9 %collective-permute-start.6 = (bf16[2,704,128]{2,1,0:T(8,128)(2,1)S(1)}, bf16[2,704,128]{2,1,0:T(8,128)(2,1)S(1)}, u32[]{:S(2)}, u32[]{:S(2)}) collective-permute-start(bf16[2,704,128]{2,1,0:T(8,128)(2,1)S(1)} %collective-permute-done.5.a1_ref), channel_id=1, source_target_pairs={{0,2},{2,4},{4,6},{6,8},{8,10},{10,12},{12,14},{14,0},{16,18},{18,... | collective-permute-start | bytes 1081352 | tf_op jit(solution)/shard_map/ppermute | solution.py:149
  74.2 15.7 %all-to-all-start = ((s16[8,400,128]{2,1,0:T(8,128)(2,1)}), s16[8,400,128]{2,1,0:T(8,128)(2,1)S(1)}, u32[]{:S(2)}, u32[]{:S(2)}) async-start(s16[8,400,128]{2,1,0:T(8,128)(2,1)} %bitcast.4), calls=%async_computation | async-start | bytes 1638400 | tf_op jit(solution)/shard_map/all_to_all | solution.py:137
  80.2 15.6 %collective-permute-start.12 = (s16[400,128]{1,0:T(8,128)(2,1)S(1)}, s16[400,128]{1,0:T(8,128)(2,1)S(1)}, u32[]{:S(2)}, u32[]{:S(2)}) collective-permute-start(s16[400,128]{1,0:T(8,128)(2,1)S(1)} %get-tuple-element.17), channel_id=1, source_target_pairs={{0,14},{1,0},{2,48},{3,50},{4,338},{5,340},{6,100},{7,102},{8,150}... | collective-permute-start | bytes 307208 | tf_op jit(solution)/shard_map/ppermute | solution.py:164
  85.6 11.6 %collective-permute-start.13 = (s16[400,128]{1,0:T(8,128)(2,1)S(1)}, s16[400,128]{1,0:T(8,128)(2,1)S(1)}, u32[]{:S(2)}, u32[]{:S(2)}) collective-permute-start(s16[400,128]{1,0:T(8,128)(2,1)S(1)} %get-tuple-element.17), channel_id=1, source_target_pairs={{48,14},{49,0},{50,48},{51,50},{52,338},{53,340},{54,100},{55,102}... | collective-permute-start | bytes 307208 | tf_op jit(solution)/shard_map/ppermute | solution.py:164
  86.2 23.9 %collective-permute-start.14 = (s16[400,128]{1,0:T(8,128)(2,1)S(1)}, s16[400,128]{1,0:T(8,128)(2,1)S(1)}, u32[]{:S(2)}, u32[]{:S(2)}) collective-permute-start(s16[400,128]{1,0:T(8,128)(2,1)S(1)} %get-tuple-element.18), channel_id=1, source_target_pairs={{96,14},{97,0},{98,48},{99,50},{100,338},{101,340},{102,100},{103,... | collective-permute-start | bytes 307208 | tf_op jit(solution)/shard_map/ppermute | solution.py:164
  89.3 22.2 %collective-permute-start.15 = (s16[400,128]{1,0:T(8,128)(2,1)S(1)}, s16[400,128]{1,0:T(8,128)(2,1)S(1)}, u32[]{:S(2)}, u32[]{:S(2)}) collective-permute-start(s16[400,128]{1,0:T(8,128)(2,1)S(1)} %get-tuple-element.18), channel_id=1, source_target_pairs={{144,14},{145,0},{146,48},{147,50},{148,338},{149,340},{150,100},{... | collective-permute-start | bytes 307208 | tf_op jit(solution)/shard_map/ppermute | solution.py:164
  91.1 20.5 %collective-permute-start.10 = (s16[400,128]{1,0:T(8,128)(2,1)S(1)}, s16[400,128]{1,0:T(8,128)(2,1)S(1)}, u32[]{:S(2)}, u32[]{:S(2)}) collective-permute-start(s16[400,128]{1,0:T(8,128)(2,1)S(1)} %get-tuple-element.16), channel_id=1, source_target_pairs={{96,10},{97,4},{98,60},{99,54},{100,350},{101,344},{102,96},{103,1... | collective-permute-start | bytes 307208 | tf_op jit(solution)/shard_map/ppermute | solution.py:164
  95.8 15.8 %collective-permute-start.11 = (s16[400,128]{1,0:T(8,128)(2,1)S(1)}, s16[400,128]{1,0:T(8,128)(2,1)S(1)}, u32[]{:S(2)}, u32[]{:S(2)}) collective-permute-start(s16[400,128]{1,0:T(8,128)(2,1)S(1)} %get-tuple-element.16), channel_id=1, source_target_pairs={{144,10},{145,4},{146,60},{147,54},{148,350},{149,344},{150,96},{1... | collective-permute-start | bytes 307208 | tf_op jit(solution)/shard_map/ppermute | solution.py:164
  97.1 27.7 %copy-start.1 = (f32[128,384]{1,0:T(8,128)S(1)}, f32[128,384]{1,0:T(8,128)}, u32[]{:S(2)}) copy-start(f32[128,384]{1,0:T(8,128)} %refs_5_.1) | copy-start | bytes 589828
  97.1 15.3 %collective-permute-start.8 = (s16[400,128]{1,0:T(8,128)(2,1)S(1)}, s16[400,128]{1,0:T(8,128)(2,1)S(1)}, u32[]{:S(2)}, u32[]{:S(2)}) collective-permute-start(s16[400,128]{1,0:T(8,128)(2,1)S(1)} %get-tuple-element.15), channel_id=1, source_target_pairs={{0,10},{1,4},{2,60},{3,54},{4,350},{5,344},{6,96},{7,106},{8,146},... | collective-permute-start | bytes 307208 | tf_op jit(solution)/shard_map/ppermute | solution.py:164
  110.2 14.7 %collective-permute-start.9 = (s16[400,128]{1,0:T(8,128)(2,1)S(1)}, s16[400,128]{1,0:T(8,128)(2,1)S(1)}, u32[]{:S(2)}, u32[]{:S(2)}) collective-permute-start(s16[400,128]{1,0:T(8,128)(2,1)S(1)} %get-tuple-element.15), channel_id=1, source_target_pairs={{48,10},{49,4},{50,60},{51,54},{52,350},{53,344},{54,96},{55,106},... | collective-permute-start | bytes 307208 | tf_op jit(solution)/shard_map/ppermute | solution.py:164

commit v7 on v5

--- a/solution.py
+++ b/solution.py
@@ -1,3 +1,4 @@
+import functools
 import math
 
 import jax
@@ -14,7 +15,8 @@
 OFFSET = (((-1, -2), (-3, -4)), ((0, 1), (2, 3)))
 LANES = 128
 ROWS = 128
-CODED = NZH * ROWS + 16
+TILE = 16
+CODED = NZH * ROWS + TILE
 TOP = 32767.0
 
 
@@ -45,23 +47,40 @@
     return pairs
 
 
-def encode(value, put):
-    most = jnp.max(jnp.abs(value), axis=(0, 1), keepdims=True)
-    e = jnp.ceil(4.0 / math.log(2.0) * jnp.log(jnp.maximum(most, 2.0**-120)))
-    root = jnp.sqrt(jnp.abs(value)) * (TOP * jnp.exp(e * (-math.log(2.0) / 8)))
-    q = jnp.where(value < 0, -root, root)
-    q = jnp.round(q).astype(jnp.int32).astype(jnp.int16)
-    for j in range(NZH):
-        put(slice(j * ROWS, (j + 1) * ROWS), q[:, j * LANES : (j + 1) * LANES])
-    scale = jnp.broadcast_to(e, (16, LANES)).astype(jnp.int32).astype(jnp.int16)
-    put(slice(NZH * ROWS, CODED), scale)
+def encode(blocks, put):
+    row = lax.broadcasted_iota(jnp.int32, (TILE, LANES), 0)
+    scales = jnp.zeros((TILE, LANES), jnp.float32)
+    for j, value in enumerate(blocks):
+        size = jnp.abs(value)
+        most = jnp.maximum(jnp.max(size, axis=0, keepdims=True), 2.0**-120)
+        e = jnp.ceil(4.0 / math.log(2.0) * jnp.log(most))
+        root = jnp.sqrt(size) * (TOP * jnp.exp(e * (-math.log(2.0) / 8)))
+        q = jnp.round(jnp.where(value < 0, -root, root))
+        put(slice(j * ROWS, (j + 1) * ROWS), q.astype(jnp.int32).astype(jnp.int16))
+        scales = jnp.where(row == j, e, scales)
+    put(slice(NZH * ROWS, CODED), scales.astype(jnp.int32).astype(jnp.int16))
 
 
-def decode(ref, at):
-    e = ref[at, NZH * ROWS : CODED].astype(jnp.int32).astype(jnp.float32)[0:1]
-    scale = jnp.exp(e * (math.log(2.0) / 8)) * (1.0 / TOP)
-    root = ref[at, 0 : NZH * ROWS].astype(jnp.int32).astype(jnp.float32) * scale
-    return root * jnp.abs(root)
+def decode(ref, *at):
+    e = ref[(*at, slice(NZH * ROWS, CODED))].astype(jnp.int32).astype(jnp.float32)
+    scales = jnp.exp(e * (math.log(2.0) / 8)) * (1.0 / TOP)
+    blocks = []
+    for j in range(NZH):
+        root = ref[(*at, slice(j * ROWS, (j + 1) * ROWS))].astype(jnp.int32).astype(jnp.float32)
+        root = root * scales[j : j + 1]
+        blocks.append(root * jnp.abs(root))
+    return blocks
+
+
+def decoded_sum(ref, at):
+    total = decode(ref, at[0])
+    for i in at[1:]:
+        total = [a + b for a, b in zip(total, decode(ref, i))]
+    return total
+
+
+def lane_blocks(value):
+    return [value[:, j * LANES : (j + 1) * LANES] for j in range(NZH)]
 
 
 def store(ref, *at):
@@ -88,7 +107,7 @@
                 rows, columns_ref[...], (((0,), (0,)), ((), ())), preferred_element_type=jnp.float32
             )
             for c in range(NC):
-                encode(out[c * ROWS : (c + 1) * ROWS], store(out_ref, i * NC + c, cw))
+                encode(lane_blocks(out[c * ROWS : (c + 1) * ROWS]), store(out_ref, i * NC + c, cw))
 
 
 def sum_x_kernel(part_ref, *refs):
@@ -97,19 +116,18 @@
     for c in range(done):
         out_ref[c] = refs[0][c]
     for c in range(NC):
-        total = decode(part_ref, c)
-        for x in range(1, NX):
-            total = total + decode(part_ref, x * NC + c)
-        blocks = [total[j * ROWS : (j + 1) * ROWS] for j in range(NZH)]
-        encode(jnp.concatenate(blocks, axis=1), store(out_ref, done + c))
+        total = decoded_sum(part_ref, [x * NC + c for x in range(NX)])
+        encode(total, store(out_ref, done + c))
 
 
 def sum_zl_kernel(part_ref, out_ref):
-    total = decode(part_ref, 0)
-    for zl in range(1, NZL):
-        total = total + decode(part_ref, zl)
-    for j in range(NZH):
-        out_ref[:, j * LANES : (j + 1) * LANES] = total[j * ROWS : (j + 1) * ROWS]
+    encode(decoded_sum(part_ref, range(NZL)), store(out_ref))
+
+
+def update_kernel(scale, total_ref, old_ref, out_ref):
+    for j, total in enumerate(decode(total_ref)):
+        at = slice(j * LANES, (j + 1) * LANES)
+        out_ref[:, at] = 0.9 * old_ref[:, at] + scale * total
 
 
 def call(kernel, shape, dtype, flops, *arrays, scalars=False):
@@ -152,9 +170,11 @@
         out = exchange(out.reshape(NX * NC, CODED, LANES), "x")
         part = [call(sum_x_kernel, (NC * (half + 1), CODED, LANES), jnp.int16, 0, out, *part)]
     part = exchange(part[0], "zl")
-    total = call(sum_zl_kernel, (ROWS, 384), jnp.float32, 0, part)
+    total = call(sum_zl_kernel, (CODED, LANES), jnp.int16, 0, part)
     total = lax.ppermute(total, ("x", "zl", "y", "core"), place_perm())
-    return 0.9 * old_factor + scale * total
+    return call(
+        functools.partial(update_kernel, scale), old_factor.shape, jnp.float32, 0, total, old_factor
+    )
 
 
 def solution(mesh):

time: 122 us -> 119 us (0.975)
  waiting for transfers between devices: 41.1 us -> 38.3 us
    ppermute x1, waiting for transfers between devices: 16 us -> 12.7 us  [body(): total = lax.ppermute(total, ('x', 'zl', 'y', 'core'), place_perm())]
    pallas_call x6 -> x7, Pallas kernels: 8.38 us -> 8.86 us  [call(): pl.pallas_call(kernel, in_specs=specs, out_specs=pl.BlockSpec(memory_spac...]
where the time goes in v7:
time: 119 us
  starting transfers between devices  53.2 us (45%)
  waiting for transfers between devices  38.3 us (32%)
  blocking collectives  15 us (13%)
  Pallas kernels  8.86 us (7%)
  local copies, waits for them, and re-layouts  2.25 us (2%)
    ppermute x3, starting transfers between devices, body(): lax.ppermute(block, ('zh', 'y', 'core'), triple_perm(i))  20.9 us
    ppermute x4, starting transfers between devices, body(): lax.ppermute(ring[-1], ('y', 'core'), ring_perm((0, 1) if step < 3 else (...  19.7 us
    all_to_all x1, blocking collectives, exchange(): return lax.all_to_all(part, axes, split_axis=0, concat_axis=0, tiled=True)  13 us
    ppermute x1, waiting for transfers between devices, body(): total = lax.ppermute(total, ('x', 'zl', 'y', 'core'), place_perm())  12.7 us
    all_to_all x2, waiting for transfers between devices, exchange(): return lax.all_to_all(part, axes, split_axis=0, concat_axis=0, tiled=True)  12 us
    pallas_call x7, Pallas kernels, call(): pl.pallas_call(kernel, in_specs=specs, out_specs=pl.BlockSpec(memory_spac...  8.86 us
    all_to_all x2, starting transfers between devices, exchange(): return lax.all_to_all(part, axes, split_axis=0, concat_axis=0, tiled=True)  8.71 us
    ppermute x4, waiting for transfers between devices, body(): lax.ppermute(ring[-1], ('y', 'core'), ring_perm((0, 1) if step < 3 else (...  6.97 us
  transfers between devices with their start and end apart: 11, of which 5 were waited for; matrix products, arithmetic and copies ran while one was open for 0% of the time, Pallas kernels for 6%

profile of v7, /device:TPU:32, one launch (start us, length us, event | category | flops | bytes accessed | tf_op | source)
XLA Modules:
  0.0 118.5 jit_solution(5668737026173477571)
XLA Ops:
  0.0 0.7 compare_select_fusion
  0.7 0.2 copy-done
  1.0 2.0 %gather_fusion = bf16[704,128]{1,0:T(8,128)(2,1)S(1)} fusion(bf16[1024,128]{1,0:T(8,128)(2,1)S(1)} %copy-done, s32[1024]{0:T(1024)S(1)} %pad_clamp_fusion), kind=kCustom, calls=%fused_computation | custom fusion | bytes 363264 | tf_op jit(solution)/shard_map/gather | solution.py:152
  3.0 2.1 %all-gather = bf16[1408,128]{1,0:T(8,128)(2,1)S(1)} all-gather(bf16[704,128]{1,0:T(8,128)(2,1)S(1)} %gather_fusion), channel_id=2, replica_groups=mesh['x'=4,'zl'=4,'zh'=3,'y'=8,'core'=2] {'core'}, dimensions={0}, use_global_device_ids=true | all-gather | bytes 540672 | tf_op jit(solution)/shard_map/all_gather | solution.py:156
  5.1 2.6 %collective-permute-start.3 = (bf16[2,704,128]{2,1,0:T(8,128)(2,1)S(1)}, bf16[2,704,128]{2,1,0:T(8,128)(2,1)S(1)}, u32[]{:S(2)}, u32[]{:S(2)}) collective-permute-start(bf16[2,704,128]{2,1,0:T(8,128)(2,1)S(1)} %bitcast.5), channel_id=1, source_target_pairs={{0,2},{1,15},{2,4},{3,1},{4,6},{5,3},{6,8},{7,5},{8,10},{9,7},{10,... | collective-permute-start | bytes 1081352 | tf_op jit(solution)/shard_map/ppermute | solution.py:158
  7.6 16.6 %collective-permute-start = (bf16[704,128]{1,0:T(8,128)(2,1)S(1)}, bf16[704,128]{1,0:T(8,128)(2,1)S(1)}, u32[]{:S(2)}, u32[]{:S(2)}) collective-permute-start(bf16[704,128]{1,0:T(8,128)(2,1)S(1)} %gather_fusion), channel_id=1, source_target_pairs={{0,0},{33,1},{3,2},{18,3},{21,4},{36,5},{6,6},{39,7},{9,8},{24,9},... | collective-permute-start | bytes 540680 | tf_op jit(solution)/shard_map/ppermute | solution.py:160
  24.2 1.9 %collective-permute-start.1 = (bf16[704,128]{1,0:T(8,128)(2,1)S(1)}, bf16[704,128]{1,0:T(8,128)(2,1)S(1)}, u32[]{:S(2)}, u32[]{:S(2)}) collective-permute-start(bf16[704,128]{1,0:T(8,128)(2,1)S(1)} %gather_fusion), channel_id=1, source_target_pairs={{1,0},{34,1},{4,2},{19,3},{22,4},{37,5},{7,6},{40,7},{10,8},{25,9}... | collective-permute-start | bytes 540680 | tf_op jit(solution)/shard_map/ppermute | solution.py:160
  26.1 2.5 %collective-permute-start.2 = (bf16[704,128]{1,0:T(8,128)(2,1)S(1)}, bf16[704,128]{1,0:T(8,128)(2,1)S(1)}, u32[]{:S(2)}, u32[]{:S(2)}) collective-permute-start(bf16[704,128]{1,0:T(8,128)(2,1)S(1)} %gather_fusion), channel_id=1, source_target_pairs={{2,0},{35,1},{5,2},{20,3},{23,4},{38,5},{8,6},{41,7},{11,8},{26,9}... | collective-permute-start | bytes 540680 | tf_op jit(solution)/shard_map/ppermute | solution.py:160
  28.6 0.1 pad_add_fusion.at_ref
  28.7 0.0 collective-permute-done.3.a1_ref
  28.7 4.8 %collective-permute-start.4 = (bf16[2,704,128]{2,1,0:T(8,128)(2,1)S(1)}, bf16[2,704,128]{2,1,0:T(8,128)(2,1)S(1)}, u32[]{:S(2)}, u32[]{:S(2)}) collective-permute-start(bf16[2,704,128]{2,1,0:T(8,128)(2,1)S(1)} %collective-permute-done.3.a1_ref), channel_id=1, source_target_pairs={{0,2},{1,15},{2,4},{3,1},{4,6},{5,3},{6,8},{7,5},{8,10},{9,7},{10,... | collective-permute-start | bytes 1081352 | tf_op jit(solution)/shard_map/ppermute | solution.py:158
  33.5 6.6 %collective-permute-done.refs_0_ = bf16[704,128]{1,0:T(8,128)(2,1)S(1)} collective-permute-done((bf16[704,128]{1,0:T(8,128)(2,1)S(1)}, bf16[704,128]{1,0:T(8,128)(2,1)S(1)}, u32[]{:S(2)}, u32[]{:S(2)}) %collective-permute-start) | collective-permute-done | bytes 180256 | tf_op jit(solution)/shard_map/ppermute | solution.py:160
  40.1 0.0 collective-permute-done.1.refs_1_
  40.1 0.0 collective-permute-done.2.refs_2_
  40.1 0.6 shard_map.37.mine_ref
  40.8 1.9 %collective-permute-start.7 = (bf16[704,384]{1,0:T(8,128)(2,1)S(1)}, bf16[704,384]{1,0:T(8,128)(2,1)S(1)}, u32[]{:S(2)}, u32[]{:S(2)}) collective-permute-start(bf16[704,384]{1,0:T(8,128)(2,1)S(1)} %shard_map.37.mine_ref), channel_id=1, source_target_pairs={{0,1},{1,0},{2,3},{3,2},{4,5},{5,4},{6,7},{7,6},{8,9},{9,8},{10,11... | collective-permute-start | bytes 1622024 | tf_op jit(solution)/shard_map/ppermute | solution.py:163
  42.7 8.7 %collective-permute-start.5 = (bf16[2,704,128]{2,1,0:T(8,128)(2,1)S(1)}, bf16[2,704,128]{2,1,0:T(8,128)(2,1)S(1)}, u32[]{:S(2)}, u32[]{:S(2)}) collective-permute-start(bf16[2,704,128]{2,1,0:T(8,128)(2,1)S(1)} %collective-permute-done.4.a0_ref.a2_ref), channel_id=1, source_target_pairs={{0,2},{1,15},{2,4},{3,1},{4,6},{5,3},{6,8},{7,5},{8,10},{9,7},{10,... | collective-permute-start | bytes 1081352 | tf_op jit(solution)/shard_map/ppermute | solution.py:158
  51.4 3.1 %shard_map.39 = s16[4,2,400,128]{3,2,1,0:T(8,128)(2,1)} custom-call(s32[2]{0:T(128)S(1)} %pad_add_fusion.at_ref, bf16[2,704,128]{2,1,0:T(8,128)(2,1)S(1)} %bitcast.6, bf16[2,704,128]{2,1,0:T(8,128)(2,1)S(1)} %collective-permute-done.3.a1_ref, bf16[2,704,128]{2,1,0:T(8,128)(2,1)S(1)} %collective-permute-done.4.a0_ref.a2_ref, ...), custom_call_target="tpu_custom_call" | custom-call | flops 553648128 | bytes 2000000 | tf_op jit(solution)/shard_map/pallas_call | solution.py:137
  54.5 4.3 %all-to-all-start.1 = ((s16[8,400,128]{2,1,0:T(8,128)(2,1)}), s16[8,400,128]{2,1,0:T(8,128)(2,1)S(1)}, u32[]{:S(2)}, u32[]{:S(2)}) async-start(s16[8,400,128]{2,1,0:T(8,128)(2,1)} %bitcast.4), calls=%async_computation.1 | async-start | bytes 1638400 | tf_op jit(solution)/shard_map/all_to_all | solution.py:148
  58.8 3.6 %collective-permute-start.6 = (bf16[2,704,128]{2,1,0:T(8,128)(2,1)S(1)}, bf16[2,704,128]{2,1,0:T(8,128)(2,1)S(1)}, u32[]{:S(2)}, u32[]{:S(2)}) collective-permute-start(bf16[2,704,128]{2,1,0:T(8,128)(2,1)S(1)} %collective-permute-done.5.a1_ref), channel_id=1, source_target_pairs={{0,2},{2,4},{4,6},{6,8},{8,10},{10,12},{12,14},{14,0},{16,18},{18,... | collective-permute-start | bytes 1081352 | tf_op jit(solution)/shard_map/ppermute | solution.py:158
  62.4 7.0 %collective-permute-done.6.a2_ref = bf16[2,704,128]{2,1,0:T(8,128)(2,1)S(1)} collective-permute-done((bf16[2,704,128]{2,1,0:T(8,128)(2,1)S(1)}, bf16[2,704,128]{2,1,0:T(8,128)(2,1)S(1)}, u32[]{:S(2)}, u32[]{:S(2)}) %collective-permute-start.6) | collective-permute-done | bytes 360480 | tf_op jit(solution)/shard_map/ppermute | solution.py:158
  69.3 3.0 %shard_map.38 = s16[4,2,400,128]{3,2,1,0:T(8,128)(2,1)} custom-call(s32[2]{0:T(128)S(1)} %pad_add_fusion.at_ref, bf16[2,704,128]{2,1,0:T(8,128)(2,1)S(1)} %collective-permute-done.4.a0_ref.a2_ref, bf16[2,704,128]{2,1,0:T(8,128)(2,1)S(1)} %collective-permute-done.5.a1_ref, bf16[2,704,128]{2,1,0:T(8,128)(2,1)S(1)} %collective-permute-done.6.a2_ref, ...), custom_call_target="tpu_custom_call" | custom-call | flops 553648128 | bytes 2000000 | tf_op jit(solution)/shard_map/pallas_call | solution.py:137
  72.4 0.4 all-to-all-done.1.part_ref
  72.7 4.4 %all-to-all-start = ((s16[8,400,128]{2,1,0:T(8,128)(2,1)}), s16[8,400,128]{2,1,0:T(8,128)(2,1)S(1)}, u32[]{:S(2)}, u32[]{:S(2)}) async-start(s16[8,400,128]{2,1,0:T(8,128)(2,1)} %bitcast.3), calls=%async_computation | async-start | bytes 1638400 | tf_op jit(solution)/shard_map/all_to_all | solution.py:148
  77.2 0.5 shard_map.40.refs_0_
  77.7 11.6 %all-to-all-done.part_ref = s16[8,400,128]{2,1,0:T(8,128)(2,1)S(1)} async-done(((s16[8,400,128]{2,1,0:T(8,128)(2,1)}), s16[8,400,128]{2,1,0:T(8,128)(2,1)S(1)}, u32[]{:S(2)}, u32[]{:S(2)}) %all-to-all-start) | async-done | bytes 819232 | tf_op jit(solution)/shard_map/all_to_all | solution.py:148
  89.3 0.6 shard_map.41
  89.9 13.0 %all_to_all.15.part_ref = s16[4,400,128]{2,1,0:T(8,128)(2,1)S(1)} all-to-all(s16[4,400,128]{2,1,0:T(8,128)(2,1)S(1)} %shard_map.41), channel_id=1, replica_groups=mesh['x'=4,'zl'=4,'zh'=3,'y'=8,'core'=2] {'zl'}, dimensions={0} | all-to-all | bytes 819200 | tf_op jit(solution)/shard_map/all_to_all | solution.py:148
  102.8 0.3 shard_map.42
  103.1 1.9 %collective-permute-start.8 = (s16[400,128]{1,0:T(8,128)(2,1)S(1)}, s16[400,128]{1,0:T(8,128)(2,1)S(1)}, u32[]{:S(2)}, u32[]{:S(2)}) collective-permute-start(s16[400,128]{1,0:T(8,128)(2,1)S(1)} %shard_map.42), channel_id=1, source_target_pairs={{0,14},{1,0},{2,48},{3,50},{4,338},{5,340},{6,100},{7,102},{8,150}... | collective-permute-start | bytes 307208 | tf_op jit(solution)/shard_map/ppermute | solution.py:174
  105.0 12.7 %collective-permute-done.8.total_ref = s16[400,128]{1,0:T(8,128)(2,1)S(1)} collective-permute-done((s16[400,128]{1,0:T(8,128)(2,1)S(1)}, s16[400,128]{1,0:T(8,128)(2,1)S(1)}, u32[]{:S(2)}, u32[]{:S(2)}) %collective-permute-start.8) | collective-permute-done | bytes 102432 | tf_op jit(solution)/shard_map/ppermute | solution.py:174
  117.8 0.7 shard_map.43
  (7 shorter events, 0.0 us)
Async XLA Ops:
  0.0 1.0 copy-start
  5.1 23.6 %collective-permute-start.3 = (bf16[2,704,128]{2,1,0:T(8,128)(2,1)S(1)}, bf16[2,704,128]{2,1,0:T(8,128)(2,1)S(1)}, u32[]{:S(2)}, u32[]{:S(2)}) collective-permute-start(bf16[2,704,128]{2,1,0:T(8,128)(2,1)S(1)} %bitcast.5), channel_id=1, source_target_pairs={{0,2},{1,15},{2,4},{3,1},{4,6},{5,3},{6,8},{7,5},{8,10},{9,7},{10,... | collective-permute-start | bytes 1081352 | tf_op jit(solution)/shard_map/ppermute | solution.py:158
  7.6 32.5 %collective-permute-start = (bf16[704,128]{1,0:T(8,128)(2,1)S(1)}, bf16[704,128]{1,0:T(8,128)(2,1)S(1)}, u32[]{:S(2)}, u32[]{:S(2)}) collective-permute-start(bf16[704,128]{1,0:T(8,128)(2,1)S(1)} %gather_fusion), channel_id=1, source_target_pairs={{0,0},{33,1},{3,2},{18,3},{21,4},{36,5},{6,6},{39,7},{9,8},{24,9},... | collective-permute-start | bytes 540680 | tf_op jit(solution)/shard_map/ppermute | solution.py:160
  24.2 15.9 %collective-permute-start.1 = (bf16[704,128]{1,0:T(8,128)(2,1)S(1)}, bf16[704,128]{1,0:T(8,128)(2,1)S(1)}, u32[]{:S(2)}, u32[]{:S(2)}) collective-permute-start(bf16[704,128]{1,0:T(8,128)(2,1)S(1)} %gather_fusion), channel_id=1, source_target_pairs={{1,0},{34,1},{4,2},{19,3},{22,4},{37,5},{7,6},{40,7},{10,8},{25,9}... | collective-permute-start | bytes 540680 | tf_op jit(solution)/shard_map/ppermute | solution.py:160
  26.1 14.0 %collective-permute-start.2 = (bf16[704,128]{1,0:T(8,128)(2,1)S(1)}, bf16[704,128]{1,0:T(8,128)(2,1)S(1)}, u32[]{:S(2)}, u32[]{:S(2)}) collective-permute-start(bf16[704,128]{1,0:T(8,128)(2,1)S(1)} %gather_fusion), channel_id=1, source_target_pairs={{2,0},{35,1},{5,2},{20,3},{23,4},{38,5},{8,6},{41,7},{11,8},{26,9}... | collective-permute-start | bytes 540680 | tf_op jit(solution)/shard_map/ppermute | solution.py:160
  28.7 12.1 %collective-permute-start.4 = (bf16[2,704,128]{2,1,0:T(8,128)(2,1)S(1)}, bf16[2,704,128]{2,1,0:T(8,128)(2,1)S(1)}, u32[]{:S(2)}, u32[]{:S(2)}) collective-permute-start(bf16[2,704,128]{2,1,0:T(8,128)(2,1)S(1)} %collective-permute-done.3.a1_ref), channel_id=1, source_target_pairs={{0,2},{1,15},{2,4},{3,1},{4,6},{5,3},{6,8},{7,5},{8,10},{9,7},{10,... | collective-permute-start | bytes 1081352 | tf_op jit(solution)/shard_map/ppermute | solution.py:158
  40.8 10.7 %collective-permute-start.7 = (bf16[704,384]{1,0:T(8,128)(2,1)S(1)}, bf16[704,384]{1,0:T(8,128)(2,1)S(1)}, u32[]{:S(2)}, u32[]{:S(2)}) collective-permute-start(bf16[704,384]{1,0:T(8,128)(2,1)S(1)} %shard_map.37.mine_ref), channel_id=1, source_target_pairs={{0,1},{1,0},{2,3},{3,2},{4,5},{5,4},{6,7},{7,6},{8,9},{9,8},{10,11... | collective-permute-start | bytes 1622024 | tf_op jit(solution)/shard_map/ppermute | solution.py:163
  42.7 16.1 %collective-permute-start.5 = (bf16[2,704,128]{2,1,0:T(8,128)(2,1)S(1)}, bf16[2,704,128]{2,1,0:T(8,128)(2,1)S(1)}, u32[]{:S(2)}, u32[]{:S(2)}) collective-permute-start(bf16[2,704,128]{2,1,0:T(8,128)(2,1)S(1)} %collective-permute-done.4.a0_ref.a2_ref), channel_id=1, source_target_pairs={{0,2},{1,15},{2,4},{3,1},{4,6},{5,3},{6,8},{7,5},{8,10},{9,7},{10,... | collective-permute-start | bytes 1081352 | tf_op jit(solution)/shard_map/ppermute | solution.py:158
  54.5 18.2 %all-to-all-start.1 = ((s16[8,400,128]{2,1,0:T(8,128)(2,1)}), s16[8,400,128]{2,1,0:T(8,128)(2,1)S(1)}, u32[]{:S(2)}, u32[]{:S(2)}) async-start(s16[8,400,128]{2,1,0:T(8,128)(2,1)} %bitcast.4), calls=%async_computation.1 | async-start | bytes 1638400 | tf_op jit(solution)/shard_map/all_to_all | solution.py:148
  58.8 10.5 %collective-permute-start.6 = (bf16[2,704,128]{2,1,0:T(8,128)(2,1)S(1)}, bf16[2,704,128]{2,1,0:T(8,128)(2,1)S(1)}, u32[]{:S(2)}, u32[]{:S(2)}) collective-permute-start(bf16[2,704,128]{2,1,0:T(8,128)(2,1)S(1)} %collective-permute-done.5.a1_ref), channel_id=1, source_target_pairs={{0,2},{2,4},{4,6},{6,8},{8,10},{10,12},{12,14},{14,0},{16,18},{18,... | collective-permute-start | bytes 1081352 | tf_op jit(solution)/shard_map/ppermute | solution.py:158
  72.7 16.6 %all-to-all-start = ((s16[8,400,128]{2,1,0:T(8,128)(2,1)}), s16[8,400,128]{2,1,0:T(8,128)(2,1)S(1)}, u32[]{:S(2)}, u32[]{:S(2)}) async-start(s16[8,400,128]{2,1,0:T(8,128)(2,1)} %bitcast.3), calls=%async_computation | async-start | bytes 1638400 | tf_op jit(solution)/shard_map/all_to_all | solution.py:148
  102.8 14.9 %copy-start.1 = (f32[128,384]{1,0:T(8,128)S(1)}, f32[128,384]{1,0:T(8,128)}, u32[]{:S(2)}) copy-start(f32[128,384]{1,0:T(8,128)} %old_ref.1) | copy-start | bytes 589828
  103.1 14.7 %collective-permute-start.8 = (s16[400,128]{1,0:T(8,128)(2,1)S(1)}, s16[400,128]{1,0:T(8,128)(2,1)S(1)}, u32[]{:S(2)}, u32[]{:S(2)}) collective-permute-start(s16[400,128]{1,0:T(8,128)(2,1)S(1)} %shard_map.42), channel_id=1, source_target_pairs={{0,14},{1,0},{2,48},{3,50},{4,338},{5,340},{6,100},{7,102},{8,150}... | collective-permute-start | bytes 307208 | tf_op jit(solution)/shard_map/ppermute | solution.py:174

commit v8 on v7

--- a/solution.py
+++ b/solution.py
@@ -12,12 +12,16 @@
 NX, NZL, NZH, NY, NC = 4, 4, 3, 8, 2
 AXES = ("x", "zl", "zh", "y", "core")
 TRIPLE = ((0, 11), (1, 6), (7, 12), (2, 13), (3, 8), (9, 14), (4, 15), (5, 10))
-OFFSET = (((-1, -2), (-3, -4)), ((0, 1), (2, 3)))
+OFFSET = (
+    (((-1, 0), (1, -2)), ((2, -3), (4, 3))),
+    (((1, 0), (-1, 2)), ((-2, 3), (4, -3))),
+)
 LANES = 128
 ROWS = 128
 TILE = 16
 CODED = NZH * ROWS + TILE
 TOP = 32767.0
+COST = (10**10, 4*10**9, 10**9, 10**10)
 
 
 def triple_perm(i):
@@ -29,10 +33,8 @@
     ]
 
 
-def ring_perm(cores):
-    return [
-        (y * NC + c, (y + 1 - 2 * c) % NY * NC + c) for y in range(NY) for c in cores
-    ]
+def ring_perm():
+    return [(y * NC + c, (y + 1 - 2 * c) % NY * NC + c) for y in range(NY) for c in range(NC)]
 
 
 def place_perm():
@@ -41,9 +43,9 @@
         for zl in range(NZL):
             for y in range(NY):
                 for c in range(NC):
-                    to_y = (y + OFFSET[c][zl // 2][x // 2]) % NY
+                    to_y = (y + OFFSET[c][zl // 2][zl % 2][x // 2]) % NY
                     source = ((x * NZL + zl) * NY + y) * NC + c
-                    pairs.append((source, (TRIPLE[y][zl % 2] * NY + to_y) * NC + x % 2))
+                    pairs.append((source, (TRIPLE[y][c] * NY + to_y) * NC + x % 2))
     return pairs
 
 
@@ -97,17 +99,31 @@
         out_ref[:, pl.ds(pl.multiple_of(j * LANES, LANES), LANES)] = refs[i][...]
 
 
-def product_kernel(at_ref, a0_ref, a1_ref, a2_ref, mine_ref, other_ref, out_ref):
-    core = at_ref[1]
-    for i, (up_ref, down_ref) in enumerate(((a1_ref, a0_ref), (a2_ref, a1_ref))):
-        rows = [jnp.where(core == 0, up_ref[c], down_ref[c]) for c in range(NC)]
-        rows = jnp.concatenate(rows, axis=1)
-        for columns_ref, cw in ((mine_ref, core), (other_ref, 1 - core)):
+def copy_kernel(in_ref, out_ref):
+    out_ref[...] = in_ref[...]
+
+
+def multiply(pairs, columns_ref, out_ref):
+    for side in range(2):
+        for i in range(2):
             out = lax.dot_general(
-                rows, columns_ref[...], (((0,), (0,)), ((), ())), preferred_element_type=jnp.float32
+                jnp.concatenate(pairs[side][i], axis=1), columns_ref[...],
+                (((0,), (0,)), ((), ())), preferred_element_type=jnp.float32,
             )
             for c in range(NC):
-                encode(lane_blocks(out[c * ROWS : (c + 1) * ROWS]), store(out_ref, i * NC + c, cw))
+                blocks = lane_blocks(out[c * ROWS : (c + 1) * ROWS])
+                encode(blocks, store(out_ref, i * NC + c, side))
+
+
+def near_kernel(own_ref, one_ref, one_other_ref, two_ref, columns_ref, out_ref):
+    pairs = [[ref[c] for c in range(NC)] for ref in (one_ref, own_ref, one_other_ref, two_ref)]
+    multiply((pairs[:2], pairs[2:]), columns_ref, out_ref)
+
+
+def far_kernel(at_ref, two_other_ref, three_ref, three_other_ref, far_ref, far_other_ref, columns_ref, out_ref):
+    pairs = [[ref[c] for c in range(NC)] for ref in (two_other_ref, three_ref, three_other_ref)]
+    far = [jnp.where(at_ref[1] == c, far_ref[...], far_other_ref[...]) for c in range(NC)]
+    multiply((pairs[:2], (far, pairs[2])), columns_ref, out_ref)
 
 
 def sum_x_kernel(part_ref, *refs):
@@ -154,19 +170,26 @@
     scale = 0.1 / float(NX * NZL * k)
     at = jnp.stack([lax.axis_index("zh"), lax.axis_index("core")]).astype(jnp.int32)
     ring = [lax.all_gather(block, "core", axis=0)]
-    for step in range(4):
-        ring.append(lax.ppermute(ring[-1], ("y", "core"), ring_perm((0, 1) if step < 3 else (0,))))
+    for _ in range(3):
+        ring.append(lax.ppermute(ring[-1], ("y", "core"), ring_perm()))
     block, _ = lax.optimization_barrier((block, ring[0]))
-    mine = [lax.ppermute(block, ("zh", "y", "core"), triple_perm(i)) for i in range(NZH)]
-    mine = call(triple_kernel, (k, 384), jnp.bfloat16, 10**10, at, *mine, scalars=True)
-    mine, ring[2] = lax.optimization_barrier((mine, ring[2]))
-    other = lax.ppermute(mine, "core", [(0, 1), (1, 0)])
+    swap = lambda value: lax.ppermute(value, "core", [(0, 1), (1, 0)])
+    columns = [lax.ppermute(block, ("zh", "y", "core"), triple_perm(i)) for i in range(NZH)]
+    one_other = swap(ring[1])
+    columns = call(triple_kernel, (k, 384), jnp.bfloat16, COST[0], at, *columns, scalars=True)
+    columns, ring[2] = lax.optimization_barrier((columns, ring[2]))
+    far = lax.ppermute(block, "y", [(y, (y + 4) % NY) for y in range(NY)])
+    far = call(copy_kernel, (k, LANES), jnp.bfloat16, COST[3], far)
+    near = call(
+        near_kernel, (NX, NC, CODED, LANES), jnp.int16, COST[1],
+        ring[0], ring[1], one_other, ring[2], columns,
+    )
+    away = call(
+        far_kernel, (NX, NC, CODED, LANES), jnp.int16, COST[2],
+        at, swap(ring[2]), ring[3], swap(ring[3]), far, swap(far), columns, scalars=True,
+    )
     part = []
-    for half in range(2):
-        out = call(
-            product_kernel, (NX, NC, CODED, LANES), jnp.int16, 2 * k * 512 * 768,
-            at, *ring[2 * half : 2 * half + 3], mine, other, scalars=True,
-        )
+    for half, out in enumerate((near, away)):
         out = exchange(out.reshape(NX * NC, CODED, LANES), "x")
         part = [call(sum_x_kernel, (NC * (half + 1), CODED, LANES), jnp.int16, 0, out, *part)]
     part = exchange(part[0], "zl")

time: 119 us -> 128 us (1.076)
  the two profiles are of different devices: /device:TPU:32 before, /device:TPU:4 now
where the time goes in v8:
time: 128 us; the launch traced here: 127 us
  starting transfers between devices  65.7 us (51%)
  waiting for transfers between devices  29.2 us (23%)
  blocking collectives  20.6 us (16%)
  Pallas kernels  8.43 us (7%)
  local copies, waits for them, and re-layouts  2.25 us (2%)
    ppermute x3, starting transfers between devices, body(): lax.ppermute(block, ('zh', 'y', 'core'), triple_perm(i))  27.1 us
    all_to_all x1, blocking collectives, exchange(): return lax.all_to_all(part, axes, split_axis=0, concat_axis=0, tiled=True)  18.5 us
    all_to_all x2, starting transfers between devices, exchange(): return lax.all_to_all(part, axes, split_axis=0, concat_axis=0, tiled=True)  11.2 us
    all_to_all x2, waiting for transfers between devices, exchange(): return lax.all_to_all(part, axes, split_axis=0, concat_axis=0, tiled=True)  11 us
    ppermute x4, starting transfers between devices, body(): swap = lambda value: lax.ppermute(value, 'core', [(0, 1), (1, 0)])  10.8 us
    ppermute x1, waiting for transfers between devices, body(): total = lax.ppermute(total, ('x', 'zl', 'y', 'core'), place_perm())  10.2 us
    ppermute x3, starting transfers between devices, body(): ring.append(lax.ppermute(ring[-1], ('y', 'core'), ring_perm()))  9.89 us
    pallas_call x8, Pallas kernels, call(): pl.pallas_call(kernel, in_specs=specs, out_specs=pl.BlockSpec(memory_spac...  8.43 us
  transfers between devices with their start and end apart: 14, of which 7 were waited for; matrix products, arithmetic and copies ran while one was open for 0% of the time, Pallas kernels for 5%

profile of v8, /device:TPU:4, one launch (start us, length us, event | category | flops | bytes accessed | tf_op | source)
XLA Modules:
  0.0 127.2 jit_solution(4099447955198932536)
XLA Ops:
  0.0 0.7 compare_select_fusion
  1.0 2.0 %gather_fusion = bf16[704,128]{1,0:T(8,128)(2,1)S(1)} fusion(bf16[1024,128]{1,0:T(8,128)(2,1)S(1)} %copy-done, s32[1024]{0:T(1024)S(1)} %pad_clamp_fusion), kind=kCustom, calls=%fused_computation | custom fusion | bytes 363264 | tf_op jit(solution)/shard_map/gather | solution.py:168
  3.0 2.1 %all-gather = bf16[1408,128]{1,0:T(8,128)(2,1)S(1)} all-gather(bf16[704,128]{1,0:T(8,128)(2,1)S(1)} %gather_fusion), channel_id=2, replica_groups=mesh['x'=4,'zl'=4,'zh'=3,'y'=8,'core'=2] {'core'}, dimensions={0}, use_global_device_ids=true | all-gather | bytes 540672 | tf_op jit(solution)/shard_map/all_gather | solution.py:172
  5.1 3.5 %collective-permute-start.3 = (bf16[2,704,128]{2,1,0:T(8,128)(2,1)S(1)}, bf16[2,704,128]{2,1,0:T(8,128)(2,1)S(1)}, u32[]{:S(2)}, u32[]{:S(2)}) collective-permute-start(bf16[2,704,128]{2,1,0:T(8,128)(2,1)S(1)} %bitcast.5), channel_id=1, source_target_pairs={{0,2},{1,15},{2,4},{3,1},{4,6},{5,3},{6,8},{7,5},{8,10},{9,7},{10,... | collective-permute-start | bytes 1081352 | tf_op jit(solution)/shard_map/ppermute | solution.py:174
  8.5 0.7 collective-permute-start
  9.2 18.5 %collective-permute-start.1 = (bf16[704,128]{1,0:T(8,128)(2,1)S(1)}, bf16[704,128]{1,0:T(8,128)(2,1)S(1)}, u32[]{:S(2)}, u32[]{:S(2)}) collective-permute-start(bf16[704,128]{1,0:T(8,128)(2,1)S(1)} %gather_fusion), channel_id=1, source_target_pairs={{1,0},{34,1},{4,2},{19,3},{22,4},{37,5},{7,6},{40,7},{10,8},{25,9}... | collective-permute-start | bytes 540680 | tf_op jit(solution)/shard_map/ppermute | solution.py:177
  27.7 7.9 %collective-permute-start.2 = (bf16[704,128]{1,0:T(8,128)(2,1)S(1)}, bf16[704,128]{1,0:T(8,128)(2,1)S(1)}, u32[]{:S(2)}, u32[]{:S(2)}) collective-permute-start(bf16[704,128]{1,0:T(8,128)(2,1)S(1)} %gather_fusion), channel_id=1, source_target_pairs={{2,0},{35,1},{5,2},{20,3},{23,4},{38,5},{8,6},{41,7},{11,8},{26,9}... | collective-permute-start | bytes 540680 | tf_op jit(solution)/shard_map/ppermute | solution.py:177
  35.7 1.9 %collective-permute-start.8 = (bf16[704,128]{1,0:T(8,128)(2,1)S(1)}, bf16[704,128]{1,0:T(8,128)(2,1)S(1)}, u32[]{:S(2)}, u32[]{:S(2)}) collective-permute-start(bf16[704,128]{1,0:T(8,128)(2,1)S(1)} %gather_fusion), channel_id=1, source_target_pairs={{0,8},{2,10},{4,12},{6,14},{8,0},{10,2},{12,4},{14,6},{1,9},{3,11}... | collective-permute-start | bytes 540680 | tf_op jit(solution)/shard_map/ppermute | solution.py:181
  37.7 3.6 %collective-permute-start.4 = (bf16[2,704,128]{2,1,0:T(8,128)(2,1)S(1)}, bf16[2,704,128]{2,1,0:T(8,128)(2,1)S(1)}, u32[]{:S(2)}, u32[]{:S(2)}) collective-permute-start(bf16[2,704,128]{2,1,0:T(8,128)(2,1)S(1)} %collective-permute-done.3.one_ref), channel_id=1, source_target_pairs={{0,2},{1,15},{2,4},{3,1},{4,6},{5,3},{6,8},{7,5},{8,10},{9,7},{10,... | collective-permute-start | bytes 1081352 | tf_op jit(solution)/shard_map/ppermute | solution.py:174
  41.3 1.9 %collective-permute-start.10 = (bf16[2,704,128]{2,1,0:T(8,128)(2,1)S(1)}, bf16[2,704,128]{2,1,0:T(8,128)(2,1)S(1)}, u32[]{:S(2)}, u32[]{:S(2)}) collective-permute-start(bf16[2,704,128]{2,1,0:T(8,128)(2,1)S(1)} %collective-permute-done.3.one_ref), channel_id=1, source_target_pairs={{0,1},{1,0},{2,3},{3,2},{4,5},{5,4},{6,7},{7,6},{8,9},{9,8},{10,11... | collective-permute-start | bytes 1081352 | tf_op jit(solution)/shard_map/ppermute | solution.py:176
  43.2 2.2 %collective-permute-done.2.refs_2_ = bf16[704,128]{1,0:T(8,128)(2,1)S(1)} collective-permute-done((bf16[704,128]{1,0:T(8,128)(2,1)S(1)}, bf16[704,128]{1,0:T(8,128)(2,1)S(1)}, u32[]{:S(2)}, u32[]{:S(2)}) %collective-permute-start.2) | collective-permute-done | bytes 180256 | tf_op jit(solution)/shard_map/ppermute | solution.py:177
  45.4 0.6 shard_map.37.columns_ref
  46.0 4.1 %collective-permute-done.4.two_ref = bf16[2,704,128]{2,1,0:T(8,128)(2,1)S(1)} collective-permute-done((bf16[2,704,128]{2,1,0:T(8,128)(2,1)S(1)}, bf16[2,704,128]{2,1,0:T(8,128)(2,1)S(1)}, u32[]{:S(2)}, u32[]{:S(2)}) %collective-permute-start.4) | collective-permute-done | bytes 360480 | tf_op jit(solution)/shard_map/ppermute | solution.py:174
  50.1 4.2 %collective-permute-start.5 = (bf16[2,704,128]{2,1,0:T(8,128)(2,1)S(1)}, bf16[2,704,128]{2,1,0:T(8,128)(2,1)S(1)}, u32[]{:S(2)}, u32[]{:S(2)}) collective-permute-start(bf16[2,704,128]{2,1,0:T(8,128)(2,1)S(1)} %collective-permute-done.4.two_ref), channel_id=1, source_target_pairs={{0,1},{1,0},{2,3},{3,2},{4,5},{5,4},{6,7},{7,6},{8,9},{9,8},{10,11... | collective-permute-start | bytes 1081352 | tf_op jit(solution)/shard_map/ppermute | solution.py:176
  54.3 2.9 %collective-permute-start.6 = (bf16[2,704,128]{2,1,0:T(8,128)(2,1)S(1)}, bf16[2,704,128]{2,1,0:T(8,128)(2,1)S(1)}, u32[]{:S(2)}, u32[]{:S(2)}) collective-permute-start(bf16[2,704,128]{2,1,0:T(8,128)(2,1)S(1)} %collective-permute-done.4.two_ref), channel_id=1, source_target_pairs={{0,2},{1,15},{2,4},{3,1},{4,6},{5,3},{6,8},{7,5},{8,10},{9,7},{10,... | collective-permute-start | bytes 1081352 | tf_op jit(solution)/shard_map/ppermute | solution.py:174
  57.2 2.6 %shard_map.40 = s16[4,2,400,128]{3,2,1,0:T(8,128)(2,1)} custom-call(bf16[2,704,128]{2,1,0:T(8,128)(2,1)S(1)} %bitcast.6, bf16[2,704,128]{2,1,0:T(8,128)(2,1)S(1)} %collective-permute-done.3.one_ref, bf16[2,704,128]{2,1,0:T(8,128)(2,1)S(1)} %collective-permute-done.10.one_other_ref, bf16[2,704,128]{2,1,0:T(8,128)(2,1)S(1)} %collective-permute-done.4.two_ref, ...), custom_call_target="tpu_custom_call" | custom-call | flops 4000000000 | bytes 2000000 | tf_op jit(solution)/shard_map/pallas_call | solution.py:153
  59.8 4.8 %all-to-all-start.1 = ((s16[8,400,128]{2,1,0:T(8,128)(2,1)}), s16[8,400,128]{2,1,0:T(8,128)(2,1)S(1)}, u32[]{:S(2)}, u32[]{:S(2)}) async-start(s16[8,400,128]{2,1,0:T(8,128)(2,1)} %bitcast.4), calls=%async_computation.1 | async-start | bytes 1638400 | tf_op jit(solution)/shard_map/all_to_all | solution.py:164
  64.6 0.3 collective-permute-done.6.three_ref
  64.9 2.7 %collective-permute-start.7 = (bf16[2,704,128]{2,1,0:T(8,128)(2,1)S(1)}, bf16[2,704,128]{2,1,0:T(8,128)(2,1)S(1)}, u32[]{:S(2)}, u32[]{:S(2)}) collective-permute-start(bf16[2,704,128]{2,1,0:T(8,128)(2,1)S(1)} %collective-permute-done.6.three_ref), channel_id=1, source_target_pairs={{0,1},{1,0},{2,3},{3,2},{4,5},{5,4},{6,7},{7,6},{8,9},{9,8},{10,11... | collective-permute-start | bytes 1081352 | tf_op jit(solution)/shard_map/ppermute | solution.py:176
  67.6 1.9 %collective-permute-start.9 = (bf16[704,128]{1,0:T(8,128)(2,1)S(1)}, bf16[704,128]{1,0:T(8,128)(2,1)S(1)}, u32[]{:S(2)}, u32[]{:S(2)}) collective-permute-start(bf16[704,128]{1,0:T(8,128)(2,1)S(1)} %shard_map.38.far_ref), channel_id=1, source_target_pairs={{0,1},{1,0},{2,3},{3,2},{4,5},{5,4},{6,7},{7,6},{8,9},{9,8},{10,11... | collective-permute-start | bytes 540680 | tf_op jit(solution)/shard_map/ppermute | solution.py:176
  69.6 1.4 %collective-permute-done.9.far_other_ref = bf16[704,128]{1,0:T(8,128)(2,1)S(1)} collective-permute-done((bf16[704,128]{1,0:T(8,128)(2,1)S(1)}, bf16[704,128]{1,0:T(8,128)(2,1)S(1)}, u32[]{:S(2)}, u32[]{:S(2)}) %collective-permute-start.9) | collective-permute-done | bytes 180256 | tf_op jit(solution)/shard_map/ppermute | solution.py:176
  71.0 3.1 %shard_map.39 = s16[4,2,400,128]{3,2,1,0:T(8,128)(2,1)} custom-call(s32[2]{0:T(128)S(1)} %pad_add_fusion.at_ref, bf16[2,704,128]{2,1,0:T(8,128)(2,1)S(1)} %collective-permute-done.5.two_other_ref, bf16[2,704,128]{2,1,0:T(8,128)(2,1)S(1)} %collective-permute-done.6.three_ref, bf16[2,704,128]{2,1,0:T(8,128)(2,1)S(1)} %collective-permute-done.7.three_other_ref, ...), custom_call_target="tpu_custom_call" | custom-call | flops 1000000000 | bytes 2000000 | tf_op jit(solution)/shard_map/pallas_call | solution.py:153
  74.1 1.2 all-to-all-done.1.part_ref
  75.3 6.4 %all-to-all-start = ((s16[8,400,128]{2,1,0:T(8,128)(2,1)}), s16[8,400,128]{2,1,0:T(8,128)(2,1)S(1)}, u32[]{:S(2)}, u32[]{:S(2)}) async-start(s16[8,400,128]{2,1,0:T(8,128)(2,1)} %bitcast.3), calls=%async_computation | async-start | bytes 1638400 | tf_op jit(solution)/shard_map/all_to_all | solution.py:164
  81.7 0.5 shard_map.41.refs_0_
  82.3 9.7 %all-to-all-done.part_ref = s16[8,400,128]{2,1,0:T(8,128)(2,1)S(1)} async-done(((s16[8,400,128]{2,1,0:T(8,128)(2,1)}), s16[8,400,128]{2,1,0:T(8,128)(2,1)S(1)}, u32[]{:S(2)}, u32[]{:S(2)}) %all-to-all-start) | async-done | bytes 819232 | tf_op jit(solution)/shard_map/all_to_all | solution.py:164
  92.0 0.6 shard_map.42
  92.6 18.5 %all_to_all.15.part_ref = s16[4,400,128]{2,1,0:T(8,128)(2,1)S(1)} all-to-all(s16[4,400,128]{2,1,0:T(8,128)(2,1)S(1)} %shard_map.42), channel_id=1, replica_groups=mesh['x'=4,'zl'=4,'zh'=3,'y'=8,'core'=2] {'zl'}, dimensions={0} | all-to-all | bytes 819200 | tf_op jit(solution)/shard_map/all_to_all | solution.py:164
  111.2 0.3 shard_map.43
  111.4 4.8 %collective-permute-start.11 = (s16[400,128]{1,0:T(8,128)(2,1)S(1)}, s16[400,128]{1,0:T(8,128)(2,1)S(1)}, u32[]{:S(2)}, u32[]{:S(2)}) collective-permute-start(s16[400,128]{1,0:T(8,128)(2,1)S(1)} %shard_map.43), channel_id=1, source_target_pairs={{0,14},{1,530},{2,48},{3,292},{4,338},{5,582},{6,100},{7,632},{8,1... | collective-permute-start | bytes 307208 | tf_op jit(solution)/shard_map/ppermute | solution.py:197
  116.2 10.2 %collective-permute-done.11.total_ref = s16[400,128]{1,0:T(8,128)(2,1)S(1)} collective-permute-done((s16[400,128]{1,0:T(8,128)(2,1)S(1)}, s16[400,128]{1,0:T(8,128)(2,1)S(1)}, u32[]{:S(2)}, u32[]{:S(2)}) %collective-permute-start.11) | collective-permute-done | bytes 102432 | tf_op jit(solution)/shard_map/ppermute | solution.py:197
  126.4 0.7 shard_map.44
  (14 shorter events, 0.3 us)
Async XLA Ops:
  0.0 1.0 copy-start
  5.1 32.6 %collective-permute-start.3 = (bf16[2,704,128]{2,1,0:T(8,128)(2,1)S(1)}, bf16[2,704,128]{2,1,0:T(8,128)(2,1)S(1)}, u32[]{:S(2)}, u32[]{:S(2)}) collective-permute-start(bf16[2,704,128]{2,1,0:T(8,128)(2,1)S(1)} %bitcast.5), channel_id=1, source_target_pairs={{0,2},{1,15},{2,4},{3,1},{4,6},{5,3},{6,8},{7,5},{8,10},{9,7},{10,... | collective-permute-start | bytes 1081352 | tf_op jit(solution)/shard_map/ppermute | solution.py:174
  8.5 32.7 %collective-permute-start = (bf16[704,128]{1,0:T(8,128)(2,1)S(1)}, bf16[704,128]{1,0:T(8,128)(2,1)S(1)}, u32[]{:S(2)}, u32[]{:S(2)}) collective-permute-start(bf16[704,128]{1,0:T(8,128)(2,1)S(1)} %gather_fusion), channel_id=1, source_target_pairs={{0,0},{33,1},{3,2},{18,3},{21,4},{36,5},{6,6},{39,7},{9,8},{24,9},... | collective-permute-start | bytes 540680 | tf_op jit(solution)/shard_map/ppermute | solution.py:177
  9.2 34.0 %collective-permute-start.1 = (bf16[704,128]{1,0:T(8,128)(2,1)S(1)}, bf16[704,128]{1,0:T(8,128)(2,1)S(1)}, u32[]{:S(2)}, u32[]{:S(2)}) collective-permute-start(bf16[704,128]{1,0:T(8,128)(2,1)S(1)} %gather_fusion), channel_id=1, source_target_pairs={{1,0},{34,1},{4,2},{19,3},{22,4},{37,5},{7,6},{40,7},{10,8},{25,9}... | collective-permute-start | bytes 540680 | tf_op jit(solution)/shard_map/ppermute | solution.py:177
  27.7 17.6 %collective-permute-start.2 = (bf16[704,128]{1,0:T(8,128)(2,1)S(1)}, bf16[704,128]{1,0:T(8,128)(2,1)S(1)}, u32[]{:S(2)}, u32[]{:S(2)}) collective-permute-start(bf16[704,128]{1,0:T(8,128)(2,1)S(1)} %gather_fusion), channel_id=1, source_target_pairs={{2,0},{35,1},{5,2},{20,3},{23,4},{38,5},{8,6},{41,7},{11,8},{26,9}... | collective-permute-start | bytes 540680 | tf_op jit(solution)/shard_map/ppermute | solution.py:177
  35.7 32.0 %collective-permute-start.8 = (bf16[704,128]{1,0:T(8,128)(2,1)S(1)}, bf16[704,128]{1,0:T(8,128)(2,1)S(1)}, u32[]{:S(2)}, u32[]{:S(2)}) collective-permute-start(bf16[704,128]{1,0:T(8,128)(2,1)S(1)} %gather_fusion), channel_id=1, source_target_pairs={{0,8},{2,10},{4,12},{6,14},{8,0},{10,2},{12,4},{14,6},{1,9},{3,11}... | collective-permute-start | bytes 540680 | tf_op jit(solution)/shard_map/ppermute | solution.py:181
  37.7 12.5 %collective-permute-start.4 = (bf16[2,704,128]{2,1,0:T(8,128)(2,1)S(1)}, bf16[2,704,128]{2,1,0:T(8,128)(2,1)S(1)}, u32[]{:S(2)}, u32[]{:S(2)}) collective-permute-start(bf16[2,704,128]{2,1,0:T(8,128)(2,1)S(1)} %collective-permute-done.3.one_ref), channel_id=1, source_target_pairs={{0,2},{1,15},{2,4},{3,1},{4,6},{5,3},{6,8},{7,5},{8,10},{9,7},{10,... | collective-permute-start | bytes 1081352 | tf_op jit(solution)/shard_map/ppermute | solution.py:174
  41.3 16.0 %collective-permute-start.10 = (bf16[2,704,128]{2,1,0:T(8,128)(2,1)S(1)}, bf16[2,704,128]{2,1,0:T(8,128)(2,1)S(1)}, u32[]{:S(2)}, u32[]{:S(2)}) collective-permute-start(bf16[2,704,128]{2,1,0:T(8,128)(2,1)S(1)} %collective-permute-done.3.one_ref), channel_id=1, source_target_pairs={{0,1},{1,0},{2,3},{3,2},{4,5},{5,4},{6,7},{7,6},{8,9},{9,8},{10,11... | collective-permute-start | bytes 1081352 | tf_op jit(solution)/shard_map/ppermute | solution.py:176
  50.1 20.8 %collective-permute-start.5 = (bf16[2,704,128]{2,1,0:T(8,128)(2,1)S(1)}, bf16[2,704,128]{2,1,0:T(8,128)(2,1)S(1)}, u32[]{:S(2)}, u32[]{:S(2)}) collective-permute-start(bf16[2,704,128]{2,1,0:T(8,128)(2,1)S(1)} %collective-permute-done.4.two_ref), channel_id=1, source_target_pairs={{0,1},{1,0},{2,3},{3,2},{4,5},{5,4},{6,7},{7,6},{8,9},{9,8},{10,11... | collective-permute-start | bytes 1081352 | tf_op jit(solution)/shard_map/ppermute | solution.py:176
  54.3 10.5 %collective-permute-start.6 = (bf16[2,704,128]{2,1,0:T(8,128)(2,1)S(1)}, bf16[2,704,128]{2,1,0:T(8,128)(2,1)S(1)}, u32[]{:S(2)}, u32[]{:S(2)}) collective-permute-start(bf16[2,704,128]{2,1,0:T(8,128)(2,1)S(1)} %collective-permute-done.4.two_ref), channel_id=1, source_target_pairs={{0,2},{1,15},{2,4},{3,1},{4,6},{5,3},{6,8},{7,5},{8,10},{9,7},{10,... | collective-permute-start | bytes 1081352 | tf_op jit(solution)/shard_map/ppermute | solution.py:174
  59.8 15.5 %all-to-all-start.1 = ((s16[8,400,128]{2,1,0:T(8,128)(2,1)}), s16[8,400,128]{2,1,0:T(8,128)(2,1)S(1)}, u32[]{:S(2)}, u32[]{:S(2)}) async-start(s16[8,400,128]{2,1,0:T(8,128)(2,1)} %bitcast.4), calls=%async_computation.1 | async-start | bytes 1638400 | tf_op jit(solution)/shard_map/all_to_all | solution.py:164
  64.9 6.1 %collective-permute-start.7 = (bf16[2,704,128]{2,1,0:T(8,128)(2,1)S(1)}, bf16[2,704,128]{2,1,0:T(8,128)(2,1)S(1)}, u32[]{:S(2)}, u32[]{:S(2)}) collective-permute-start(bf16[2,704,128]{2,1,0:T(8,128)(2,1)S(1)} %collective-permute-done.6.three_ref), channel_id=1, source_target_pairs={{0,1},{1,0},{2,3},{3,2},{4,5},{5,4},{6,7},{7,6},{8,9},{9,8},{10,11... | collective-permute-start | bytes 1081352 | tf_op jit(solution)/shard_map/ppermute | solution.py:176
  67.6 3.3 %collective-permute-start.9 = (bf16[704,128]{1,0:T(8,128)(2,1)S(1)}, bf16[704,128]{1,0:T(8,128)(2,1)S(1)}, u32[]{:S(2)}, u32[]{:S(2)}) collective-permute-start(bf16[704,128]{1,0:T(8,128)(2,1)S(1)} %shard_map.38.far_ref), channel_id=1, source_target_pairs={{0,1},{1,0},{2,3},{3,2},{4,5},{5,4},{6,7},{7,6},{8,9},{9,8},{10,11... | collective-permute-start | bytes 540680 | tf_op jit(solution)/shard_map/ppermute | solution.py:176
  75.3 16.7 %all-to-all-start = ((s16[8,400,128]{2,1,0:T(8,128)(2,1)}), s16[8,400,128]{2,1,0:T(8,128)(2,1)S(1)}, u32[]{:S(2)}, u32[]{:S(2)}) async-start(s16[8,400,128]{2,1,0:T(8,128)(2,1)} %bitcast.3), calls=%async_computation | async-start | bytes 1638400 | tf_op jit(solution)/shard_map/all_to_all | solution.py:164
  111.1 15.3 %copy-start.1 = (f32[128,384]{1,0:T(8,128)S(1)}, f32[128,384]{1,0:T(8,128)}, u32[]{:S(2)}) copy-start(f32[128,384]{1,0:T(8,128)} %old_ref.1) | copy-start | bytes 589828
  111.4 15.0 %collective-permute-start.11 = (s16[400,128]{1,0:T(8,128)(2,1)S(1)}, s16[400,128]{1,0:T(8,128)(2,1)S(1)}, u32[]{:S(2)}, u32[]{:S(2)}) collective-permute-start(s16[400,128]{1,0:T(8,128)(2,1)S(1)} %shard_map.43), channel_id=1, source_target_pairs={{0,14},{1,530},{2,48},{3,292},{4,338},{5,582},{6,100},{7,632},{8,1... | collective-permute-start | bytes 307208 | tf_op jit(solution)/shard_map/ppermute | solution.py:197

commit v9 on v7

--- a/solution.py
+++ b/solution.py
@@ -16,8 +16,9 @@
 LANES = 128
 ROWS = 128
 TILE = 16
+LEAST = 2.0**-120
 CODED = NZH * ROWS + TILE
-TOP = 32767.0
+TOP = 32700.0
 
 
 def triple_perm(i):
@@ -52,10 +53,11 @@
     scales = jnp.zeros((TILE, LANES), jnp.float32)
     for j, value in enumerate(blocks):
         size = jnp.abs(value)
-        most = jnp.maximum(jnp.max(size, axis=0, keepdims=True), 2.0**-120)
+        most = jnp.maximum(jnp.max(size, axis=0, keepdims=True), LEAST)
         e = jnp.ceil(4.0 / math.log(2.0) * jnp.log(most))
-        root = jnp.sqrt(size) * (TOP * jnp.exp(e * (-math.log(2.0) / 8)))
-        q = jnp.round(jnp.where(value < 0, -root, root))
+        root = size * lax.rsqrt(jnp.maximum(size, LEAST))
+        root = root * (TOP * jnp.exp(e * (-math.log(2.0) / 8))) + 0.5
+        q = jnp.where(value < 0, -root, root)
         put(slice(j * ROWS, (j + 1) * ROWS), q.astype(jnp.int32).astype(jnp.int16))
         scales = jnp.where(row == j, e, scales)
     put(slice(NZH * ROWS, CODED), scales.astype(jnp.int32).astype(jnp.int16))

time: 119 us -> 119 us (level)
  no operation moved by 1% of the time
where the time goes in v9:
time: 119 us
  starting transfers between devices  53.1 us (45%)
  waiting for transfers between devices  38.5 us (32%)
  blocking collectives  15.1 us (13%)
  Pallas kernels  8.66 us (7%)
  local copies, waits for them, and re-layouts  2.25 us (2%)
    ppermute x3, starting transfers between devices, body(): lax.ppermute(block, ('zh', 'y', 'core'), triple_perm(i))  20.9 us
    ppermute x4, starting transfers between devices, body(): lax.ppermute(ring[-1], ('y', 'core'), ring_perm((0, 1) if step < 3 else (...  19.6 us
    all_to_all x1, blocking collectives, exchange(): return lax.all_to_all(part, axes, split_axis=0, concat_axis=0, tiled=True)  13 us
    ppermute x1, waiting for transfers between devices, body(): total = lax.ppermute(total, ('x', 'zl', 'y', 'core'), place_perm())  12.7 us
    all_to_all x2, waiting for transfers between devices, exchange(): return lax.all_to_all(part, axes, split_axis=0, concat_axis=0, tiled=True)  12.2 us
    pallas_call x7, Pallas kernels, call(): pl.pallas_call(kernel, in_specs=specs, out_specs=pl.BlockSpec(memory_spac...  8.66 us
    all_to_all x2, starting transfers between devices, exchange(): return lax.all_to_all(part, axes, split_axis=0, concat_axis=0, tiled=True)  8.63 us
    ppermute x4, waiting for transfers between devices, body(): lax.ppermute(ring[-1], ('y', 'core'), ring_perm((0, 1) if step < 3 else (...  6.99 us
  transfers between devices with their start and end apart: 11, of which 5 were waited for; matrix products, arithmetic and copies ran while one was open for 0% of the time, Pallas kernels for 6%

profile of v9, /device:TPU:32, one launch (start us, length us, event | category | flops | bytes accessed | tf_op | source)
XLA Modules:
  0.0 118.5 jit_solution(17045469572208389992)
XLA Ops:
  0.0 0.7 compare_select_fusion
  0.7 0.2 copy-done
  1.0 2.0 %gather_fusion = bf16[704,128]{1,0:T(8,128)(2,1)S(1)} fusion(bf16[1024,128]{1,0:T(8,128)(2,1)S(1)} %copy-done, s32[1024]{0:T(1024)S(1)} %pad_clamp_fusion), kind=kCustom, calls=%fused_computation | custom fusion | bytes 363264 | tf_op jit(solution)/shard_map/gather | solution.py:154
  3.0 2.1 %all-gather = bf16[1408,128]{1,0:T(8,128)(2,1)S(1)} all-gather(bf16[704,128]{1,0:T(8,128)(2,1)S(1)} %gather_fusion), channel_id=2, replica_groups=mesh['x'=4,'zl'=4,'zh'=3,'y'=8,'core'=2] {'core'}, dimensions={0}, use_global_device_ids=true | all-gather | bytes 540672 | tf_op jit(solution)/shard_map/all_gather | solution.py:158
  5.1 2.6 %collective-permute-start.3 = (bf16[2,704,128]{2,1,0:T(8,128)(2,1)S(1)}, bf16[2,704,128]{2,1,0:T(8,128)(2,1)S(1)}, u32[]{:S(2)}, u32[]{:S(2)}) collective-permute-start(bf16[2,704,128]{2,1,0:T(8,128)(2,1)S(1)} %bitcast.5), channel_id=1, source_target_pairs={{0,2},{1,15},{2,4},{3,1},{4,6},{5,3},{6,8},{7,5},{8,10},{9,7},{10,... | collective-permute-start | bytes 1081352 | tf_op jit(solution)/shard_map/ppermute | solution.py:160
  7.6 16.6 %collective-permute-start = (bf16[704,128]{1,0:T(8,128)(2,1)S(1)}, bf16[704,128]{1,0:T(8,128)(2,1)S(1)}, u32[]{:S(2)}, u32[]{:S(2)}) collective-permute-start(bf16[704,128]{1,0:T(8,128)(2,1)S(1)} %gather_fusion), channel_id=1, source_target_pairs={{0,0},{33,1},{3,2},{18,3},{21,4},{36,5},{6,6},{39,7},{9,8},{24,9},... | collective-permute-start | bytes 540680 | tf_op jit(solution)/shard_map/ppermute | solution.py:162
  24.2 1.9 %collective-permute-start.1 = (bf16[704,128]{1,0:T(8,128)(2,1)S(1)}, bf16[704,128]{1,0:T(8,128)(2,1)S(1)}, u32[]{:S(2)}, u32[]{:S(2)}) collective-permute-start(bf16[704,128]{1,0:T(8,128)(2,1)S(1)} %gather_fusion), channel_id=1, source_target_pairs={{1,0},{34,1},{4,2},{19,3},{22,4},{37,5},{7,6},{40,7},{10,8},{25,9}... | collective-permute-start | bytes 540680 | tf_op jit(solution)/shard_map/ppermute | solution.py:162
  26.1 2.5 %collective-permute-start.2 = (bf16[704,128]{1,0:T(8,128)(2,1)S(1)}, bf16[704,128]{1,0:T(8,128)(2,1)S(1)}, u32[]{:S(2)}, u32[]{:S(2)}) collective-permute-start(bf16[704,128]{1,0:T(8,128)(2,1)S(1)} %gather_fusion), channel_id=1, source_target_pairs={{2,0},{35,1},{5,2},{20,3},{23,4},{38,5},{8,6},{41,7},{11,8},{26,9}... | collective-permute-start | bytes 540680 | tf_op jit(solution)/shard_map/ppermute | solution.py:162
  28.6 0.1 pad_add_fusion.at_ref
  28.7 0.0 collective-permute-done.3.a1_ref
  28.7 4.8 %collective-permute-start.4 = (bf16[2,704,128]{2,1,0:T(8,128)(2,1)S(1)}, bf16[2,704,128]{2,1,0:T(8,128)(2,1)S(1)}, u32[]{:S(2)}, u32[]{:S(2)}) collective-permute-start(bf16[2,704,128]{2,1,0:T(8,128)(2,1)S(1)} %collective-permute-done.3.a1_ref), channel_id=1, source_target_pairs={{0,2},{1,15},{2,4},{3,1},{4,6},{5,3},{6,8},{7,5},{8,10},{9,7},{10,... | collective-permute-start | bytes 1081352 | tf_op jit(solution)/shard_map/ppermute | solution.py:160
  33.5 6.6 %collective-permute-done.refs_0_ = bf16[704,128]{1,0:T(8,128)(2,1)S(1)} collective-permute-done((bf16[704,128]{1,0:T(8,128)(2,1)S(1)}, bf16[704,128]{1,0:T(8,128)(2,1)S(1)}, u32[]{:S(2)}, u32[]{:S(2)}) %collective-permute-start) | collective-permute-done | bytes 180256 | tf_op jit(solution)/shard_map/ppermute | solution.py:162
  40.1 0.0 collective-permute-done.1.refs_1_
  40.1 0.6 shard_map.37.mine_ref
  40.8 1.9 %collective-permute-start.7 = (bf16[704,384]{1,0:T(8,128)(2,1)S(1)}, bf16[704,384]{1,0:T(8,128)(2,1)S(1)}, u32[]{:S(2)}, u32[]{:S(2)}) collective-permute-start(bf16[704,384]{1,0:T(8,128)(2,1)S(1)} %shard_map.37.mine_ref), channel_id=1, source_target_pairs={{0,1},{1,0},{2,3},{3,2},{4,5},{5,4},{6,7},{7,6},{8,9},{9,8},{10,11... | collective-permute-start | bytes 1622024 | tf_op jit(solution)/shard_map/ppermute | solution.py:165
  42.7 8.7 %collective-permute-start.5 = (bf16[2,704,128]{2,1,0:T(8,128)(2,1)S(1)}, bf16[2,704,128]{2,1,0:T(8,128)(2,1)S(1)}, u32[]{:S(2)}, u32[]{:S(2)}) collective-permute-start(bf16[2,704,128]{2,1,0:T(8,128)(2,1)S(1)} %collective-permute-done.4.a0_ref.a2_ref), channel_id=1, source_target_pairs={{0,2},{1,15},{2,4},{3,1},{4,6},{5,3},{6,8},{7,5},{8,10},{9,7},{10,... | collective-permute-start | bytes 1081352 | tf_op jit(solution)/shard_map/ppermute | solution.py:160
  51.4 0.0 collective-permute-done.7.other_ref
  51.4 3.0 %shard_map.39 = s16[4,2,400,128]{3,2,1,0:T(8,128)(2,1)} custom-call(s32[2]{0:T(128)S(1)} %pad_add_fusion.at_ref, bf16[2,704,128]{2,1,0:T(8,128)(2,1)S(1)} %bitcast.6, bf16[2,704,128]{2,1,0:T(8,128)(2,1)S(1)} %collective-permute-done.3.a1_ref, bf16[2,704,128]{2,1,0:T(8,128)(2,1)S(1)} %collective-permute-done.4.a0_ref.a2_ref, ...), custom_call_target="tpu_custom_call" | custom-call | flops 553648128 | bytes 2000000 | tf_op jit(solution)/shard_map/pallas_call | solution.py:139
  54.4 4.3 %all-to-all-start.1 = ((s16[8,400,128]{2,1,0:T(8,128)(2,1)}), s16[8,400,128]{2,1,0:T(8,128)(2,1)S(1)}, u32[]{:S(2)}, u32[]{:S(2)}) async-start(s16[8,400,128]{2,1,0:T(8,128)(2,1)} %bitcast.4), calls=%async_computation.1 | async-start | bytes 1638400 | tf_op jit(solution)/shard_map/all_to_all | solution.py:150
  58.7 3.5 %collective-permute-start.6 = (bf16[2,704,128]{2,1,0:T(8,128)(2,1)S(1)}, bf16[2,704,128]{2,1,0:T(8,128)(2,1)S(1)}, u32[]{:S(2)}, u32[]{:S(2)}) collective-permute-start(bf16[2,704,128]{2,1,0:T(8,128)(2,1)S(1)} %collective-permute-done.5.a1_ref), channel_id=1, source_target_pairs={{0,2},{2,4},{4,6},{6,8},{8,10},{10,12},{12,14},{14,0},{16,18},{18,... | collective-permute-start | bytes 1081352 | tf_op jit(solution)/shard_map/ppermute | solution.py:160
  62.3 7.0 %collective-permute-done.6.a2_ref = bf16[2,704,128]{2,1,0:T(8,128)(2,1)S(1)} collective-permute-done((bf16[2,704,128]{2,1,0:T(8,128)(2,1)S(1)}, bf16[2,704,128]{2,1,0:T(8,128)(2,1)S(1)}, u32[]{:S(2)}, u32[]{:S(2)}) %collective-permute-start.6) | collective-permute-done | bytes 360480 | tf_op jit(solution)/shard_map/ppermute | solution.py:160
  69.2 3.0 %shard_map.38 = s16[4,2,400,128]{3,2,1,0:T(8,128)(2,1)} custom-call(s32[2]{0:T(128)S(1)} %pad_add_fusion.at_ref, bf16[2,704,128]{2,1,0:T(8,128)(2,1)S(1)} %collective-permute-done.4.a0_ref.a2_ref, bf16[2,704,128]{2,1,0:T(8,128)(2,1)S(1)} %collective-permute-done.5.a1_ref, bf16[2,704,128]{2,1,0:T(8,128)(2,1)S(1)} %collective-permute-done.6.a2_ref, ...), custom_call_target="tpu_custom_call" | custom-call | flops 553648128 | bytes 2000000 | tf_op jit(solution)/shard_map/pallas_call | solution.py:139
  72.2 0.5 all-to-all-done.1.part_ref
  72.7 4.3 %all-to-all-start = ((s16[8,400,128]{2,1,0:T(8,128)(2,1)}), s16[8,400,128]{2,1,0:T(8,128)(2,1)S(1)}, u32[]{:S(2)}, u32[]{:S(2)}) async-start(s16[8,400,128]{2,1,0:T(8,128)(2,1)} %bitcast.3), calls=%async_computation | async-start | bytes 1638400 | tf_op jit(solution)/shard_map/all_to_all | solution.py:150
  77.0 0.5 shard_map.40.refs_0_
  77.6 11.7 %all-to-all-done.part_ref = s16[8,400,128]{2,1,0:T(8,128)(2,1)S(1)} async-done(((s16[8,400,128]{2,1,0:T(8,128)(2,1)}), s16[8,400,128]{2,1,0:T(8,128)(2,1)S(1)}, u32[]{:S(2)}, u32[]{:S(2)}) %all-to-all-start) | async-done | bytes 819232 | tf_op jit(solution)/shard_map/all_to_all | solution.py:150
  89.2 0.5 shard_map.41
  89.8 13.0 %all_to_all.15.part_ref = s16[4,400,128]{2,1,0:T(8,128)(2,1)S(1)} all-to-all(s16[4,400,128]{2,1,0:T(8,128)(2,1)S(1)} %shard_map.41), channel_id=1, replica_groups=mesh['x'=4,'zl'=4,'zh'=3,'y'=8,'core'=2] {'zl'}, dimensions={0} | all-to-all | bytes 819200 | tf_op jit(solution)/shard_map/all_to_all | solution.py:150
  102.8 0.3 shard_map.42
  103.1 1.9 %collective-permute-start.8 = (s16[400,128]{1,0:T(8,128)(2,1)S(1)}, s16[400,128]{1,0:T(8,128)(2,1)S(1)}, u32[]{:S(2)}, u32[]{:S(2)}) collective-permute-start(s16[400,128]{1,0:T(8,128)(2,1)S(1)} %shard_map.42), channel_id=1, source_target_pairs={{0,14},{1,0},{2,48},{3,50},{4,338},{5,340},{6,100},{7,102},{8,150}... | collective-permute-start | bytes 307208 | tf_op jit(solution)/shard_map/ppermute | solution.py:176
  105.0 12.7 %collective-permute-done.8.total_ref = s16[400,128]{1,0:T(8,128)(2,1)S(1)} collective-permute-done((s16[400,128]{1,0:T(8,128)(2,1)S(1)}, s16[400,128]{1,0:T(8,128)(2,1)S(1)}, u32[]{:S(2)}, u32[]{:S(2)}) %collective-permute-start.8) | collective-permute-done | bytes 102432 | tf_op jit(solution)/shard_map/ppermute | solution.py:176
  117.8 0.7 shard_map.43
  (7 shorter events, 0.0 us)
Async XLA Ops:
  0.0 1.0 copy-start
  5.1 23.6 %collective-permute-start.3 = (bf16[2,704,128]{2,1,0:T(8,128)(2,1)S(1)}, bf16[2,704,128]{2,1,0:T(8,128)(2,1)S(1)}, u32[]{:S(2)}, u32[]{:S(2)}) collective-permute-start(bf16[2,704,128]{2,1,0:T(8,128)(2,1)S(1)} %bitcast.5), channel_id=1, source_target_pairs={{0,2},{1,15},{2,4},{3,1},{4,6},{5,3},{6,8},{7,5},{8,10},{9,7},{10,... | collective-permute-start | bytes 1081352 | tf_op jit(solution)/shard_map/ppermute | solution.py:160
  7.6 32.5 %collective-permute-start = (bf16[704,128]{1,0:T(8,128)(2,1)S(1)}, bf16[704,128]{1,0:T(8,128)(2,1)S(1)}, u32[]{:S(2)}, u32[]{:S(2)}) collective-permute-start(bf16[704,128]{1,0:T(8,128)(2,1)S(1)} %gather_fusion), channel_id=1, source_target_pairs={{0,0},{33,1},{3,2},{18,3},{21,4},{36,5},{6,6},{39,7},{9,8},{24,9},... | collective-permute-start | bytes 540680 | tf_op jit(solution)/shard_map/ppermute | solution.py:162
  24.2 15.9 %collective-permute-start.1 = (bf16[704,128]{1,0:T(8,128)(2,1)S(1)}, bf16[704,128]{1,0:T(8,128)(2,1)S(1)}, u32[]{:S(2)}, u32[]{:S(2)}) collective-permute-start(bf16[704,128]{1,0:T(8,128)(2,1)S(1)} %gather_fusion), channel_id=1, source_target_pairs={{1,0},{34,1},{4,2},{19,3},{22,4},{37,5},{7,6},{40,7},{10,8},{25,9}... | collective-permute-start | bytes 540680 | tf_op jit(solution)/shard_map/ppermute | solution.py:162
  26.1 14.0 %collective-permute-start.2 = (bf16[704,128]{1,0:T(8,128)(2,1)S(1)}, bf16[704,128]{1,0:T(8,128)(2,1)S(1)}, u32[]{:S(2)}, u32[]{:S(2)}) collective-permute-start(bf16[704,128]{1,0:T(8,128)(2,1)S(1)} %gather_fusion), channel_id=1, source_target_pairs={{2,0},{35,1},{5,2},{20,3},{23,4},{38,5},{8,6},{41,7},{11,8},{26,9}... | collective-permute-start | bytes 540680 | tf_op jit(solution)/shard_map/ppermute | solution.py:162
  28.7 12.1 %collective-permute-start.4 = (bf16[2,704,128]{2,1,0:T(8,128)(2,1)S(1)}, bf16[2,704,128]{2,1,0:T(8,128)(2,1)S(1)}, u32[]{:S(2)}, u32[]{:S(2)}) collective-permute-start(bf16[2,704,128]{2,1,0:T(8,128)(2,1)S(1)} %collective-permute-done.3.a1_ref), channel_id=1, source_target_pairs={{0,2},{1,15},{2,4},{3,1},{4,6},{5,3},{6,8},{7,5},{8,10},{9,7},{10,... | collective-permute-start | bytes 1081352 | tf_op jit(solution)/shard_map/ppermute | solution.py:160
  40.8 10.7 %collective-permute-start.7 = (bf16[704,384]{1,0:T(8,128)(2,1)S(1)}, bf16[704,384]{1,0:T(8,128)(2,1)S(1)}, u32[]{:S(2)}, u32[]{:S(2)}) collective-permute-start(bf16[704,384]{1,0:T(8,128)(2,1)S(1)} %shard_map.37.mine_ref), channel_id=1, source_target_pairs={{0,1},{1,0},{2,3},{3,2},{4,5},{5,4},{6,7},{7,6},{8,9},{9,8},{10,11... | collective-permute-start | bytes 1622024 | tf_op jit(solution)/shard_map/ppermute | solution.py:165
  42.7 16.0 %collective-permute-start.5 = (bf16[2,704,128]{2,1,0:T(8,128)(2,1)S(1)}, bf16[2,704,128]{2,1,0:T(8,128)(2,1)S(1)}, u32[]{:S(2)}, u32[]{:S(2)}) collective-permute-start(bf16[2,704,128]{2,1,0:T(8,128)(2,1)S(1)} %collective-permute-done.4.a0_ref.a2_ref), channel_id=1, source_target_pairs={{0,2},{1,15},{2,4},{3,1},{4,6},{5,3},{6,8},{7,5},{8,10},{9,7},{10,... | collective-permute-start | bytes 1081352 | tf_op jit(solution)/shard_map/ppermute | solution.py:160
  54.4 18.2 %all-to-all-start.1 = ((s16[8,400,128]{2,1,0:T(8,128)(2,1)}), s16[8,400,128]{2,1,0:T(8,128)(2,1)S(1)}, u32[]{:S(2)}, u32[]{:S(2)}) async-start(s16[8,400,128]{2,1,0:T(8,128)(2,1)} %bitcast.4), calls=%async_computation.1 | async-start | bytes 1638400 | tf_op jit(solution)/shard_map/all_to_all | solution.py:150
  58.7 10.5 %collective-permute-start.6 = (bf16[2,704,128]{2,1,0:T(8,128)(2,1)S(1)}, bf16[2,704,128]{2,1,0:T(8,128)(2,1)S(1)}, u32[]{:S(2)}, u32[]{:S(2)}) collective-permute-start(bf16[2,704,128]{2,1,0:T(8,128)(2,1)S(1)} %collective-permute-done.5.a1_ref), channel_id=1, source_target_pairs={{0,2},{2,4},{4,6},{6,8},{8,10},{10,12},{12,14},{14,0},{16,18},{18,... | collective-permute-start | bytes 1081352 | tf_op jit(solution)/shard_map/ppermute | solution.py:160
  72.7 16.6 %all-to-all-start = ((s16[8,400,128]{2,1,0:T(8,128)(2,1)}), s16[8,400,128]{2,1,0:T(8,128)(2,1)S(1)}, u32[]{:S(2)}, u32[]{:S(2)}) async-start(s16[8,400,128]{2,1,0:T(8,128)(2,1)} %bitcast.3), calls=%async_computation | async-start | bytes 1638400 | tf_op jit(solution)/shard_map/all_to_all | solution.py:150
  102.8 14.9 %copy-start.1 = (f32[128,384]{1,0:T(8,128)S(1)}, f32[128,384]{1,0:T(8,128)}, u32[]{:S(2)}) copy-start(f32[128,384]{1,0:T(8,128)} %old_ref.1) | copy-start | bytes 589828
  103.1 14.7 %collective-permute-start.8 = (s16[400,128]{1,0:T(8,128)(2,1)S(1)}, s16[400,128]{1,0:T(8,128)(2,1)S(1)}, u32[]{:S(2)}, u32[]{:S(2)}) collective-permute-start(s16[400,128]{1,0:T(8,128)(2,1)S(1)} %shard_map.42), channel_id=1, source_target_pairs={{0,14},{1,0},{2,48},{3,50},{4,338},{5,340},{6,100},{7,102},{8,150}... | collective-permute-start | bytes 307208 | tf_op jit(solution)/shard_map/ppermute | solution.py:176

commit v10 on v9

--- a/solution.py
+++ b/solution.py
@@ -11,7 +11,7 @@
 
 NX, NZL, NZH, NY, NC = 4, 4, 3, 8, 2
 AXES = ("x", "zl", "zh", "y", "core")
-TRIPLE = ((0, 11), (1, 6), (7, 12), (2, 13), (3, 8), (9, 14), (4, 15), (5, 10))
+TRIPLE = ((0, 11), (1, 6), (7, 12), (2, 13), (3, 8), (9, 14), (4, 10), (5, 15))
 OFFSET = (((-1, -2), (-3, -4)), ((0, 1), (2, 3)))
 LANES = 128
 ROWS = 128

time: 119 us -> 120 us (level)
  the two profiles are of different devices: /device:TPU:32 before, /device:TPU:62 now
where the time goes in v10:
time: 120 us; the launch traced here: 119 us
  starting transfers between devices  53.9 us (45%)
  waiting for transfers between devices  33.7 us (28%)
  blocking collectives  19.5 us (16%)
  Pallas kernels  8.66 us (7%)
  local copies, waits for them, and re-layouts  2.25 us (2%)
    ppermute x3, starting transfers between devices, body(): lax.ppermute(block, ('zh', 'y', 'core'), triple_perm(i))  21.9 us
    ppermute x4, starting transfers between devices, body(): lax.ppermute(ring[-1], ('y', 'core'), ring_perm((0, 1) if step < 3 else (...  18.6 us
    all_to_all x1, blocking collectives, exchange(): return lax.all_to_all(part, axes, split_axis=0, concat_axis=0, tiled=True)  17.4 us
    ppermute x1, waiting for transfers between devices, body(): total = lax.ppermute(total, ('x', 'zl', 'y', 'core'), place_perm())  12.4 us
    all_to_all x2, starting transfers between devices, exchange(): return lax.all_to_all(part, axes, split_axis=0, concat_axis=0, tiled=True)  9.6 us
    pallas_call x7, Pallas kernels, call(): pl.pallas_call(kernel, in_specs=specs, out_specs=pl.BlockSpec(memory_spac...  8.66 us
    ppermute x3, waiting for transfers between devices, body(): lax.ppermute(block, ('zh', 'y', 'core'), triple_perm(i))  7.64 us
    all_to_all x2, waiting for transfers between devices, exchange(): return lax.all_to_all(part, axes, split_axis=0, concat_axis=0, tiled=True)  7.07 us
  transfers between devices with their start and end apart: 11, of which 6 were waited for; matrix products, arithmetic and copies ran while one was open for 0% of the time, Pallas kernels for 6%

profile of v10, /device:TPU:62, one launch (start us, length us, event | category | flops | bytes accessed | tf_op | source)
XLA Modules:
  0.0 119.0 jit_solution(7125200804454047357)
XLA Ops:
  0.0 0.7 compare_select_fusion
  0.7 0.2 copy-done
  1.0 2.0 %gather_fusion = bf16[704,128]{1,0:T(8,128)(2,1)S(1)} fusion(bf16[1024,128]{1,0:T(8,128)(2,1)S(1)} %copy-done, s32[1024]{0:T(1024)S(1)} %pad_clamp_fusion), kind=kCustom, calls=%fused_computation | custom fusion | bytes 363264 | tf_op jit(solution)/shard_map/gather | solution.py:154
  3.0 2.1 %all-gather = bf16[1408,128]{1,0:T(8,128)(2,1)S(1)} all-gather(bf16[704,128]{1,0:T(8,128)(2,1)S(1)} %gather_fusion), channel_id=2, replica_groups=mesh['x'=4,'zl'=4,'zh'=3,'y'=8,'core'=2] {'core'}, dimensions={0}, use_global_device_ids=true | all-gather | bytes 540672 | tf_op jit(solution)/shard_map/all_gather | solution.py:158
  5.1 1.9 %collective-permute-start.3 = (bf16[2,704,128]{2,1,0:T(8,128)(2,1)S(1)}, bf16[2,704,128]{2,1,0:T(8,128)(2,1)S(1)}, u32[]{:S(2)}, u32[]{:S(2)}) collective-permute-start(bf16[2,704,128]{2,1,0:T(8,128)(2,1)S(1)} %bitcast.5), channel_id=1, source_target_pairs={{0,2},{1,15},{2,4},{3,1},{4,6},{5,3},{6,8},{7,5},{8,10},{9,7},{10,... | collective-permute-start | bytes 1081352 | tf_op jit(solution)/shard_map/ppermute | solution.py:160
  7.0 16.0 %collective-permute-start = (bf16[704,128]{1,0:T(8,128)(2,1)S(1)}, bf16[704,128]{1,0:T(8,128)(2,1)S(1)}, u32[]{:S(2)}, u32[]{:S(2)}) collective-permute-start(bf16[704,128]{1,0:T(8,128)(2,1)S(1)} %gather_fusion), channel_id=1, source_target_pairs={{0,0},{33,1},{3,2},{18,3},{21,4},{36,5},{6,6},{39,7},{9,8},{24,9},... | collective-permute-start | bytes 540680 | tf_op jit(solution)/shard_map/ppermute | solution.py:162
  23.0 1.9 %collective-permute-start.1 = (bf16[704,128]{1,0:T(8,128)(2,1)S(1)}, bf16[704,128]{1,0:T(8,128)(2,1)S(1)}, u32[]{:S(2)}, u32[]{:S(2)}) collective-permute-start(bf16[704,128]{1,0:T(8,128)(2,1)S(1)} %gather_fusion), channel_id=1, source_target_pairs={{1,0},{34,1},{4,2},{19,3},{22,4},{37,5},{7,6},{40,7},{10,8},{25,9}... | collective-permute-start | bytes 540680 | tf_op jit(solution)/shard_map/ppermute | solution.py:162
  24.9 3.9 %collective-permute-start.2 = (bf16[704,128]{1,0:T(8,128)(2,1)S(1)}, bf16[704,128]{1,0:T(8,128)(2,1)S(1)}, u32[]{:S(2)}, u32[]{:S(2)}) collective-permute-start(bf16[704,128]{1,0:T(8,128)(2,1)S(1)} %gather_fusion), channel_id=1, source_target_pairs={{2,0},{35,1},{5,2},{20,3},{23,4},{38,5},{8,6},{41,7},{11,8},{26,9}... | collective-permute-start | bytes 540680 | tf_op jit(solution)/shard_map/ppermute | solution.py:162
  28.9 0.1 pad_add_fusion.at_ref
  29.0 0.0 collective-permute-done.3.a1_ref
  29.0 8.5 %collective-permute-start.4 = (bf16[2,704,128]{2,1,0:T(8,128)(2,1)S(1)}, bf16[2,704,128]{2,1,0:T(8,128)(2,1)S(1)}, u32[]{:S(2)}, u32[]{:S(2)}) collective-permute-start(bf16[2,704,128]{2,1,0:T(8,128)(2,1)S(1)} %collective-permute-done.3.a1_ref), channel_id=1, source_target_pairs={{0,2},{1,15},{2,4},{3,1},{4,6},{5,3},{6,8},{7,5},{8,10},{9,7},{10,... | collective-permute-start | bytes 1081352 | tf_op jit(solution)/shard_map/ppermute | solution.py:160
  37.4 2.0 %collective-permute-done.refs_0_ = bf16[704,128]{1,0:T(8,128)(2,1)S(1)} collective-permute-done((bf16[704,128]{1,0:T(8,128)(2,1)S(1)}, bf16[704,128]{1,0:T(8,128)(2,1)S(1)}, u32[]{:S(2)}, u32[]{:S(2)}) %collective-permute-start) | collective-permute-done | bytes 180256 | tf_op jit(solution)/shard_map/ppermute | solution.py:162
  39.4 3.3 %collective-permute-done.1.refs_1_ = bf16[704,128]{1,0:T(8,128)(2,1)S(1)} collective-permute-done((bf16[704,128]{1,0:T(8,128)(2,1)S(1)}, bf16[704,128]{1,0:T(8,128)(2,1)S(1)}, u32[]{:S(2)}, u32[]{:S(2)}) %collective-permute-start.1) | collective-permute-done | bytes 180256 | tf_op jit(solution)/shard_map/ppermute | solution.py:162
  42.7 2.3 %collective-permute-done.2.refs_2_ = bf16[704,128]{1,0:T(8,128)(2,1)S(1)} collective-permute-done((bf16[704,128]{1,0:T(8,128)(2,1)S(1)}, bf16[704,128]{1,0:T(8,128)(2,1)S(1)}, u32[]{:S(2)}, u32[]{:S(2)}) %collective-permute-start.2) | collective-permute-done | bytes 180256 | tf_op jit(solution)/shard_map/ppermute | solution.py:162
  45.1 0.6 shard_map.37.mine_ref
  45.7 0.0 collective-permute-done.4.a0_ref.a2_ref
  45.7 1.9 %collective-permute-start.7 = (bf16[704,384]{1,0:T(8,128)(2,1)S(1)}, bf16[704,384]{1,0:T(8,128)(2,1)S(1)}, u32[]{:S(2)}, u32[]{:S(2)}) collective-permute-start(bf16[704,384]{1,0:T(8,128)(2,1)S(1)} %shard_map.37.mine_ref), channel_id=1, source_target_pairs={{0,1},{1,0},{2,3},{3,2},{4,5},{5,4},{6,7},{7,6},{8,9},{9,8},{10,11... | collective-permute-start | bytes 1622024 | tf_op jit(solution)/shard_map/ppermute | solution.py:165
  47.6 5.5 %collective-permute-start.5 = (bf16[2,704,128]{2,1,0:T(8,128)(2,1)S(1)}, bf16[2,704,128]{2,1,0:T(8,128)(2,1)S(1)}, u32[]{:S(2)}, u32[]{:S(2)}) collective-permute-start(bf16[2,704,128]{2,1,0:T(8,128)(2,1)S(1)} %collective-permute-done.4.a0_ref.a2_ref), channel_id=1, source_target_pairs={{0,2},{1,15},{2,4},{3,1},{4,6},{5,3},{6,8},{7,5},{8,10},{9,7},{10,... | collective-permute-start | bytes 1081352 | tf_op jit(solution)/shard_map/ppermute | solution.py:160
  53.1 3.0 %shard_map.39 = s16[4,2,400,128]{3,2,1,0:T(8,128)(2,1)} custom-call(s32[2]{0:T(128)S(1)} %pad_add_fusion.at_ref, bf16[2,704,128]{2,1,0:T(8,128)(2,1)S(1)} %bitcast.6, bf16[2,704,128]{2,1,0:T(8,128)(2,1)S(1)} %collective-permute-done.3.a1_ref, bf16[2,704,128]{2,1,0:T(8,128)(2,1)S(1)} %collective-permute-done.4.a0_ref.a2_ref, ...), custom_call_target="tpu_custom_call" | custom-call | flops 553648128 | bytes 2000000 | tf_op jit(solution)/shard_map/pallas_call | solution.py:139
  56.1 4.8 %all-to-all-start.1 = ((s16[8,400,128]{2,1,0:T(8,128)(2,1)}), s16[8,400,128]{2,1,0:T(8,128)(2,1)S(1)}, u32[]{:S(2)}, u32[]{:S(2)}) async-start(s16[8,400,128]{2,1,0:T(8,128)(2,1)} %bitcast.4), calls=%async_computation.1 | async-start | bytes 1638400 | tf_op jit(solution)/shard_map/all_to_all | solution.py:150
  60.9 2.7 %collective-permute-start.6 = (bf16[2,704,128]{2,1,0:T(8,128)(2,1)S(1)}, bf16[2,704,128]{2,1,0:T(8,128)(2,1)S(1)}, u32[]{:S(2)}, u32[]{:S(2)}) collective-permute-start(bf16[2,704,128]{2,1,0:T(8,128)(2,1)S(1)} %collective-permute-done.5.a1_ref), channel_id=1, source_target_pairs={{0,2},{2,4},{4,6},{6,8},{8,10},{10,12},{12,14},{14,0},{16,18},{18,... | collective-permute-start | bytes 1081352 | tf_op jit(solution)/shard_map/ppermute | solution.py:160
  63.6 6.6 %collective-permute-done.6.a2_ref = bf16[2,704,128]{2,1,0:T(8,128)(2,1)S(1)} collective-permute-done((bf16[2,704,128]{2,1,0:T(8,128)(2,1)S(1)}, bf16[2,704,128]{2,1,0:T(8,128)(2,1)S(1)}, u32[]{:S(2)}, u32[]{:S(2)}) %collective-permute-start.6) | collective-permute-done | bytes 360480 | tf_op jit(solution)/shard_map/ppermute | solution.py:160
  70.2 3.0 %shard_map.38 = s16[4,2,400,128]{3,2,1,0:T(8,128)(2,1)} custom-call(s32[2]{0:T(128)S(1)} %pad_add_fusion.at_ref, bf16[2,704,128]{2,1,0:T(8,128)(2,1)S(1)} %collective-permute-done.4.a0_ref.a2_ref, bf16[2,704,128]{2,1,0:T(8,128)(2,1)S(1)} %collective-permute-done.5.a1_ref, bf16[2,704,128]{2,1,0:T(8,128)(2,1)S(1)} %collective-permute-done.6.a2_ref, ...), custom_call_target="tpu_custom_call" | custom-call | flops 553648128 | bytes 2000000 | tf_op jit(solution)/shard_map/pallas_call | solution.py:139
  73.2 4.8 %all-to-all-start = ((s16[8,400,128]{2,1,0:T(8,128)(2,1)}), s16[8,400,128]{2,1,0:T(8,128)(2,1)S(1)}, u32[]{:S(2)}, u32[]{:S(2)}) async-start(s16[8,400,128]{2,1,0:T(8,128)(2,1)} %bitcast.3), calls=%async_computation | async-start | bytes 1638400 | tf_op jit(solution)/shard_map/all_to_all | solution.py:150
  78.0 0.5 shard_map.40.refs_0_
  78.5 7.1 %all-to-all-done.part_ref = s16[8,400,128]{2,1,0:T(8,128)(2,1)S(1)} async-done(((s16[8,400,128]{2,1,0:T(8,128)(2,1)}), s16[8,400,128]{2,1,0:T(8,128)(2,1)S(1)}, u32[]{:S(2)}, u32[]{:S(2)}) %all-to-all-start) | async-done | bytes 819232 | tf_op jit(solution)/shard_map/all_to_all | solution.py:150
  85.6 0.5 shard_map.41
  86.2 17.4 %all_to_all.15.part_ref = s16[4,400,128]{2,1,0:T(8,128)(2,1)S(1)} all-to-all(s16[4,400,128]{2,1,0:T(8,128)(2,1)S(1)} %shard_map.41), channel_id=1, replica_groups=mesh['x'=4,'zl'=4,'zh'=3,'y'=8,'core'=2] {'zl'}, dimensions={0} | all-to-all | bytes 819200 | tf_op jit(solution)/shard_map/all_to_all | solution.py:150
  103.6 0.3 shard_map.42
  103.9 1.9 %collective-permute-start.8 = (s16[400,128]{1,0:T(8,128)(2,1)S(1)}, s16[400,128]{1,0:T(8,128)(2,1)S(1)}, u32[]{:S(2)}, u32[]{:S(2)}) collective-permute-start(s16[400,128]{1,0:T(8,128)(2,1)S(1)} %shard_map.42), channel_id=1, source_target_pairs={{0,14},{1,0},{2,48},{3,50},{4,338},{5,340},{6,100},{7,102},{8,150}... | collective-permute-start | bytes 307208 | tf_op jit(solution)/shard_map/ppermute | solution.py:176
  105.8 12.4 %collective-permute-done.8.total_ref = s16[400,128]{1,0:T(8,128)(2,1)S(1)} collective-permute-done((s16[400,128]{1,0:T(8,128)(2,1)S(1)}, s16[400,128]{1,0:T(8,128)(2,1)S(1)}, u32[]{:S(2)}, u32[]{:S(2)}) %collective-permute-start.8) | collective-permute-done | bytes 102432 | tf_op jit(solution)/shard_map/ppermute | solution.py:176
  118.3 0.7 shard_map.43
  (7 shorter events, 0.0 us)
Async XLA Ops:
  0.0 1.0 copy-start
  5.1 23.9 %collective-permute-start.3 = (bf16[2,704,128]{2,1,0:T(8,128)(2,1)S(1)}, bf16[2,704,128]{2,1,0:T(8,128)(2,1)S(1)}, u32[]{:S(2)}, u32[]{:S(2)}) collective-permute-start(bf16[2,704,128]{2,1,0:T(8,128)(2,1)S(1)} %bitcast.5), channel_id=1, source_target_pairs={{0,2},{1,15},{2,4},{3,1},{4,6},{5,3},{6,8},{7,5},{8,10},{9,7},{10,... | collective-permute-start | bytes 1081352 | tf_op jit(solution)/shard_map/ppermute | solution.py:160
  7.0 32.4 %collective-permute-start = (bf16[704,128]{1,0:T(8,128)(2,1)S(1)}, bf16[704,128]{1,0:T(8,128)(2,1)S(1)}, u32[]{:S(2)}, u32[]{:S(2)}) collective-permute-start(bf16[704,128]{1,0:T(8,128)(2,1)S(1)} %gather_fusion), channel_id=1, source_target_pairs={{0,0},{33,1},{3,2},{18,3},{21,4},{36,5},{6,6},{39,7},{9,8},{24,9},... | collective-permute-start | bytes 540680 | tf_op jit(solution)/shard_map/ppermute | solution.py:162
  23.0 19.7 %collective-permute-start.1 = (bf16[704,128]{1,0:T(8,128)(2,1)S(1)}, bf16[704,128]{1,0:T(8,128)(2,1)S(1)}, u32[]{:S(2)}, u32[]{:S(2)}) collective-permute-start(bf16[704,128]{1,0:T(8,128)(2,1)S(1)} %gather_fusion), channel_id=1, source_target_pairs={{1,0},{34,1},{4,2},{19,3},{22,4},{37,5},{7,6},{40,7},{10,8},{25,9}... | collective-permute-start | bytes 540680 | tf_op jit(solution)/shard_map/ppermute | solution.py:162
  24.9 20.1 %collective-permute-start.2 = (bf16[704,128]{1,0:T(8,128)(2,1)S(1)}, bf16[704,128]{1,0:T(8,128)(2,1)S(1)}, u32[]{:S(2)}, u32[]{:S(2)}) collective-permute-start(bf16[704,128]{1,0:T(8,128)(2,1)S(1)} %gather_fusion), channel_id=1, source_target_pairs={{2,0},{35,1},{5,2},{20,3},{23,4},{38,5},{8,6},{41,7},{11,8},{26,9}... | collective-permute-start | bytes 540680 | tf_op jit(solution)/shard_map/ppermute | solution.py:162
  29.0 16.7 %collective-permute-start.4 = (bf16[2,704,128]{2,1,0:T(8,128)(2,1)S(1)}, bf16[2,704,128]{2,1,0:T(8,128)(2,1)S(1)}, u32[]{:S(2)}, u32[]{:S(2)}) collective-permute-start(bf16[2,704,128]{2,1,0:T(8,128)(2,1)S(1)} %collective-permute-done.3.a1_ref), channel_id=1, source_target_pairs={{0,2},{1,15},{2,4},{3,1},{4,6},{5,3},{6,8},{7,5},{8,10},{9,7},{10,... | collective-permute-start | bytes 1081352 | tf_op jit(solution)/shard_map/ppermute | solution.py:160
  45.7 7.4 %collective-permute-start.7 = (bf16[704,384]{1,0:T(8,128)(2,1)S(1)}, bf16[704,384]{1,0:T(8,128)(2,1)S(1)}, u32[]{:S(2)}, u32[]{:S(2)}) collective-permute-start(bf16[704,384]{1,0:T(8,128)(2,1)S(1)} %shard_map.37.mine_ref), channel_id=1, source_target_pairs={{0,1},{1,0},{2,3},{3,2},{4,5},{5,4},{6,7},{7,6},{8,9},{9,8},{10,11... | collective-permute-start | bytes 1622024 | tf_op jit(solution)/shard_map/ppermute | solution.py:165
  47.6 13.3 %collective-permute-start.5 = (bf16[2,704,128]{2,1,0:T(8,128)(2,1)S(1)}, bf16[2,704,128]{2,1,0:T(8,128)(2,1)S(1)}, u32[]{:S(2)}, u32[]{:S(2)}) collective-permute-start(bf16[2,704,128]{2,1,0:T(8,128)(2,1)S(1)} %collective-permute-done.4.a0_ref.a2_ref), channel_id=1, source_target_pairs={{0,2},{1,15},{2,4},{3,1},{4,6},{5,3},{6,8},{7,5},{8,10},{9,7},{10,... | collective-permute-start | bytes 1081352 | tf_op jit(solution)/shard_map/ppermute | solution.py:160
  56.1 17.1 %all-to-all-start.1 = ((s16[8,400,128]{2,1,0:T(8,128)(2,1)}), s16[8,400,128]{2,1,0:T(8,128)(2,1)S(1)}, u32[]{:S(2)}, u32[]{:S(2)}) async-start(s16[8,400,128]{2,1,0:T(8,128)(2,1)} %bitcast.4), calls=%async_computation.1 | async-start | bytes 1638400 | tf_op jit(solution)/shard_map/all_to_all | solution.py:150
  60.9 9.3 %collective-permute-start.6 = (bf16[2,704,128]{2,1,0:T(8,128)(2,1)S(1)}, bf16[2,704,128]{2,1,0:T(8,128)(2,1)S(1)}, u32[]{:S(2)}, u32[]{:S(2)}) collective-permute-start(bf16[2,704,128]{2,1,0:T(8,128)(2,1)S(1)} %collective-permute-done.5.a1_ref), channel_id=1, source_target_pairs={{0,2},{2,4},{4,6},{6,8},{8,10},{10,12},{12,14},{14,0},{16,18},{18,... | collective-permute-start | bytes 1081352 | tf_op jit(solution)/shard_map/ppermute | solution.py:160
  73.2 12.4 %all-to-all-start = ((s16[8,400,128]{2,1,0:T(8,128)(2,1)}), s16[8,400,128]{2,1,0:T(8,128)(2,1)S(1)}, u32[]{:S(2)}, u32[]{:S(2)}) async-start(s16[8,400,128]{2,1,0:T(8,128)(2,1)} %bitcast.3), calls=%async_computation | async-start | bytes 1638400 | tf_op jit(solution)/shard_map/all_to_all | solution.py:150
  103.6 14.7 %copy-start.1 = (f32[128,384]{1,0:T(8,128)S(1)}, f32[128,384]{1,0:T(8,128)}, u32[]{:S(2)}) copy-start(f32[128,384]{1,0:T(8,128)} %old_ref.1) | copy-start | bytes 589828
  103.9 14.4 %collective-permute-start.8 = (s16[400,128]{1,0:T(8,128)(2,1)S(1)}, s16[400,128]{1,0:T(8,128)(2,1)S(1)}, u32[]{:S(2)}, u32[]{:S(2)}) collective-permute-start(s16[400,128]{1,0:T(8,128)(2,1)S(1)} %shard_map.42), channel_id=1, source_target_pairs={{0,14},{1,0},{2,48},{3,50},{4,338},{5,340},{6,100},{7,102},{8,150}... | collective-permute-start | bytes 307208 | tf_op jit(solution)/shard_map/ppermute | solution.py:176

commit v11 on v9

--- a/solution.py
+++ b/solution.py
@@ -12,13 +12,18 @@
 NX, NZL, NZH, NY, NC = 4, 4, 3, 8, 2
 AXES = ("x", "zl", "zh", "y", "core")
 TRIPLE = ((0, 11), (1, 6), (7, 12), (2, 13), (3, 8), (9, 14), (4, 15), (5, 10))
-OFFSET = (((-1, -2), (-3, -4)), ((0, 1), (2, 3)))
 LANES = 128
 ROWS = 128
 TILE = 16
 LEAST = 2.0**-120
 CODED = NZH * ROWS + TILE
 TOP = 32700.0
+
+
+def rows_of(core, half, x):
+    if half == 1 and x >= 2:
+        return (0 if x == 2 else 4), core
+    return (3 if half else 1 + x // 2) * (1 if core else -1), x % 2
 
 
 def triple_perm(i):
@@ -30,10 +35,8 @@
     ]
 
 
-def ring_perm(cores):
-    return [
-        (y * NC + c, (y + 1 - 2 * c) % NY * NC + c) for y in range(NY) for c in cores
-    ]
+def ring_perm():
+    return [(y * NC + c, (y + 1 - 2 * c) % NY * NC + c) for y in range(NY) for c in range(NC)]
 
 
 def place_perm():
@@ -42,9 +45,9 @@
         for zl in range(NZL):
             for y in range(NY):
                 for c in range(NC):
-                    to_y = (y + OFFSET[c][zl // 2][x // 2]) % NY
+                    far, to_c = rows_of(c, zl // 2, x)
                     source = ((x * NZL + zl) * NY + y) * NC + c
-                    pairs.append((source, (TRIPLE[y][zl % 2] * NY + to_y) * NC + x % 2))
+                    pairs.append((source, (TRIPLE[y][zl % 2] * NY + (y + far) % NY) * NC + to_c))
     return pairs
 
 
@@ -99,17 +102,20 @@
         out_ref[:, pl.ds(pl.multiple_of(j * LANES, LANES), LANES)] = refs[i][...]
 
 
-def product_kernel(at_ref, a0_ref, a1_ref, a2_ref, mine_ref, other_ref, out_ref):
+def product_kernel(at_ref, *refs):
+    *row_refs, mine_ref, other_ref, out_ref = refs
     core = at_ref[1]
-    for i, (up_ref, down_ref) in enumerate(((a1_ref, a0_ref), (a2_ref, a1_ref))):
-        rows = [jnp.where(core == 0, up_ref[c], down_ref[c]) for c in range(NC)]
-        rows = jnp.concatenate(rows, axis=1)
+    rows = []
+    for ref in row_refs:
+        rows += [ref[...]] if len(ref.shape) == 2 else [ref[c] for c in range(NC)]
+    for i in range(0, NX, 2):
+        pair = jnp.concatenate(rows[i : i + 2], axis=1)
         for columns_ref, cw in ((mine_ref, core), (other_ref, 1 - core)):
             out = lax.dot_general(
-                rows, columns_ref[...], (((0,), (0,)), ((), ())), preferred_element_type=jnp.float32
+                pair, columns_ref[...], (((0,), (0,)), ((), ())), preferred_element_type=jnp.float32
             )
-            for c in range(NC):
-                encode(lane_blocks(out[c * ROWS : (c + 1) * ROWS]), store(out_ref, i * NC + c, cw))
+            for c in range(2):
+                encode(lane_blocks(out[c * ROWS : (c + 1) * ROWS]), store(out_ref, i + c, cw))
 
 
 def sum_x_kernel(part_ref, *refs):
@@ -156,18 +162,19 @@
     scale = 0.1 / float(NX * NZL * k)
     at = jnp.stack([lax.axis_index("zh"), lax.axis_index("core")]).astype(jnp.int32)
     ring = [lax.all_gather(block, "core", axis=0)]
-    for step in range(4):
-        ring.append(lax.ppermute(ring[-1], ("y", "core"), ring_perm((0, 1) if step < 3 else (0,))))
+    for _ in range(3):
+        ring.append(lax.ppermute(ring[-1], ("y", "core"), ring_perm()))
     block, _ = lax.optimization_barrier((block, ring[0]))
     mine = [lax.ppermute(block, ("zh", "y", "core"), triple_perm(i)) for i in range(NZH)]
     mine = call(triple_kernel, (k, 384), jnp.bfloat16, 10**10, at, *mine, scalars=True)
-    mine, ring[2] = lax.optimization_barrier((mine, ring[2]))
+    far = lax.ppermute(block, "y", [(y, (y + 4) % NY) for y in range(NY)])
+    mine, ring[2], far = lax.optimization_barrier((mine, ring[2], far))
     other = lax.ppermute(mine, "core", [(0, 1), (1, 0)])
     part = []
-    for half in range(2):
+    for half, rows in enumerate(((ring[1], ring[2]), (ring[3], block, far))):
         out = call(
-            product_kernel, (NX, NC, CODED, LANES), jnp.int16, 2 * k * 512 * 768,
-            at, *ring[2 * half : 2 * half + 3], mine, other, scalars=True,
+            product_kernel, (NX, NC, CODED, LANES), jnp.int16, 4 * 10**9,
+            at, *rows, mine, other, scalars=True,
         )
         out = exchange(out.reshape(NX * NC, CODED, LANES), "x")
         part = [call(sum_x_kernel, (NC * (half + 1), CODED, LANES), jnp.int16, 0, out, *part)]

time: 119 us -> 123 us (1.034)
  waiting for transfers between devices: 38.5 us -> 43.6 us
  starting transfers between devices: 53.1 us -> 49.7 us
  blocking collectives: 15.1 us -> 17.5 us
    all_to_all x2, waiting for transfers between devices: 12.2 us -> 22.9 us  [exchange(): return lax.all_to_all(part, axes, split_axis=0, concat_axis=0, tiled=True)]
    ppermute x3, waiting for transfers between devices: 6.6 us -> 0.01 us  [body(): lax.ppermute(block, ('zh', 'y', 'core'), triple_perm(i))]
    ppermute x4, starting transfers between devices: 19.6 us -> 16 us  [the longest x3 14.1 us: body(): ring.append(lax.ppermute(ring[-1], ('y', 'core'), ring_perm()))]
    all_to_all x1, blocking collectives: 13 us -> 15.4 us  [exchange(): return lax.all_to_all(part, axes, split_axis=0, concat_axis=0, tiled=True)]
  transfers between devices with their start and end apart: 11 -> 11, of which waited for: 5 -> 6; matrix products, arithmetic and copies ran while one was open for 0% -> 0% of each run, Pallas kernels for 6% -> 6%
where the time goes in v11:
time: 123 us; the launch traced here: 122 us
  starting transfers between devices  49.7 us (40%)
  waiting for transfers between devices  43.6 us (35%)
  blocking collectives  17.5 us (14%)
  Pallas kernels  8.45 us (7%)
  local copies, waits for them, and re-layouts  2.25 us (2%)
    all_to_all x2, waiting for transfers between devices, exchange(): return lax.all_to_all(part, axes, split_axis=0, concat_axis=0, tiled=True)  22.9 us
    ppermute x3, starting transfers between devices, body(): lax.ppermute(block, ('zh', 'y', 'core'), triple_perm(i))  22 us
    all_to_all x1, blocking collectives, exchange(): return lax.all_to_all(part, axes, split_axis=0, concat_axis=0, tiled=True)  15.4 us
    ppermute x3, starting transfers between devices, body(): ring.append(lax.ppermute(ring[-1], ('y', 'core'), ring_perm()))  14.1 us
    ppermute x1, waiting for transfers between devices, body(): total = lax.ppermute(total, ('x', 'zl', 'y', 'core'), place_perm())  12.4 us
    pallas_call x7, Pallas kernels, call(): pl.pallas_call(kernel, in_specs=specs, out_specs=pl.BlockSpec(memory_spac...  8.45 us
    all_to_all x2, starting transfers between devices, exchange(): return lax.all_to_all(part, axes, split_axis=0, concat_axis=0, tiled=True)  7.78 us
    ppermute x3, waiting for transfers between devices, body(): ring.append(lax.ppermute(ring[-1], ('y', 'core'), ring_perm()))  4.88 us
  transfers between devices with their start and end apart: 11, of which 6 were waited for; matrix products, arithmetic and copies ran while one was open for 0% of the time, Pallas kernels for 6%

profile of v11, /device:TPU:32, one launch (start us, length us, event | category | flops | bytes accessed | tf_op | source)
XLA Modules:
  0.0 122.4 jit_solution(8665305488075329570)
XLA Ops:
  0.0 0.7 compare_select_fusion
  0.7 0.2 copy-done
  1.0 2.0 %gather_fusion = bf16[704,128]{1,0:T(8,128)(2,1)S(1)} fusion(bf16[1024,128]{1,0:T(8,128)(2,1)S(1)} %copy-done, s32[1024]{0:T(1024)S(1)} %pad_clamp_fusion), kind=kCustom, calls=%fused_computation | custom fusion | bytes 363264 | tf_op jit(solution)/shard_map/gather | solution.py:160
  3.0 2.1 %all-gather = bf16[1408,128]{1,0:T(8,128)(2,1)S(1)} all-gather(bf16[704,128]{1,0:T(8,128)(2,1)S(1)} %gather_fusion), channel_id=2, replica_groups=mesh['x'=4,'zl'=4,'zh'=3,'y'=8,'core'=2] {'core'}, dimensions={0}, use_global_device_ids=true | all-gather | bytes 540672 | tf_op jit(solution)/shard_map/all_gather | solution.py:164
  5.1 2.6 %collective-permute-start = (bf16[2,704,128]{2,1,0:T(8,128)(2,1)S(1)}, bf16[2,704,128]{2,1,0:T(8,128)(2,1)S(1)}, u32[]{:S(2)}, u32[]{:S(2)}) collective-permute-start(bf16[2,704,128]{2,1,0:T(8,128)(2,1)S(1)} %bitcast.5), channel_id=1, source_target_pairs={{0,2},{1,15},{2,4},{3,1},{4,6},{5,3},{6,8},{7,5},{8,10},{9,7},{10,... | collective-permute-start | bytes 1081352 | tf_op jit(solution)/shard_map/ppermute | solution.py:166
  7.6 4.5 %collective-permute-start.5 = (bf16[704,128]{1,0:T(8,128)(2,1)S(1)}, bf16[704,128]{1,0:T(8,128)(2,1)S(1)}, u32[]{:S(2)}, u32[]{:S(2)}) collective-permute-start(bf16[704,128]{1,0:T(8,128)(2,1)S(1)} %gather_fusion), channel_id=1, source_target_pairs={{2,0},{35,1},{5,2},{20,3},{23,4},{38,5},{8,6},{41,7},{11,8},{26,9}... | collective-permute-start | bytes 540680 | tf_op jit(solution)/shard_map/ppermute | solution.py:168
  12.1 15.6 %collective-permute-start.4 = (bf16[704,128]{1,0:T(8,128)(2,1)S(1)}, bf16[704,128]{1,0:T(8,128)(2,1)S(1)}, u32[]{:S(2)}, u32[]{:S(2)}) collective-permute-start(bf16[704,128]{1,0:T(8,128)(2,1)S(1)} %gather_fusion), channel_id=1, source_target_pairs={{1,0},{34,1},{4,2},{19,3},{22,4},{37,5},{7,6},{40,7},{10,8},{25,9}... | collective-permute-start | bytes 540680 | tf_op jit(solution)/shard_map/ppermute | solution.py:168
  27.8 1.9 %collective-permute-start.3 = (bf16[704,128]{1,0:T(8,128)(2,1)S(1)}, bf16[704,128]{1,0:T(8,128)(2,1)S(1)}, u32[]{:S(2)}, u32[]{:S(2)}) collective-permute-start(bf16[704,128]{1,0:T(8,128)(2,1)S(1)} %gather_fusion), channel_id=1, source_target_pairs={{0,0},{33,1},{3,2},{18,3},{21,4},{36,5},{6,6},{39,7},{9,8},{24,9},... | collective-permute-start | bytes 540680 | tf_op jit(solution)/shard_map/ppermute | solution.py:168
  29.7 1.9 %collective-permute-start.6 = (bf16[704,128]{1,0:T(8,128)(2,1)S(1)}, bf16[704,128]{1,0:T(8,128)(2,1)S(1)}, u32[]{:S(2)}, u32[]{:S(2)}) collective-permute-start(bf16[704,128]{1,0:T(8,128)(2,1)S(1)} %gather_fusion), channel_id=1, source_target_pairs={{0,8},{2,10},{4,12},{6,14},{8,0},{10,2},{12,4},{14,6},{1,9},{3,11}... | collective-permute-start | bytes 540680 | tf_op jit(solution)/shard_map/ppermute | solution.py:170
  31.6 0.1 pad_add_fusion.at_ref
  31.7 0.0 collective-permute-done.refs_0_
  31.7 8.5 %collective-permute-start.1 = (bf16[2,704,128]{2,1,0:T(8,128)(2,1)S(1)}, bf16[2,704,128]{2,1,0:T(8,128)(2,1)S(1)}, u32[]{:S(2)}, u32[]{:S(2)}) collective-permute-start(bf16[2,704,128]{2,1,0:T(8,128)(2,1)S(1)} %collective-permute-done.refs_0_), channel_id=1, source_target_pairs={{0,2},{1,15},{2,4},{3,1},{4,6},{5,3},{6,8},{7,5},{8,10},{9,7},{10,... | collective-permute-start | bytes 1081352 | tf_op jit(solution)/shard_map/ppermute | solution.py:166
  40.2 0.0 collective-permute-done.5.refs_2_
  40.2 0.6 shard_map.37.refs_3_.refs_2_
  40.9 3.3 %collective-permute-done.6.refs_2_ = bf16[704,128]{1,0:T(8,128)(2,1)S(1)} collective-permute-done((bf16[704,128]{1,0:T(8,128)(2,1)S(1)}, bf16[704,128]{1,0:T(8,128)(2,1)S(1)}, u32[]{:S(2)}, u32[]{:S(2)}) %collective-permute-start.6) | collective-permute-done | bytes 180256 | tf_op jit(solution)/shard_map/ppermute | solution.py:170
  44.2 4.5 %collective-permute-done.1.refs_1_ = bf16[2,704,128]{2,1,0:T(8,128)(2,1)S(1)} collective-permute-done((bf16[2,704,128]{2,1,0:T(8,128)(2,1)S(1)}, bf16[2,704,128]{2,1,0:T(8,128)(2,1)S(1)}, u32[]{:S(2)}, u32[]{:S(2)}) %collective-permute-start.1) | collective-permute-done | bytes 360480 | tf_op jit(solution)/shard_map/ppermute | solution.py:166
  48.7 2.0 %collective-permute-start.7 = (bf16[704,384]{1,0:T(8,128)(2,1)S(1)}, bf16[704,384]{1,0:T(8,128)(2,1)S(1)}, u32[]{:S(2)}, u32[]{:S(2)}) collective-permute-start(bf16[704,384]{1,0:T(8,128)(2,1)S(1)} %shard_map.37.refs_3_.refs_2_), channel_id=1, source_target_pairs={{0,1},{1,0},{2,3},{3,2},{4,5},{5,4},{6,7},{7,6},{8,9},{9,8},{10,11... | collective-permute-start | bytes 1622024 | tf_op jit(solution)/shard_map/ppermute | solution.py:172
  50.7 3.0 %collective-permute-start.2 = (bf16[2,704,128]{2,1,0:T(8,128)(2,1)S(1)}, bf16[2,704,128]{2,1,0:T(8,128)(2,1)S(1)}, u32[]{:S(2)}, u32[]{:S(2)}) collective-permute-start(bf16[2,704,128]{2,1,0:T(8,128)(2,1)S(1)} %collective-permute-done.1.refs_1_), channel_id=1, source_target_pairs={{0,2},{1,15},{2,4},{3,1},{4,6},{5,3},{6,8},{7,5},{8,10},{9,7},{10,... | collective-permute-start | bytes 1081352 | tf_op jit(solution)/shard_map/ppermute | solution.py:166
  53.7 2.9 %shard_map.39 = s16[4,2,400,128]{3,2,1,0:T(8,128)(2,1)} custom-call(s32[2]{0:T(128)S(1)} %pad_add_fusion.at_ref, bf16[2,704,128]{2,1,0:T(8,128)(2,1)S(1)} %collective-permute-done.refs_0_, bf16[2,704,128]{2,1,0:T(8,128)(2,1)S(1)} %collective-permute-done.1.refs_1_, bf16[704,384]{1,0:T(8,128)(2,1)S(1)} %shard_map.37.refs_3_.refs_2_, ...), custom_call_target="tpu_custom_call" | custom-call | flops 4000000000 | bytes 2000000 | tf_op jit(solution)/shard_map/pallas_call | solution.py:145
  56.6 4.3 %all-to-all-start.1 = ((s16[8,400,128]{2,1,0:T(8,128)(2,1)}), s16[8,400,128]{2,1,0:T(8,128)(2,1)S(1)}, u32[]{:S(2)}, u32[]{:S(2)}) async-start(s16[8,400,128]{2,1,0:T(8,128)(2,1)} %bitcast.4), calls=%async_computation.1 | async-start | bytes 1638400 | tf_op jit(solution)/shard_map/all_to_all | solution.py:156
  60.9 0.4 collective-permute-done.2.refs_0_
  61.2 2.9 %shard_map.38 = s16[4,2,400,128]{3,2,1,0:T(8,128)(2,1)} custom-call(s32[2]{0:T(128)S(1)} %pad_add_fusion.at_ref, bf16[2,704,128]{2,1,0:T(8,128)(2,1)S(1)} %collective-permute-done.2.refs_0_, bf16[704,128]{1,0:T(8,128)(2,1)S(1)} %gather_fusion, bf16[704,128]{1,0:T(8,128)(2,1)S(1)} %collective-permute-done.6.refs_2_, ...), custom_call_target="tpu_custom_call" | custom-call | flops 4000000000 | bytes 2000000 | tf_op jit(solution)/shard_map/pallas_call | solution.py:145
  64.1 10.6 %all-to-all-done.1.part_ref = s16[8,400,128]{2,1,0:T(8,128)(2,1)S(1)} async-done(((s16[8,400,128]{2,1,0:T(8,128)(2,1)}), s16[8,400,128]{2,1,0:T(8,128)(2,1)S(1)}, u32[]{:S(2)}, u32[]{:S(2)}) %all-to-all-start.1) | async-done | bytes 819232 | tf_op jit(solution)/shard_map/all_to_all | solution.py:156
  74.7 3.5 %all-to-all-start = ((s16[8,400,128]{2,1,0:T(8,128)(2,1)}), s16[8,400,128]{2,1,0:T(8,128)(2,1)S(1)}, u32[]{:S(2)}, u32[]{:S(2)}) async-start(s16[8,400,128]{2,1,0:T(8,128)(2,1)} %bitcast.3), calls=%async_computation | async-start | bytes 1638400 | tf_op jit(solution)/shard_map/all_to_all | solution.py:156
  78.2 0.5 shard_map.40.refs_0_
  78.7 12.4 %all-to-all-done.part_ref = s16[8,400,128]{2,1,0:T(8,128)(2,1)S(1)} async-done(((s16[8,400,128]{2,1,0:T(8,128)(2,1)}), s16[8,400,128]{2,1,0:T(8,128)(2,1)S(1)}, u32[]{:S(2)}, u32[]{:S(2)}) %all-to-all-start) | async-done | bytes 819232 | tf_op jit(solution)/shard_map/all_to_all | solution.py:156
  91.1 0.5 shard_map.41
  91.6 15.4 %all_to_all.15.part_ref = s16[4,400,128]{2,1,0:T(8,128)(2,1)S(1)} all-to-all(s16[4,400,128]{2,1,0:T(8,128)(2,1)S(1)} %shard_map.41), channel_id=1, replica_groups=mesh['x'=4,'zl'=4,'zh'=3,'y'=8,'core'=2] {'zl'}, dimensions={0} | all-to-all | bytes 819200 | tf_op jit(solution)/shard_map/all_to_all | solution.py:156
  107.0 0.3 shard_map.42
  107.3 1.9 %collective-permute-start.8 = (s16[400,128]{1,0:T(8,128)(2,1)S(1)}, s16[400,128]{1,0:T(8,128)(2,1)S(1)}, u32[]{:S(2)}, u32[]{:S(2)}) collective-permute-start(s16[400,128]{1,0:T(8,128)(2,1)S(1)} %shard_map.42), channel_id=1, source_target_pairs={{0,14},{1,2},{2,48},{3,52},{4,338},{5,342},{6,100},{7,104},{8,150}... | collective-permute-start | bytes 307208 | tf_op jit(solution)/shard_map/ppermute | solution.py:183
  109.2 12.4 %collective-permute-done.8.total_ref = s16[400,128]{1,0:T(8,128)(2,1)S(1)} collective-permute-done((s16[400,128]{1,0:T(8,128)(2,1)S(1)}, s16[400,128]{1,0:T(8,128)(2,1)S(1)}, u32[]{:S(2)}, u32[]{:S(2)}) %collective-permute-start.8) | collective-permute-done | bytes 102432 | tf_op jit(solution)/shard_map/ppermute | solution.py:183
  121.7 0.7 shard_map.43
  (7 shorter events, 0.0 us)
Async XLA Ops:
  0.0 1.0 copy-start
  5.1 26.6 %collective-permute-start = (bf16[2,704,128]{2,1,0:T(8,128)(2,1)S(1)}, bf16[2,704,128]{2,1,0:T(8,128)(2,1)S(1)}, u32[]{:S(2)}, u32[]{:S(2)}) collective-permute-start(bf16[2,704,128]{2,1,0:T(8,128)(2,1)S(1)} %bitcast.5), channel_id=1, source_target_pairs={{0,2},{1,15},{2,4},{3,1},{4,6},{5,3},{6,8},{7,5},{8,10},{9,7},{10,... | collective-permute-start | bytes 1081352 | tf_op jit(solution)/shard_map/ppermute | solution.py:166
  7.6 32.6 %collective-permute-start.5 = (bf16[704,128]{1,0:T(8,128)(2,1)S(1)}, bf16[704,128]{1,0:T(8,128)(2,1)S(1)}, u32[]{:S(2)}, u32[]{:S(2)}) collective-permute-start(bf16[704,128]{1,0:T(8,128)(2,1)S(1)} %gather_fusion), channel_id=1, source_target_pairs={{2,0},{35,1},{5,2},{20,3},{23,4},{38,5},{8,6},{41,7},{11,8},{26,9}... | collective-permute-start | bytes 540680 | tf_op jit(solution)/shard_map/ppermute | solution.py:168
  12.1 28.1 %collective-permute-start.4 = (bf16[704,128]{1,0:T(8,128)(2,1)S(1)}, bf16[704,128]{1,0:T(8,128)(2,1)S(1)}, u32[]{:S(2)}, u32[]{:S(2)}) collective-permute-start(bf16[704,128]{1,0:T(8,128)(2,1)S(1)} %gather_fusion), channel_id=1, source_target_pairs={{1,0},{34,1},{4,2},{19,3},{22,4},{37,5},{7,6},{40,7},{10,8},{25,9}... | collective-permute-start | bytes 540680 | tf_op jit(solution)/shard_map/ppermute | solution.py:168
  27.8 12.5 %collective-permute-start.3 = (bf16[704,128]{1,0:T(8,128)(2,1)S(1)}, bf16[704,128]{1,0:T(8,128)(2,1)S(1)}, u32[]{:S(2)}, u32[]{:S(2)}) collective-permute-start(bf16[704,128]{1,0:T(8,128)(2,1)S(1)} %gather_fusion), channel_id=1, source_target_pairs={{0,0},{33,1},{3,2},{18,3},{21,4},{36,5},{6,6},{39,7},{9,8},{24,9},... | collective-permute-start | bytes 540680 | tf_op jit(solution)/shard_map/ppermute | solution.py:168
  29.7 14.5 %collective-permute-start.6 = (bf16[704,128]{1,0:T(8,128)(2,1)S(1)}, bf16[704,128]{1,0:T(8,128)(2,1)S(1)}, u32[]{:S(2)}, u32[]{:S(2)}) collective-permute-start(bf16[704,128]{1,0:T(8,128)(2,1)S(1)} %gather_fusion), channel_id=1, source_target_pairs={{0,8},{2,10},{4,12},{6,14},{8,0},{10,2},{12,4},{14,6},{1,9},{3,11}... | collective-permute-start | bytes 540680 | tf_op jit(solution)/shard_map/ppermute | solution.py:170
  31.7 17.0 %collective-permute-start.1 = (bf16[2,704,128]{2,1,0:T(8,128)(2,1)S(1)}, bf16[2,704,128]{2,1,0:T(8,128)(2,1)S(1)}, u32[]{:S(2)}, u32[]{:S(2)}) collective-permute-start(bf16[2,704,128]{2,1,0:T(8,128)(2,1)S(1)} %collective-permute-done.refs_0_), channel_id=1, source_target_pairs={{0,2},{1,15},{2,4},{3,1},{4,6},{5,3},{6,8},{7,5},{8,10},{9,7},{10,... | collective-permute-start | bytes 1081352 | tf_op jit(solution)/shard_map/ppermute | solution.py:166
  48.7 5.0 %collective-permute-start.7 = (bf16[704,384]{1,0:T(8,128)(2,1)S(1)}, bf16[704,384]{1,0:T(8,128)(2,1)S(1)}, u32[]{:S(2)}, u32[]{:S(2)}) collective-permute-start(bf16[704,384]{1,0:T(8,128)(2,1)S(1)} %shard_map.37.refs_3_.refs_2_), channel_id=1, source_target_pairs={{0,1},{1,0},{2,3},{3,2},{4,5},{5,4},{6,7},{7,6},{8,9},{9,8},{10,11... | collective-permute-start | bytes 1622024 | tf_op jit(solution)/shard_map/ppermute | solution.py:172
  50.7 10.5 %collective-permute-start.2 = (bf16[2,704,128]{2,1,0:T(8,128)(2,1)S(1)}, bf16[2,704,128]{2,1,0:T(8,128)(2,1)S(1)}, u32[]{:S(2)}, u32[]{:S(2)}) collective-permute-start(bf16[2,704,128]{2,1,0:T(8,128)(2,1)S(1)} %collective-permute-done.1.refs_1_), channel_id=1, source_target_pairs={{0,2},{1,15},{2,4},{3,1},{4,6},{5,3},{6,8},{7,5},{8,10},{9,7},{10,... | collective-permute-start | bytes 1081352 | tf_op jit(solution)/shard_map/ppermute | solution.py:166
  56.6 18.1 %all-to-all-start.1 = ((s16[8,400,128]{2,1,0:T(8,128)(2,1)}), s16[8,400,128]{2,1,0:T(8,128)(2,1)S(1)}, u32[]{:S(2)}, u32[]{:S(2)}) async-start(s16[8,400,128]{2,1,0:T(8,128)(2,1)} %bitcast.4), calls=%async_computation.1 | async-start | bytes 1638400 | tf_op jit(solution)/shard_map/all_to_all | solution.py:156
  74.7 16.4 %all-to-all-start = ((s16[8,400,128]{2,1,0:T(8,128)(2,1)}), s16[8,400,128]{2,1,0:T(8,128)(2,1)S(1)}, u32[]{:S(2)}, u32[]{:S(2)}) async-start(s16[8,400,128]{2,1,0:T(8,128)(2,1)} %bitcast.3), calls=%async_computation | async-start | bytes 1638400 | tf_op jit(solution)/shard_map/all_to_all | solution.py:156
  107.0 14.7 %copy-start.1 = (f32[128,384]{1,0:T(8,128)S(1)}, f32[128,384]{1,0:T(8,128)}, u32[]{:S(2)}) copy-start(f32[128,384]{1,0:T(8,128)} %old_ref.1) | copy-start | bytes 589828
  107.3 14.4 %collective-permute-start.8 = (s16[400,128]{1,0:T(8,128)(2,1)S(1)}, s16[400,128]{1,0:T(8,128)(2,1)S(1)}, u32[]{:S(2)}, u32[]{:S(2)}) collective-permute-start(s16[400,128]{1,0:T(8,128)(2,1)S(1)} %shard_map.42), channel_id=1, source_target_pairs={{0,14},{1,2},{2,48},{3,52},{4,338},{5,342},{6,100},{7,104},{8,150}... | collective-permute-start | bytes 307208 | tf_op jit(solution)/shard_map/ppermute | solution.py:183
